TPU v7x, 32 devices: a whole 2x2x4 slice. The times are simulated.
32 devices in a mesh: dp: 32 (over z, y, x, core).
Axes of the slice: x: 2, y: 2, z: 4, core: 2. Of those that a mesh axis runs over, the one named last changes fastest.
Arguments:
- block_input: bfloat16 [640, 197, 384], P('dp'), may hold values from -6 to 6
- first_gain: float32 [384], replicated, may hold values from 0.5 to 1.5
- first_shift: float32 [384], replicated, may hold values from -3 to 3
- qkv_weight: bfloat16 [384, 1152], P('dp'), may hold values from -0.3125 to 0.3125
- query_value_bias: float32 [768], replicated, may hold values from -3 to 3
- proj_weight: bfloat16 [384, 384], P('dp'), may hold values from -1.25 to 1.25
- proj_bias: float32 [384], replicated, may hold values from -3 to 3
- second_gain: float32 [384], replicated, may hold values from 0.5 to 1.5
- second_shift: float32 [384], replicated, may hold values from -3 to 3
- up_weight: bfloat16 [384, 1536], P('dp'), may hold values from -0.3125 to 0.3125
- up_bias: float32 [1536], replicated, may hold values from -3 to 3
- down_weight: bfloat16 [1536, 384], P('dp'), may hold values from -0.15625 to 0.15625
- down_bias: float32 [384], replicated, may hold values from -3 to 3
- output_cotangent: bfloat16 [640, 197, 384], P('dp'), may hold values from -6 to 6
Outputs:
- block_output: float32 [640, 197, 384], P('dp')
- input_grad: float32 [640, 197, 384], P('dp')
- grad_first_gain: float32 [384], P('dp')
- grad_first_shift: float32 [384], P('dp')
- grad_qkv_weight: float32 [384, 1152], P('dp')
- grad_query_value_bias: float32 [768], P('dp')
- grad_proj_weight: float32 [384, 384], P('dp')
- grad_proj_bias: float32 [384], P('dp')
- grad_second_gain: float32 [384], P('dp')
- grad_second_shift: float32 [384], P('dp')
- grad_up_weight: float32 [384, 1536], P('dp')
- grad_up_bias: float32 [1536], P('dp')
- grad_down_weight: float32 [1536, 384], P('dp')
- grad_down_bias: float32 [384], P('dp')
All inputs are finite; a program needn't handle non-finite values.
Results may differ from a plain program's by a relative error of at most 0.011.
Values may be sent and summed in bfloat16 or wider, within the bound.
No kernel may reach another device: no remote copies, remote signals or barrier semaphores. Data moves between devices by JAX's collectives and lax.ppermute only.
A program may use at most 256 MiB of HBM per device.

v0:
```python
from functools import partial

import jax
import jax.numpy as jnp
from jax import lax
from jax.sharding import PartitionSpec as P

D = 384
H = 6
DH = 64


norm_eps = 1e-06
f32 = jnp.float32
bf16 = jnp.bfloat16


def layer_norm(values, gain, shift):
    center = values - jnp.mean(values, axis=-1, keepdims=True)
    spread = jnp.mean(center * center, axis=-1, keepdims=True)
    return center * lax.rsqrt(spread + norm_eps) * gain + shift


def exact_gelu(values):
    return jax.nn.gelu(values, approximate=False)


def attend(packed, heads):
    count, seq_len, triple = packed.shape
    width = heads * DH
    query_rows = packed[..., :width].reshape(count, seq_len, heads, DH)
    key_rows = packed[..., width : 2 * width].reshape(count, seq_len, heads, DH)
    value_rows = packed[..., 2 * width :].reshape(count, seq_len, heads, DH)
    scores = jnp.einsum("iqhe,ikhe->ihqk", query_rows, key_rows, preferred_element_type=f32) * 0.125
    weights_full, soft_pull = jax.vjp(partial(jax.nn.softmax, axis=-1), scores)
    weights = weights_full.astype(bf16)
    mixed = jnp.einsum("ihqk,ikhe->iqhe", weights, value_rows, preferred_element_type=f32)
    mixed = mixed.reshape(count, seq_len, width).astype(bf16)
    return (mixed, (query_rows, key_rows, value_rows, weights, soft_pull))


def attend_back(grad_mixed, kept, heads):
    query_rows, key_rows, value_rows, weights, soft_pull = kept
    count, seq_len = (grad_mixed.shape[0], grad_mixed.shape[1])
    width = heads * DH
    grad_mixed = grad_mixed.reshape(count, seq_len, heads, DH)
    grad_values = jnp.einsum("ihqk,iqhe->ikhe", weights, grad_mixed, preferred_element_type=f32)
    grad_weights = jnp.einsum("iqhe,ikhe->ihqk", grad_mixed, value_rows, preferred_element_type=f32)
    grad_scores = soft_pull(grad_weights)[0].astype(bf16)
    grad_queries = (
        jnp.einsum("ihqk,ikhe->iqhe", grad_scores, key_rows, preferred_element_type=f32) * 0.125
    )
    grad_keys = (
        jnp.einsum("ihqk,iqhe->ikhe", grad_scores, query_rows, preferred_element_type=f32) * 0.125
    )
    return jnp.concatenate(
        [
            grad_queries.reshape(count, seq_len, width),
            grad_keys.reshape(count, seq_len, width),
            grad_values.reshape(count, seq_len, width),
        ],
        axis=-1,
    ).astype(bf16)


def on_device(
    block_input,
    first_gain,
    first_shift,
    qkv_weight,
    query_value_bias,
    proj_weight,
    proj_bias,
    second_gain,
    second_shift,
    up_weight,
    up_bias,
    down_weight,
    down_bias,
    output_cotangent,
):
    qkv_full, proj_full, up_full, down_full = (
        lax.all_gather(qkv_weight, "dp", axis=0, tiled=True),
        lax.all_gather(proj_weight, "dp", axis=0, tiled=True),
        lax.all_gather(up_weight, "dp", axis=0, tiled=True),
        lax.all_gather(down_weight, "dp", axis=0, tiled=True),
    )
    inputs = block_input.astype(f32)
    normed_full, first_pull = jax.vjp(layer_norm, inputs, first_gain, first_shift)
    normed = normed_full.astype(bf16)
    full_bias = jnp.concatenate([query_value_bias[:D], jnp.zeros((D,), f32), query_value_bias[D:]])
    packed = (
        jnp.einsum("isd,de->ise", normed, qkv_full, preferred_element_type=f32) + full_bias
    ).astype(bf16)
    mixed, kept = attend(packed, H)
    middle = (
        inputs + jnp.einsum("isd,de->ise", mixed, proj_full, preferred_element_type=f32) + proj_bias
    )
    second_full, second_pull = jax.vjp(layer_norm, middle, second_gain, second_shift)
    second = second_full.astype(bf16)
    upper = jnp.einsum("isd,df->isf", second, up_full, preferred_element_type=f32) + up_bias
    hidden_full, gelu_pull = jax.vjp(exact_gelu, upper)
    hidden = hidden_full.astype(bf16)
    output = (
        middle
        + jnp.einsum("isf,fd->isd", hidden, down_full, preferred_element_type=f32)
        + down_bias
    )
    qkv_full, proj_full, up_full, down_full = (
        lax.all_gather(qkv_weight, "dp", axis=0, tiled=True),
        lax.all_gather(proj_weight, "dp", axis=0, tiled=True),
        lax.all_gather(up_weight, "dp", axis=0, tiled=True),
        lax.all_gather(down_weight, "dp", axis=0, tiled=True),
    )
    upstream = output_cotangent.astype(f32)
    grad_down = jnp.einsum("isf,isd->fd", hidden, output_cotangent, preferred_element_type=f32)
    grad_down_b = jnp.sum(upstream, axis=(0, 1))
    grad_hidden = jnp.einsum("isd,fd->isf", output_cotangent, down_full, preferred_element_type=f32)
    grad_upper = gelu_pull(grad_hidden)[0].astype(bf16)
    grad_up = jnp.einsum("isd,isf->df", second, grad_upper, preferred_element_type=f32)
    grad_up_b = jnp.sum(grad_upper.astype(f32), axis=(0, 1))
    grad_second = jnp.einsum("isf,df->isd", grad_upper, up_full, preferred_element_type=f32)
    grad_mid_norm, grad_gain_two, grad_shift_two = second_pull(grad_second)
    grad_middle = upstream + grad_mid_norm
    mlp_parts = (grad_gain_two, grad_shift_two, grad_up, grad_up_b, grad_down, grad_down_b)
    grad_branch = grad_middle.astype(bf16)
    grad_proj = jnp.einsum("isd,ise->de", mixed, grad_branch, preferred_element_type=f32)
    grad_proj_b = jnp.sum(grad_branch.astype(f32), axis=(0, 1))
    grad_mixed = jnp.einsum(
        "ise,de->isd", grad_branch, proj_full, preferred_element_type=f32
    ).astype(bf16)
    grad_packed = attend_back(grad_mixed, kept, H)
    grad_qkv = jnp.einsum("isd,ise->de", normed, grad_packed, preferred_element_type=f32)
    packed_sums = jnp.sum(grad_packed.astype(f32), axis=(0, 1))
    grad_qv_b = jnp.concatenate([packed_sums[:D], packed_sums[2 * D :]])
    grad_normed = jnp.einsum("ise,de->isd", grad_packed, qkv_full, preferred_element_type=f32)
    grad_in_norm, grad_gain_one, grad_shift_one = first_pull(grad_normed)
    input_grad = grad_middle + grad_in_norm
    attn_parts = (grad_gain_one, grad_shift_one, grad_qkv, grad_qv_b, grad_proj, grad_proj_b)
    summed = lax.psum_scatter(attn_parts + mlp_parts, "dp", scatter_dimension=0, tiled=True)
    (
        gain_one,
        shift_one,
        qkv_sum,
        qv_sum,
        proj_sum,
        projb_sum,
        gain_two,
        shift_two,
        up_sum,
        upb_sum,
        down_sum,
        downb_sum,
    ) = summed
    return (
        output,
        input_grad,
        gain_one,
        shift_one,
        qkv_sum,
        qv_sum,
        proj_sum,
        projb_sum,
        gain_two,
        shift_two,
        up_sum,
        upb_sum,
        down_sum,
        downb_sum,
    )


def solution(mesh):
    in_specs = (
        P("dp", None, None),
        P(),
        P(),
        P("dp", None),
        P(),
        P("dp", None),
        P(),
        P(),
        P(),
        P("dp", None),
        P(),
        P("dp", None),
        P(),
        P("dp", None, None),
    )
    out_specs = (
        P("dp", None, None),
        P("dp", None, None),
        P("dp"),
        P("dp"),
        P("dp", None),
        P("dp"),
        P("dp", None),
        P("dp"),
        P("dp"),
        P("dp"),
        P("dp", None),
        P("dp"),
        P("dp", None),
        P("dp"),
    )
    return jax.shard_map(
        on_device, mesh=mesh, in_specs=in_specs, out_specs=out_specs, check_vma=False
    )
```

profile of v0, /device:TPU:0, one launch (start us, length us, event | category | flops | bytes accessed | tf_op | source)
XLA Modules:
  0.0 702.4 jit_solution(15541279212954708640)
XLA Ops:
  11.4 3.0 fusion.24
  15.1 49.5 %all-gather = bf16[32,12,1152]{2,1,0:T(8,128)(2,1)} all-gather(bf16[1,12,1152]{2,1,0:T(8,128)(2,1)S(1)} %bitcast.80), channel_id=1, replica_groups=mesh['dp'=32] {'dp'}, dimensions={0}, use_global_device_ids=true | all-gather | bytes 912384 | tf_op jit(solution)/shard_map/all_gather | solution.py:83
  66.8 7.2 %fusion.13 = bf16[20,197,1152]{2,1,0:T(8,128)(2,1)S(1)} fusion(bf16[384,1152,1]{1,0,2:T(8,128)(2,1)} %reshape.147, f32[1152]{0:T(1024)S(1)} %pad_maximum_fusion.1, bf16[20,197,384]{2,1,0:T(8,128)(2,1)S(1)} %copy-done.2, f32[384]{0:T(512)S(1)} %copy-done.41, f32[384]{0:T(512)S(1)} %copy-done.30, f32[20,197]{1,0:T(8,128)S(1)} %fusion.36, ...), kind=kOutput, calls=%fused_computation.31 | convolution fusion | flops 3504015360 | bytes 13027616 | tf_op jit(solution)/shard_map/isd,de->ise/dot_general | solution.py:93
  74.0 3.8 fusion.45
  77.8 5.7 copy.59
  83.5 5.7 copy.60
  89.2 15.6 %fusion.48 = (f32[20,6,197]{2,1,0:T(8,128)S(1)}, f32[20,6,197,197]{2,3,1,0:T(8,128)}) fusion(bf16[20,197,6,64]{1,3,2,0:T(8,128)(2,1)} %bitcast.73, bf16[20,197,6,64]{1,3,2,0:T(8,128)(2,1)} %bitcast.68), kind=kOutput, calls=%fused_computation.98 | convolution fusion | flops 610077696 | bytes 24774720 | tf_op jit(solution)/shard_map/jvp()/sub | solution.py:35
  105.5 13.6 %divide_convert_fusion = bf16[20,6,197,197]{2,3,1,0:T(8,128)(2,1)} fusion(f32[20,6,197,197]{2,3,1,0:T(8,128)} %get-tuple-element.53, f32[20,6,197]{2,1,0:T(8,128)S(1)} %get-tuple-element.52), kind=kLoop, calls=%fused_computation.25 | loop fusion | flops 9314160 | bytes 28037040 | tf_op jit(solution)/shard_map/convert_element_type | solution.py:36
  119.1 5.7 copy.58
  124.8 37.9 %all-gather.1 = bf16[32,12,384]{2,1,0:T(8,128)(2,1)S(1)} all-gather(bf16[1,12,384]{2,1,0:T(8,128)(2,1)S(1)} %bitcast.81), channel_id=1, replica_groups=mesh['dp'=32] {'dp'}, dimensions={0}, use_global_device_ids=true | all-gather | bytes 304128 | tf_op jit(solution)/shard_map/all_gather | solution.py:84
  163.6 8.2 %convolution_convert_fusion.1 = bf16[20,6,64,197]{3,2,1,0:T(8,128)(2,1)S(1)} fusion(bf16[20,197,6,64]{1,3,2,0:T(8,128)(2,1)} %bitcast.64, bf16[20,6,197,197]{2,3,1,0:T(8,128)(2,1)} %divide_convert_fusion), kind=kOutput, calls=%fused_computation.68 | convolution fusion | flops 597619200 | bytes 15366000 | tf_op jit(solution)/shard_map/ihqk,ikhe->iqhe/dot_general | solution.py:37
  178.5 3.0 reshape.149
  181.6 16.8 %convert_reduce_fusion.1 = (u32[197,1536]{1,0:T(8,128)}, u32[197,1536]{1,0:T(8,128)}, f32[20,197,1536]{2,1,0:T(8,128)S(1)}) fusion(f32[1536]{0:T(1024)S(1)} %copy-done.29, bf16[384,1536,1]{1,0,2:T(8,128)(2,1)} %reshape.149, f32[20,197,384]{2,1,0:T(8,128)} %copy-done.7, f32[384]{0:T(512)S(1)} %copy-done.40, f32[384]{0:T(512)S(1)} %copy-done.35, ...), kind=kOutput, calls=%fused_computation.7 | convolution fusion | flops 4727394816 | bytes 33900320 | tf_op jit(solution)/shard_map/isd,df->isf/dot_general | solution.py:101
  198.4 8.2 %copy-done.5 = f32[20,197,1536]{2,1,0:T(8,128)} copy-done((f32[20,197,1536]{2,1,0:T(8,128)}, f32[20,197,1536]{2,1,0:T(8,128)S(1)}, u32[]{:S(2)}) %copy-start.5) | copy-done | bytes 24207384
  206.6 58.8 %multiply_convert_fusion.1 = (bf16[20,197,1536]{2,1,0:T(8,128)(2,1)}, f32[20,197,1536]{2,1,0:T(8,128)}) fusion(f32[20,197,1536]{2,1,0:T(8,128)S(1)} %get-tuple-element.56, f32[1536]{0:T(1024)S(1)} %copy-done.29, u32[197,1536]{1,0:T(8,128)} %get-tuple-element.15, u32[197,1536]{1,0:T(8,128)} %get-tuple-element.14), kind=kLoop, calls=%fused_computation.12 | loop fusion | flops 417576960 | bytes 62945280 | tf_op jit(solution)/shard_map/convert_element_type | solution.py:103
  265.4 39.9 %convert_reduce_fusion.2 = (f32[1536]{0:T(1024)}, bf16[20,197,1536]{2,1,0:T(8,128)(2,1)}) fusion(f32[20,197,1536]{2,1,0:T(8,128)} %get-tuple-element.42, bf16[20,197,384]{2,1,0:T(8,128)(2,1)} %param.27, bf16[1536,384]{1,0:T(8,128)(2,1)} %all-gather.6.cloned.1.call-done, f32[20,197,1536]{2,1,0:T(8,128)} %copy-done.5, f32[1536]{0:T(1024)S(1)} %copy-done.29), kind=kOutput, calls=%fused_computation.8 | convolution fusion | flops 4750692864 | bytes 64736256 | tf_op jit(solution)/shard_map/isd,fd->isf/dot_general | solution.py:118
  305.3 13.1 %convolution_bitcast_fusion.1 = f32[384,1536]{1,0:T(8,128)} fusion(bf16[20,197,1536]{2,1,0:T(8,128)(2,1)} %get-tuple-element.62, f32[20,197,384]{2,1,0:T(8,128)} %copy-done.7, f32[384]{0:T(512)S(1)} %copy-done.40, f32[384]{0:T(512)S(1)} %copy-done.35, f32[20,197]{1,0:T(8,128)S(1)} %fusion.37, f32[20,197]{1,0:T(8,128)S(1)} %broadcast_multiply_fusion), kind=kOutput, calls=%fused_computation.64 | convolution fusion | flops 4655377920 | bytes 20549408 | tf_op jit(solution)/shard_map/isd,isf->df/dot_general | solution.py:120
  318.4 13.2 %multiply_reduce_fusion.2 = (f32[384]{0:T(512)}, f32[20,197]{1,0:T(8,128)S(1)}, f32[384]{0:T(512)}, f32[20,197,384]{2,1,0:T(8,128)S(1)}) fusion(f32[20,197,384]{2,1,0:T(8,128)} %copy-done.7, f32[20,197]{1,0:T(8,128)S(1)} %fusion.37, f32[20,197]{1,0:T(8,128)S(1)} %broadcast_multiply_fusion, f32[384]{0:T(512)S(1)} %copy-done.35, ...), kind=kOutput, calls=%fused_computation.55 | convolution fusion | flops 4659911680 | bytes 25438896 | tf_op jit(solution)/shard_map/isf,df->isd/dot_general | solution.py:122
  331.8 3.0 fusion.43
  341.3 3.7 copy.63
  345.1 21.5 %multiply_reduce_fusion = (f32[20,6,197]{2,1,0:T(8,128)S(1)}, f32[20,6,197,197]{2,3,1,0:T(8,128)}) fusion(f32[20,6,197,197]{2,3,1,0:T(8,128)} %get-tuple-element.53, f32[20,6,197]{2,1,0:T(8,128)S(1)} %copy-done.18, bf16[20,197,6,64]{1,3,2,0:T(8,128)(2,1)} %bitcast.66, bf16[20,197,6,64]{1,3,2,0:T(8,128)(2,1)} %bitcast.65), kind=kOutput, calls=%fused_computation.10 | convolution fusion | flops 610053888 | bytes 43497600 | tf_op jit(solution)/shard_map/iqhe,ikhe->ihqk/dot_general | solution.py:48
  366.7 16.3 %multiply_convert_fusion = bf16[20,6,197,197]{2,3,1,0:T(8,128)(2,1)S(1)} fusion(f32[20,6,197,197]{2,3,1,0:T(8,128)} %get-tuple-element.53, f32[20,6,197,197]{2,3,1,0:T(8,128)} %get-tuple-element.59, f32[20,6,197]{2,1,0:T(8,128)S(1)} %neg.22, f32[20,6,197]{2,1,0:T(8,128)S(1)} %copy-done.17), kind=kLoop, calls=%fused_computation.9 | loop fusion | flops 18628320 | bytes 46759920 | tf_op jit(solution)/shard_map/convert_element_type | solution.py:49
  383.0 4.4 copy-done
  387.4 4.3 multiply_convert_fusion.3
  391.8 14.1 %multiply_convert_fusion.2 = bf16[20,6,64,197]{3,2,1,0:T(8,128)(2,1)} fusion(bf16[20,197,6,64]{1,3,2,0:T(8,128)(2,1)} %bitcast.74, bf16[20,6,197,197]{2,3,1,0:T(8,128)(2,1)} %copy-done), kind=kOutput, calls=%fused_computation.43 | convolution fusion | flops 599132160 | bytes 15366000 | tf_op jit(solution)/shard_map/ihqk,iqhe->ikhe/dot_general | solution.py:54
  405.8 14.0 %convolution_convert_fusion = bf16[20,6,64,197]{3,2,1,0:T(8,128)(2,1)} fusion(bf16[20,197,6,64]{1,3,2,0:T(8,128)(2,1)} %bitcast.67, bf16[20,6,197,197]{2,3,1,0:T(8,128)(2,1)} %divide_convert_fusion), kind=kOutput, calls=%fused_computation.67 | convolution fusion | flops 597619200 | bytes 15366000 | tf_op jit(solution)/shard_map/ihqk,iqhe->ikhe/dot_general | solution.py:47
  419.8 4.8 convolution_bitcast_fusion.3
  424.6 5.8 copy.67
  430.4 6.0 copy.68
  436.4 5.8 copy.69
  442.3 8.8 %convolution_bitcast_fusion.2 = f32[384,1152]{1,0:T(8,128)} fusion(bf16[20,197,384]{2,1,0:T(8,128)(2,1)S(1)} %copy-done.3, f32[384]{0:T(512)S(1)} %copy-done.42, f32[384]{0:T(512)S(1)} %copy-done.31, f32[20,197]{1,0:T(8,128)S(1)} %copy-done.26, f32[20,197]{1,0:T(8,128)S(1)} %copy-done.22, bf16[20,197,384]{2,1,0:T(8,128)(2,1)} %copy.69, ...), kind=kOutput, calls=%fused_computation.65 | convolution fusion | flops 3522170880 | bytes 13907744 | tf_op jit(solution)/shard_map/isd,ise->de/dot_general | solution.py:133
  451.1 81.0 %fusion.41 = (f32[16,1152]{1,0:T(8,128)S(1)}, f32[16,384]{1,0:T(8,128)S(1)}, f32[16,1536]{1,0:T(8,128)S(1)}) fusion(f32[384,1152]{1,0:T(8,128)} %convolution_bitcast_fusion.2, f32[384,384]{1,0:T(8,128)} %convolution_bitcast_fusion.3, f32[384,1536]{1,0:T(8,128)} %convolution_bitcast_fusion.1), kind=kCustom, calls=%all-reduce-scatter.3 | all-reduce-scatter fusion | flops 1572865 | bytes 4915200
  538.2 8.5 %fusion.40 = (f32[384]{0:T(512)S(1)}, f32[20,197]{1,0:T(8,128)S(1)}, f32[20,197,384]{2,1,0:T(8,128)S(1)}) fusion(f32[384]{0:T(512)S(1)} %copy-done.31, f32[20,197]{1,0:T(8,128)S(1)} %copy-done.22, bf16[20,197,384]{2,1,0:T(8,128)(2,1)S(1)} %copy-done.3, bf16[384,1152,1]{1,0,2:T(8,128)(2,1)} %reshape.147, bf16[20,197,384]{2,1,0:T(8,128)(2,1)} %copy.69, ...), kind=kOutput, calls=%fused_computation.93 | convolution fusion | flops 3522166528 | bytes 19074848 | tf_op jit(solution)/shard_map/ise,de->isd/dot_general | solution.py:136
  549.8 3.5 fusion.23
  553.3 10.8 %convolution_bitcast_fusion = f32[1536,384]{1,0:T(8,128)} fusion(bf16[20,197,1536]{2,1,0:T(8,128)(2,1)} %get-tuple-element.41, bf16[20,197,384]{2,1,0:T(8,128)(2,1)S(1)} %copy-done.12), kind=kOutput, calls=%fused_computation.63 | convolution fusion | flops 4647813120 | bytes 17488896 | tf_op jit(solution)/shard_map/isf,isd->fd/dot_general | solution.py:116
  564.1 10.7 %convert_reduce_fusion.5 = (f32[384]{0:T(512)S(1)}, f32[20,197,384]{2,1,0:T(8,128)}) fusion(bf16[20,197,384]{2,1,0:T(8,128)(2,1)} %param.27, f32[20,197]{1,0:T(8,128)S(1)} %negate_multiply_fusion.1, f32[20,197]{1,0:T(8,128)S(1)} %multiply_multiply_fusion.5, f32[20,197]{1,0:T(8,128)S(1)} %copy-done.22, bf16[20,197,384]{2,1,0:T(8,128)(2,1)S(1)} %copy-done.3, ...), kind=kLoop, calls=%fused_computation.45 | loop fusion | flops 19668096 | bytes 24289232 | tf_op jit(solution)/shard_map/reduce_sum | solution.py:117
  574.9 12.4 %add_add_fusion.3 = f32[20,197,384]{2,1,0:T(8,128)} fusion(f32[20,197,384]{2,1,0:T(8,128)} %copy-done.7, f32[384]{0:T(512)S(1)} %copy-done.43, bf16[20,197,1536]{2,1,0:T(8,128)(2,1)} %get-tuple-element.41, bf16[1536,384]{1,0:T(8,128)(2,1)S(1)} %copy-done.38), kind=kOutput, calls=%fused_computation.59 | convolution fusion | flops 4650839040 | bytes 25388544 | tf_op jit(solution)/shard_map/isf,fd->isd/dot_general | solution.py:106
  591.2 5.0 collective-permute-start.8
  596.2 3.4 collective-permute-start.9
  602.4 3.4 collective-permute-start
  610.6 4.0 collective-permute-start.3
  616.0 37.8 %all-reduce.14 = (f32[384]{0:T(512)S(1)}, f32[384]{0:T(512)S(1)}, f32[768]{0:T(1024)S(1)}, f32[384]{0:T(512)S(1)}, f32[384]{0:T(512)S(1)}, /*index=5*/f32[384]{0:T(512)S(1)}, f32[1536]{0:T(1024)S(1)}, f32[384]{0:T(512)S(1)}) all-reduce(f32[384]{0:T(512)S(1)} %get-tuple-element.18, ...), channel_id=2, replica_groups=mesh['dp'=32] {'dp'}, use_global_device_ids=true, to_apply=%region_12.0.clone | all-reduce | flops 4608 | bytes 36864
  660.7 4.8 collective-permute-start.17
  665.6 4.4 collective-permute-start.5
  670.0 3.6 collective-permute-start.6
  679.0 3.2 collective-permute-start.19
  683.4 2.8 collective-permute-start.20
  686.2 3.5 collective-permute-start.21
  (178 shorter events, 63.0 us)
Async XLA Ops:
  7.2 59.6 %copy-start.2 = (bf16[20,197,384]{2,1,0:T(8,128)(2,1)S(1)}, bf16[20,197,384]{2,1,0:T(8,128)(2,1)}, u32[]{:S(2)}) copy-start(bf16[20,197,384]{2,1,0:T(8,128)(2,1)} %param.14) | copy-start | bytes 9077764
  7.2 59.6 %copy-start.30 = (f32[384]{0:T(512)S(1)}, f32[384]{0:T(512)}, u32[]{:S(2)}) copy-start(f32[384]{0:T(512)} %param.15) | copy-start | bytes 4612
  7.2 59.6 %copy-start.41 = (f32[384]{0:T(512)S(1)}, f32[384]{0:T(512)}, u32[]{:S(2)}) copy-start(f32[384]{0:T(512)} %param.16) | copy-start | bytes 4612
  7.2 171.3 %all-gather.8.cloned.1.call-start = ((), (), s32[]{:S(2)}) async-start(), calls=%async_computation.3 | async-start | bytes 1622016 | tf_op jit(solution)/shard_map/all_gather | solution.py:85
  8.0 257.4 %all-gather.6.cloned.1.call-start = ((), (), s32[]{:S(2)}) async-start(), calls=%async_computation.1 | async-start | bytes 1216512 | tf_op jit(solution)/shard_map/all_gather | solution.py:86
  8.7 687.0 %reduce-scatter.8.cloned.1.call-start = ((), (), s32[]{:S(2)}) async-start(), calls=%async_computation.2 | async-start | bytes 2433024 | tf_op jit(solution)/shard_map/reduce_scatter | solution.py:140
  11.4 62.6 %copy-start.21 = (f32[20,197]{1,0:T(8,128)}, f32[20,197]{1,0:T(8,128)S(1)}, u32[]{:S(2)}) copy-start(f32[20,197]{1,0:T(8,128)S(1)} %broadcast_multiply_fusion.1) | copy-start | bytes 47284
  15.1 59.0 %copy-start.25 = (f32[20,197]{1,0:T(8,128)}, f32[20,197]{1,0:T(8,128)S(1)}, u32[]{:S(2)}) copy-start(f32[20,197]{1,0:T(8,128)S(1)} %fusion.36) | copy-start | bytes 47284
  104.8 14.3 %copy-start.16 = (f32[20,6,197]{2,1,0:T(8,128)}, f32[20,6,197]{2,1,0:T(8,128)S(1)}, u32[]{:S(2)}) copy-start(f32[20,6,197]{2,1,0:T(8,128)S(1)} %get-tuple-element.52) | copy-start | bytes 283684
  305.3 13.1 %copy-start.20 = (bf16[384,1536,1]{1,0,2:T(8,128)(2,1)S(1)}, bf16[384,1536,1]{1,0,2:T(8,128)(2,1)}, u32[]{:S(2)}) copy-start(bf16[384,1536,1]{1,0,2:T(8,128)(2,1)} %reshape.149) | copy-start | bytes 3538948
  305.3 26.4 %slice-start = ((s8[6144000]{0:T(1024)(128)(4,1)}), s8[4194304]{0:T(1024)(128)(4,1)S(1)}, s32[]{:S(2)}) async-start(s8[6144000]{0:T(1024)(128)(4,1)} %bitcast.71), calls=%async_computation.4 | async-start | bytes 8388608
  318.4 13.3 %slice-start.1 = ((s8[6144000]{0:T(1024)(128)(4,1)}), s8[1949696]{0:T(1024)(128)(4,1)S(1)}, s32[]{:S(2)}) async-start(s8[6144000]{0:T(1024)(128)(4,1)} %bitcast.71), calls=%async_computation.5 | async-start | bytes 3899392
  345.1 21.6 %copy-start.17 = (f32[20,6,197]{2,1,0:T(8,128)S(1)}, f32[20,6,197]{2,1,0:T(8,128)}, u32[]{:S(2)}) copy-start(f32[20,6,197]{2,1,0:T(8,128)} %copy-done.16) | copy-start | bytes 283684
  366.6 20.8 %copy-start.4 = (bf16[20,197,384]{1,2,0:T(8,128)(2,1)S(1)}, bf16[20,197,384]{1,2,0:T(8,128)(2,1)}, u32[]{:S(2)}) copy-start(bf16[20,197,384]{1,2,0:T(8,128)(2,1)} %copy.60) | copy-start | bytes 9077764
  405.8 14.0 %copy-start.14 = (bf16[20,197,384]{2,1,0:T(8,128)(2,1)S(1)}, bf16[20,197,384]{2,1,0:T(8,128)(2,1)}, u32[]{:S(2)}) copy-start(bf16[20,197,384]{2,1,0:T(8,128)(2,1)} %copy-done.13) | copy-start | bytes 9077764
  430.4 11.9 %copy-start.42 = (f32[384]{0:T(512)S(1)}, f32[384]{0:T(512)}, u32[]{:S(2)}) copy-start(f32[384]{0:T(512)} %param.16) | copy-start | bytes 4612
  532.7 15.6 %copy-start.24 = (f32[20,197]{1,0:T(8,128)S(1)}, f32[20,197]{1,0:T(8,128)}, u32[]{:S(2)}) copy-start(f32[20,197]{1,0:T(8,128)} %copy-done.23) | copy-start | bytes 47284
  532.7 58.4 %collective-permute-start.10 = (f32[16,384]{1,0:T(8,128)S(1)}, f32[16,384]{1,0:T(8,128)S(1)}, u32[]{:S(2)}, u32[]{:S(2)}) collective-permute-start(f32[16,384]{1,0:T(8,128)S(1)} %get-tuple-element.35), channel_id=1, source_target_pairs={{0,3},{1,4},{2,5},{3,6},{4,7},{5,8},{6,9},{7,10},{8,11},{9,12},{10... | collective-permute-start | bytes 73736
  534.1 62.1 %collective-permute-start.11 = (f32[16,384]{1,0:T(8,128)S(1)}, f32[16,384]{1,0:T(8,128)S(1)}, u32[]{:S(2)}, u32[]{:S(2)}) collective-permute-start(f32[16,384]{1,0:T(8,128)S(1)} %get-tuple-element.35), channel_id=1, source_target_pairs={{0,4},{1,5},{2,6},{3,7},{4,8},{5,9},{6,10},{7,11},{8,12},{9,13},{1... | collective-permute-start | bytes 73736
  535.4 64.2 %collective-permute-start.12 = (f32[16,384]{1,0:T(8,128)S(1)}, f32[16,384]{1,0:T(8,128)S(1)}, u32[]{:S(2)}, u32[]{:S(2)}) collective-permute-start(f32[16,384]{1,0:T(8,128)S(1)} %get-tuple-element.35), channel_id=1, source_target_pairs={{0,5},{1,6},{2,7},{3,8},{4,9},{5,10},{6,11},{7,12},{8,13},{9,14},{... | collective-permute-start | bytes 73736
  536.7 65.7 %collective-permute-start.13 = (f32[16,384]{1,0:T(8,128)S(1)}, f32[16,384]{1,0:T(8,128)S(1)}, u32[]{:S(2)}, u32[]{:S(2)}) collective-permute-start(f32[16,384]{1,0:T(8,128)S(1)} %get-tuple-element.35), channel_id=1, source_target_pairs={{0,6},{1,7},{2,8},{3,9},{4,10},{5,11},{6,12},{7,13},{8,14},{9,15},... | collective-permute-start | bytes 73736
  546.7 42.2 %collective-permute-start.15 = (f32[12,384]{1,0:T(8,128)}, f32[12,384]{1,0:T(8,128)S(1)}, u32[]{:S(2)}, u32[]{:S(2)}) collective-permute-start(f32[12,384]{1,0:T(8,128)} %slice.34), channel_id=1, source_target_pairs={{0,8},{1,9},{2,10},{3,11},{4,12},{5,13},{6,14},{7,15},{8,16},{9,17... | collective-permute-start | bytes 55304
  574.8 12.4 %copy-start.8 = (bf16[20,197,384]{2,1,0:T(8,128)(2,1)S(1)}, bf16[20,197,384]{2,1,0:T(8,128)(2,1)}, u32[]{:S(2)}) copy-start(bf16[20,197,384]{2,1,0:T(8,128)(2,1)} %copy.67) | copy-start | bytes 9077764
  574.8 12.4 %copy-start.9 = (bf16[20,197,384]{2,1,0:T(8,128)(2,1)S(1)}, bf16[20,197,384]{2,1,0:T(8,128)(2,1)}, u32[]{:S(2)}) copy-start(bf16[20,197,384]{2,1,0:T(8,128)(2,1)} %copy.68) | copy-start | bytes 9077764
  574.9 12.4 %copy-start.10 = (bf16[20,197,384]{2,1,0:T(8,128)(2,1)S(1)}, bf16[20,197,384]{2,1,0:T(8,128)(2,1)}, u32[]{:S(2)}) copy-start(bf16[20,197,384]{2,1,0:T(8,128)(2,1)} %copy.69) | copy-start | bytes 9077764
  587.2 28.7 %copy-start.32 = (f32[384]{0:T(512)S(1)}, f32[384]{0:T(512)}, u32[]{:S(2)}) copy-start(f32[384]{0:T(512)} %get-tuple-element.37) | copy-start | bytes 4612
  587.3 28.7 %copy-start.33 = (f32[1536]{0:T(1024)S(1)}, f32[1536]{0:T(1024)}, u32[]{:S(2)}) copy-start(f32[1536]{0:T(1024)} %get-tuple-element.61) | copy-start | bytes 18436
  587.3 28.7 %copy-start.36 = (f32[384]{0:T(512)S(1)}, f32[384]{0:T(512)}, u32[]{:S(2)}) copy-start(f32[384]{0:T(512)} %get-tuple-element.16) | copy-start | bytes 4612
  587.3 28.7 %copy-start.37 = (f32[384]{0:T(512)S(1)}, f32[384]{0:T(512)}, u32[]{:S(2)}) copy-start(f32[384]{0:T(512)} %get-tuple-element.20) | copy-start | bytes 4612
  588.9 16.9 %collective-permute-start.14 = (f32[16,384]{1,0:T(8,128)S(1)}, f32[16,384]{1,0:T(8,128)S(1)}, u32[]{:S(2)}, u32[]{:S(2)}) collective-permute-start(f32[16,384]{1,0:T(8,128)S(1)} %get-tuple-element.35), channel_id=1, source_target_pairs={{0,7},{1,8},{2,9},{3,10},{4,11},{5,12},{6,13},{7,14},{8,15},{9,16}... | collective-permute-start | bytes 73736
  591.2 17.5 %collective-permute-start.8 = (f32[16,384]{1,0:T(8,128)S(1)}, f32[16,384]{1,0:T(8,128)S(1)}, u32[]{:S(2)}, u32[]{:S(2)}) collective-permute-start(f32[16,384]{1,0:T(8,128)S(1)} %get-tuple-element.35), channel_id=1, source_target_pairs={{0,1},{1,2},{2,3},{3,4},{4,5},{5,6},{6,7},{7,8},{8,9},{9,10},{10,1... | collective-permute-start | bytes 73736
  596.2 14.4 %collective-permute-start.9 = (f32[16,384]{1,0:T(8,128)S(1)}, f32[16,384]{1,0:T(8,128)S(1)}, u32[]{:S(2)}, u32[]{:S(2)}) collective-permute-start(f32[16,384]{1,0:T(8,128)S(1)} %get-tuple-element.35), channel_id=1, source_target_pairs={{0,2},{1,3},{2,4},{3,5},{4,6},{5,7},{6,8},{7,9},{8,10},{9,11},{10,... | collective-permute-start | bytes 73736
  599.6 15.0 %collective-permute-start.7 = (f32[12,1152]{1,0:T(8,128)S(1)}, f32[12,1152]{1,0:T(8,128)S(1)}, u32[]{:S(2)}, u32[]{:S(2)}) collective-permute-start(f32[12,1152]{1,0:T(8,128)S(1)} %slice.33), channel_id=1, source_target_pairs={{0,8},{1,9},{2,10},{3,11},{4,12},{5,13},{6,14},{7,15},{8,16},{9,17... | collective-permute-start | bytes 165896
  602.4 57.0 %collective-permute-start = (f32[16,1152]{1,0:T(8,128)S(1)}, f32[16,1152]{1,0:T(8,128)S(1)}, u32[]{:S(2)}, u32[]{:S(2)}) collective-permute-start(f32[16,1152]{1,0:T(8,128)S(1)} %get-tuple-element.34), channel_id=1, source_target_pairs={{0,1},{1,2},{2,3},{3,4},{4,5},{5,6},{6,7},{7,8},{8,9},{9,10},{10,1... | collective-permute-start | bytes 221192
  605.9 54.8 %collective-permute-start.1 = (f32[16,1152]{1,0:T(8,128)S(1)}, f32[16,1152]{1,0:T(8,128)S(1)}, u32[]{:S(2)}, u32[]{:S(2)}) collective-permute-start(f32[16,1152]{1,0:T(8,128)S(1)} %get-tuple-element.34), channel_id=1, source_target_pairs={{0,2},{1,3},{2,4},{3,5},{4,6},{5,7},{6,8},{7,9},{8,10},{9,11},{10,... | collective-permute-start | bytes 221192
  608.7 56.9 %collective-permute-start.2 = (f32[16,1152]{1,0:T(8,128)S(1)}, f32[16,1152]{1,0:T(8,128)S(1)}, u32[]{:S(2)}, u32[]{:S(2)}) collective-permute-start(f32[16,1152]{1,0:T(8,128)S(1)} %get-tuple-element.34), channel_id=1, source_target_pairs={{0,3},{1,4},{2,5},{3,6},{4,7},{5,8},{6,9},{7,10},{8,11},{9,12},{10... | collective-permute-start | bytes 221192
  610.6 59.4 %collective-permute-start.3 = (f32[16,1152]{1,0:T(8,128)S(1)}, f32[16,1152]{1,0:T(8,128)S(1)}, u32[]{:S(2)}, u32[]{:S(2)}) collective-permute-start(f32[16,1152]{1,0:T(8,128)S(1)} %get-tuple-element.34), channel_id=1, source_target_pairs={{0,4},{1,5},{2,6},{3,7},{4,8},{5,9},{6,10},{7,11},{8,12},{9,13},{1... | collective-permute-start | bytes 221192
  614.6 59.0 %collective-permute-start.4 = (f32[16,1152]{1,0:T(8,128)S(1)}, f32[16,1152]{1,0:T(8,128)S(1)}, u32[]{:S(2)}, u32[]{:S(2)}) collective-permute-start(f32[16,1152]{1,0:T(8,128)S(1)} %get-tuple-element.34), channel_id=1, source_target_pairs={{0,5},{1,6},{2,7},{3,8},{4,9},{5,10},{6,11},{7,12},{8,13},{9,14},{... | collective-permute-start | bytes 221192
  659.4 26.8 %collective-permute-start.16 = (f32[16,1536]{1,0:T(8,128)S(1)}, f32[16,1536]{1,0:T(8,128)S(1)}, u32[]{:S(2)}, u32[]{:S(2)}) collective-permute-start(f32[16,1536]{1,0:T(8,128)S(1)} %get-tuple-element.36), channel_id=1, source_target_pairs={{0,1},{1,2},{2,3},{3,4},{4,5},{5,6},{6,7},{7,8},{8,9},{9,10},{10,1... | collective-permute-start | bytes 294920
  660.7 29.0 %collective-permute-start.17 = (f32[16,1536]{1,0:T(8,128)S(1)}, f32[16,1536]{1,0:T(8,128)S(1)}, u32[]{:S(2)}, u32[]{:S(2)}) collective-permute-start(f32[16,1536]{1,0:T(8,128)S(1)} %get-tuple-element.36), channel_id=1, source_target_pairs={{0,2},{1,3},{2,4},{3,5},{4,6},{5,7},{6,8},{7,9},{8,10},{9,11},{10,... | collective-permute-start | bytes 294920
  665.6 11.5 %collective-permute-start.5 = (f32[16,1152]{1,0:T(8,128)S(1)}, f32[16,1152]{1,0:T(8,128)S(1)}, u32[]{:S(2)}, u32[]{:S(2)}) collective-permute-start(f32[16,1152]{1,0:T(8,128)S(1)} %get-tuple-element.34), channel_id=1, source_target_pairs={{0,6},{1,7},{2,8},{3,9},{4,10},{5,11},{6,12},{7,13},{8,14},{9,15},... | collective-permute-start | bytes 221192
  670.0 9.0 %collective-permute-start.6 = (f32[16,1152]{1,0:T(8,128)S(1)}, f32[16,1152]{1,0:T(8,128)S(1)}, u32[]{:S(2)}, u32[]{:S(2)}) collective-permute-start(f32[16,1152]{1,0:T(8,128)S(1)} %get-tuple-element.34), channel_id=1, source_target_pairs={{0,7},{1,8},{2,9},{3,10},{4,11},{5,12},{6,13},{7,14},{8,15},{9,16}... | collective-permute-start | bytes 221192
  673.7 9.7 %collective-permute-start.23 = (f32[12,1536]{1,0:T(8,128)S(1)}, f32[12,1536]{1,0:T(8,128)S(1)}, u32[]{:S(2)}, u32[]{:S(2)}) collective-permute-start(f32[12,1536]{1,0:T(8,128)S(1)} %slice.35), channel_id=1, source_target_pairs={{0,8},{1,9},{2,10},{3,11},{4,12},{5,13},{6,14},{7,15},{8,16},{9,17... | collective-permute-start | bytes 221192
  677.1 15.2 %collective-permute-start.18 = (f32[16,1536]{1,0:T(8,128)S(1)}, f32[16,1536]{1,0:T(8,128)S(1)}, u32[]{:S(2)}, u32[]{:S(2)}) collective-permute-start(f32[16,1536]{1,0:T(8,128)S(1)} %get-tuple-element.36), channel_id=1, source_target_pairs={{0,3},{1,4},{2,5},{3,6},{4,7},{5,8},{6,9},{7,10},{8,11},{9,12},{10... | collective-permute-start | bytes 294920
  679.0 13.3 %collective-permute-start.19 = (f32[16,1536]{1,0:T(8,128)S(1)}, f32[16,1536]{1,0:T(8,128)S(1)}, u32[]{:S(2)}, u32[]{:S(2)}) collective-permute-start(f32[16,1536]{1,0:T(8,128)S(1)} %get-tuple-element.36), channel_id=1, source_target_pairs={{0,4},{1,5},{2,6},{3,7},{4,8},{5,9},{6,10},{7,11},{8,12},{9,13},{1... | collective-permute-start | bytes 294920
  683.4 8.9 %collective-permute-start.20 = (f32[16,1536]{1,0:T(8,128)S(1)}, f32[16,1536]{1,0:T(8,128)S(1)}, u32[]{:S(2)}, u32[]{:S(2)}) collective-permute-start(f32[16,1536]{1,0:T(8,128)S(1)} %get-tuple-element.36), channel_id=1, source_target_pairs={{0,5},{1,6},{2,7},{3,8},{4,9},{5,10},{6,11},{7,12},{8,13},{9,14},{... | collective-permute-start | bytes 294920
  686.2 6.1 collective-permute-start.21
  689.7 4.1 collective-permute-start.22
  (25 other events, 170.1 us)
Sparse Core Ops, SparseCore 0:
  10.9 58.2 all-gather.7
  72.1 52.7 all-gather.5
  564.2 102.3 reduce-scatter.7
where the time goes:
time: 714 us; the launch traced here: 702 us
  matrix products  218 us (31%)
  blocking collectives  206 us (29%)
  other arithmetic  118 us (17%)
  local copies, waits for them, and re-layouts  78.2 us (11%)
  starting transfers between devices  64.2 us (9%)
  between operations  15 us (2%)
    unnamed x2, blocking collectives  119 us
    unnamed x24, starting transfers between devices  64.1 us
    convert_element_type x1, other arithmetic, on_device(): hidden = hidden_full.astype(bf16)  58.8 us
    all_gather x1, blocking collectives, on_device(): lax.all_gather(qkv_weight, 'dp', axis=0, tiled=True)  49.5 us
    dot_general x1, matrix products, on_device(): jnp.einsum('isd,fd->isf', output_cotangent, down_full, preferred_element_...  39.9 us
    all_gather x1, blocking collectives, on_device(): lax.all_gather(proj_weight, 'dp', axis=0, tiled=True)  37.9 us
    unnamed x112, local copies, waits for them, and re-layouts  36 us
    dot_general x1, matrix products, attend_back(): jnp.einsum('iqhe,ikhe->ihqk', grad_mixed, value_rows, preferred_element_t...  21.5 us
  transfers between devices with their start and end apart: 27, of which 1 were waited for; matrix products, arithmetic and copies ran while one was open for 31% of the time, Pallas kernels for 0%

commit v1 on v0

v1 whole, which is shorter than its diff:
```python
import jax
import jax.numpy as jnp
from jax import lax
from jax.experimental import pallas as pl
from jax.experimental.pallas import tpu as pltpu
from jax.sharding import PartitionSpec as P

D = 384
H = 6
DH = 64
FF = 1536
S = 197
SR = 208
SL = 256
CH = 256
norm_eps = 1e-06
f32 = jnp.float32
bf16 = jnp.bfloat16
NN = (((1,), (0,)), ((), ()))
NT = (((1,), (1,)), ((), ()))
TN = (((0,), (0,)), ((), ()))


def dot(a, b, dims):
    return lax.dot_general(a, b, dims, preferred_element_type=f32)


def norm(x):
    c = x - jnp.mean(x, axis=-1, keepdims=True)
    r = lax.rsqrt(jnp.mean(c * c, axis=-1, keepdims=True) + norm_eps)
    return c * r, r


def for_parity(me, body):
    for parity in (0, 1):
        @pl.when((me & 1) == parity)
        def _():
            body(parity)


def attn_fwd(me_ref, ga_ref, gb_ref, x_ref, g_ref, b_ref, bias_ref,
             pt_ref, wt_ref, ot_ref, w_ref, a_s, wT_s, *, n):
    me = me_ref[0]
    rows_of = D // n

    @pl.when(pl.program_id(0) == 0)
    def _():
        a_s[...] = jnp.zeros_like(a_s)

        def gather(parity):
            for k in range(n):
                src = ga_ref if (k & 1) == parity else gb_ref
                w_ref[rows_of * k : rows_of * (k + 1), :] = src[(me ^ k) >> 1]

        for_parity(me, gather)
        wT_s[...] = w_ref[...].T

    n1, _ = norm(x_ref[0].astype(f32))
    a_s[:S, :] = (n1 * g_ref[...] + b_ref[...]).astype(bf16)
    for j in range(9):
        rows = slice(128 * j, 128 * (j + 1))
        pT = dot(wT_s[rows, :], a_s[...], NT) + bias_ref[rows, :]
        pt_ref[0, rows, :] = pT.astype(bf16)
    scale = 0.125 * 1.4426950408889634
    valid = lax.broadcasted_iota(jnp.int32, (16, SL), 0) < S - 192
    for h in range(H):
        qT = pt_ref[0, 64 * h : 64 * h + 64, :]
        kT = pt_ref[0, D + 64 * h : D + 64 * h + 64, :SR]
        vT = pt_ref[0, 2 * D + 64 * h : 2 * D + 64 * h + 64, :SR]
        z = dot(kT, qT, TN)
        zt = z[:192]
        zb = jnp.where(valid, z[192:], -jnp.inf)
        m = jnp.maximum(jnp.max(zt, axis=0, keepdims=True), jnp.max(zb, axis=0, keepdims=True))
        et = jnp.exp2((zt - m) * scale)
        eb = jnp.exp2((zb - m) * scale)
        l = jnp.sum(et, axis=0, keepdims=True) + jnp.sum(eb, axis=0, keepdims=True)
        inv = 1.0 / l
        wt_ref[0, h, :192, :] = (et * inv).astype(bf16)
        wt_ref[0, h, 192:, :] = (eb * inv).astype(bf16)
        ot_ref[0, 64 * h : 64 * h + 64, :] = dot(vT, wt_ref[0, h], NN).astype(bf16)


ERF_P = 0.3275911
ERF_A = (0.254829592, -0.284496736, 1.421413741, -1.453152027, 1.061405429)


def gelu_parts(u):
    e = jnp.exp2(u * u * (-0.5 * 1.4426950408889634))
    t = 1.0 / (1.0 + jnp.abs(u) * (ERF_P * 0.7071067811865476))
    poly = ERF_A[4] * 0.5
    for a in ERF_A[3::-1]:
        poly = poly * t + a * 0.5
    q = poly * t * e
    phi = jnp.where(u >= 0, 1.0 - q, q)
    return u * phi, phi + u * (e * 0.3989422804014327)


def spread(vec, width, shift, n):
    size = n * width
    d = lax.broadcasted_iota(jnp.int32, (n, size), 1)
    k = lax.broadcasted_iota(jnp.int32, (n, size), 0)
    picked = jnp.where(d // width == k, jnp.broadcast_to(vec, (n, size)), 0.0).astype(bf16)
    dd = lax.broadcasted_iota(jnp.int32, (size, 128), 0)
    j = lax.broadcasted_iota(jnp.int32, (size, 128), 1)
    place = jnp.where(dd % width + shift == j, 1.0, 0.0).astype(bf16)
    return dot(picked, place, NN)


def emit(me, stage, keep_ref, send_ref, n, bits):
    def one(k, carry):
        m = me ^ k
        pos = 0
        for b in bits:
            pos = pos * 2 + ((m >> b) & 1)

        @pl.when((m & 1) == 0)
        def _():
            keep_ref[pos] = stage[k]

        @pl.when((m & 1) == 1)
        def _():
            send_ref[pos] = stage[k].astype(bf16)
        return carry

    lax.fori_loop(0, n, one, 0)


def mlp(me_ref, ga_ref, gb_ref, x_ref, ot_ref, e_ref, pb_ref, g_ref, b_ref, ub_ref, db_ref,
        out_ref, dx1_ref, dot_ref, keep_ref, send_ref,
        xs, es, fs, pj_s, up_s, dn_s, gup, gdn, gpj, small, stage, *, n, bits):
    me = me_ref[0]
    step = pl.program_id(0)
    r1, r4 = D // n, FF // n

    @pl.when(step == 0)
    def _():
        xs[...] = jnp.zeros_like(xs)
        es[...] = jnp.zeros_like(es)
        fs[...] = jnp.zeros_like(fs)
        gup[...] = jnp.zeros_like(gup)
        gdn[...] = jnp.zeros_like(gdn)
        gpj[...] = jnp.zeros_like(gpj)
        small[...] = jnp.zeros_like(small)

        def gather(parity):
            for k in range(n):
                src = ga_ref if (k & 1) == parity else gb_ref
                part = src[(me ^ k) >> 1]
                rows = slice(r1 * k, r1 * (k + 1))
                pj_s[rows, :] = part[:r1]
                for q in range(4):
                    up_s[rows, D * q : D * (q + 1)] = part[r1 * (1 + q) : r1 * (2 + q)]
                dn_s[r4 * k : r4 * (k + 1), :] = part[5 * r1 :]

        for_parity(me, gather)

    xs[:S, :] = x_ref[0]
    es[:S, :] = e_ref[0]
    oT = ot_ref[0, :, :SR]
    x1 = xs[...].astype(f32) + dot(oT, pj_s[...], TN) + pb_ref[...]
    n2, r2 = norm(x1)
    bb = (n2 * g_ref[...] + b_ref[...]).astype(bf16)
    bT = bb.T
    e2 = es[...]
    eT = e2.T
    acc = x1 + db_ref[...]
    dB = jnp.zeros((SR, D), f32)

    def fold(v):
        return jnp.sum(v.reshape(SR // 8, 8, v.shape[1]), axis=0)

    for c in range(FF // CH):
        cols = slice(c * CH, (c + 1) * CH)
        u = dot(bb, up_s[:, cols], NN) + ub_ref[:, cols]
        g, gp = gelu_parts(u)
        gb = g.astype(bf16)
        acc = acc + dot(gb, dn_s[cols, :], NN)
        dU = (dot(e2, dn_s[cols, :], NT) * gp).astype(bf16)
        small[:, FF + c * CH : FF + (c + 1) * CH] += fold(dU.astype(f32))
        dB = dB + dot(dU, up_s[:, cols], NT)
        gdn[:, cols] += dot(eT, gb, NN)
        gup[:, cols] += dot(bT, dU, NN)
    out_ref[0] = acc[:S]
    dn = dB * g_ref[...]
    ef = e2.astype(f32)
    dx1 = ef + r2 * (dn - jnp.mean(dn, axis=-1, keepdims=True) - n2 * jnp.mean(dn * n2, axis=-1, keepdims=True))
    dx1_ref[0] = dx1[:S]
    ff = dx1.astype(bf16)
    fs[:SR, :] = ff
    small[:, 0:D] += fold(dB * n2)
    small[:, D : 2 * D] += fold(dB)
    small[:, 2 * D : 3 * D] += fold(ff.astype(f32))
    small[:, 3 * D : 4 * D] += fold(ef)
    gpj[...] += dot(oT, ff, NN)
    dot_ref[0] = dot(pj_s[...], fs[...], NT).astype(bf16)

    @pl.when(step == pl.num_programs(0) - 1)
    def _():
        tot = jnp.sum(small[...], axis=0, keepdims=True)
        sm = spread(tot[:, FF:], r4, 4 * r1, n)
        for q in range(4):
            sm = sm + spread(tot[:, D * q : D * (q + 1)], r1, r1 * q, n)
        for k in range(n):
            rows = slice(r1 * k, r1 * (k + 1))
            stage[k, :r1, :] = gpj[rows, :]
            for q in range(4):
                stage[k, r1 * (1 + q) : r1 * (2 + q), :] = gup[rows, D * q : D * (q + 1)]
            stage[k, 9 * r1 : 9 * r1 + 1, :128] = sm[k : k + 1]
        for c in range(FF // 384):
            gT = gdn[:, 384 * c : 384 * (c + 1)].T
            for k in range(384 // r4):
                stage[c * (384 // r4) + k, 5 * r1 : 9 * r1, :] = gT[r4 * k : r4 * (k + 1)]
        emit(me, stage, keep_ref, send_ref, n, bits)


def attn_bwd(me_ref, x_ref, pt_ref, wt_ref, dot_ref, dx1_ref, g_ref, b_ref, w_ref,
             din_ref, keep_ref, send_ref, as_, dp_s, gq, small, stage, *, n, bits):
    me = me_ref[0]
    step = pl.program_id(0)
    r1 = D // n

    @pl.when(step == 0)
    def _():
        as_[:, :D] = jnp.zeros((SR, D), bf16)
        as_[:, D:] = jnp.ones((SR, 128), bf16)
        gq[...] = jnp.zeros_like(gq)
        small[...] = jnp.zeros_like(small)

    n1, rr = norm(x_ref[0].astype(f32))
    as_[:S, :D] = (n1 * g_ref[...] + b_ref[...]).astype(bf16)
    for h in range(H):
        hs = slice(64 * h, 64 * h + 64)
        ks = slice(D + 64 * h, D + 64 * h + 64)
        vs = slice(2 * D + 64 * h, 2 * D + 64 * h + 64)
        qT = pt_ref[0, hs, :]
        kT = pt_ref[0, ks, :SR]
        vT = pt_ref[0, vs, :SR]
        doT = dot_ref[0, hs, :]
        wt = wt_ref[0, h]
        w = wt.astype(f32)
        dW = dot(vT, doT, TN)
        t = dW * w
        dZ = (t - w * jnp.sum(t, axis=0, keepdims=True)).astype(bf16)
        dp_s[hs, :] = (dot(kT, dZ, NN) * 0.125)[:, :SR].astype(bf16)
        dp_s[ks, :] = (dot(qT, dZ, NT) * 0.125).astype(bf16)
        dp_s[vs, :] = dot(doT, wt, NT).astype(bf16)
    gq[...] += dot(dp_s[...], as_[...], NN)
    dA = dot(dp_s[...], w_ref[...], (((0,), (1,)), ((), ())))[:S]
    dm = dA * g_ref[...]
    din_ref[0] = dx1_ref[0] + rr * (
        dm - jnp.mean(dm, axis=-1, keepdims=True) - n1 * jnp.mean(dm * n1, axis=-1, keepdims=True))
    small[0:1, 0:D] += jnp.sum(dA * n1, axis=0, keepdims=True)
    small[0:1, D : 2 * D] += jnp.sum(dA, axis=0, keepdims=True)

    @pl.when(step == pl.num_programs(0) - 1)
    def _():
        cs = gq[:, D : D + 128].T[0:1, :]
        sm = spread(small[0:1, :D], r1, 0, n) + spread(small[0:1, D : 2 * D], r1, r1, n)
        sm = sm + spread(jnp.concatenate([cs[:, :D], cs[:, 2 * D :]], axis=1), 2 * r1, 2 * r1, n)
        for q in range(3):
            gT = gq[D * q : D * (q + 1), :D].T
            for k in range(n):
                stage[k, r1 * q : r1 * (q + 1), :] = gT[r1 * k : r1 * (k + 1)]
        for k in range(n):
            stage[k, 3 * r1 : 3 * r1 + 1, :128] = sm[k : k + 1]
        emit(me, stage, keep_ref, send_ref, n, bits)


def img(shape):
    return pl.BlockSpec((1,) + shape, lambda i: (i,) + (0,) * len(shape))


def res(shape):
    return pl.BlockSpec(shape, lambda i: (0,) * len(shape))


smem = pl.BlockSpec(memory_space=pltpu.SMEM)
params = pltpu.CompilerParams(dimension_semantics=("arbitrary",), vmem_limit_bytes=60 * 2**20)


def shape_of(*dims, dtype=f32):
    return jax.ShapeDtypeStruct(dims, dtype)


def run_fwd(n, me, ga, gb, x, g1, b1, bias):
    m = x.shape[0]
    return pl.pallas_call(
        lambda *refs: attn_fwd(*refs, n=n), grid=(m,), name="attn_fwd",
        in_specs=[smem, res(ga.shape), res(gb.shape), img((S, D)), res((1, D)), res((1, D)), res((3 * D, SL))],
        out_specs=[img((3 * D, SL)), img((H, SR, SL)), img((D, SL)), res((D, 3 * D))],
        out_shape=[shape_of(m, 3 * D, SL, dtype=bf16), shape_of(m, H, SR, SL, dtype=bf16),
                   shape_of(m, D, SL, dtype=bf16), shape_of(D, 3 * D, dtype=bf16)],
        scratch_shapes=[pltpu.VMEM((SL, D), bf16), pltpu.VMEM((3 * D, D), bf16)],
        compiler_params=params,
    )(me, ga, gb, x, g1, b1, bias)


def chunk_rows(n, parts):
    return -(-(parts * (D // n) + 1) // 16) * 16


def run_mlp(n, bits, me, ga, gb, x, oT, e, pb, g2, b2, ub, db):
    m = x.shape[0]
    cr = chunk_rows(n, 9)
    return pl.pallas_call(
        lambda *refs: mlp(*refs, n=n, bits=bits), grid=(m,), name="mlp",
        in_specs=[smem, res(ga.shape), res(gb.shape), img((S, D)), img((D, SL)), img((S, D)),
                  res((1, D)), res((1, D)), res((1, D)), res((1, FF)), res((1, D))],
        out_specs=[img((S, D)), img((S, D)), img((D, SL)), res((n // 2, cr, D)), res((n // 2, cr, D))],
        out_shape=[shape_of(m, S, D), shape_of(m, S, D), shape_of(m, D, SL, dtype=bf16),
                   shape_of(n // 2, cr, D), shape_of(n // 2, cr, D, dtype=bf16)],
        scratch_shapes=[pltpu.VMEM((SR, D), bf16), pltpu.VMEM((SR, D), bf16), pltpu.VMEM((SL, D), bf16),
                        pltpu.VMEM((D, D), bf16), pltpu.VMEM((D, FF), bf16), pltpu.VMEM((FF, D), bf16),
                        pltpu.VMEM((D, FF), f32), pltpu.VMEM((D, FF), f32), pltpu.VMEM((D, D), f32),
                        pltpu.VMEM((8, 2 * FF), f32), pltpu.VMEM((n, cr, D), f32)],
        compiler_params=params,
    )(me, ga, gb, x, oT, e, pb, g2, b2, ub, db)


def run_bwd(n, bits, me, x, pt, wt, doT, dx1, g1, b1, qkv):
    m = x.shape[0]
    cr = chunk_rows(n, 3)
    return pl.pallas_call(
        lambda *refs: attn_bwd(*refs, n=n, bits=bits), grid=(m,), name="attn_bwd",
        in_specs=[smem, img((S, D)), img((3 * D, SL)), img((H, SR, SL)), img((D, SL)), img((S, D)),
                  res((1, D)), res((1, D)), res((D, 3 * D))],
        out_specs=[img((S, D)), res((n // 2, cr, D)), res((n // 2, cr, D))],
        out_shape=[shape_of(m, S, D), shape_of(n // 2, cr, D), shape_of(n // 2, cr, D, dtype=bf16)],
        scratch_shapes=[pltpu.VMEM((SR, 512), bf16), pltpu.VMEM((3 * D, SR), bf16),
                        pltpu.VMEM((3 * D, 512), f32), pltpu.VMEM((8, 2 * D), f32), pltpu.VMEM((n, cr, D), f32)],
        compiler_params=params,
    )(me, x, pt, wt, doT, dx1, g1, b1, qkv)


def swap(v, bit, n):
    return lax.ppermute(v, "dp", [(i, i ^ (1 << bit)) for i in range(n)])


def gather_halves(v, n, bits):
    v = v[None]
    for b in range(1, bits):
        v = jnp.concatenate([v, swap(v, b, n)], axis=0)
    return v, swap(v, 0, n)


def reduce_parts(keep, send, n, bits):
    total = keep + swap(send, 0, n).astype(f32)
    for b in bits:
        half = total.shape[0] // 2
        total = total[:half] + swap(total[half:].astype(bf16), b, n).astype(f32)
    return total[0]


def on_device(n, block_input, first_gain, first_shift, qkv_weight, query_value_bias, proj_weight, proj_bias,
              second_gain, second_shift, up_weight, up_bias, down_weight, down_bias, output_cotangent):
    n_bits = n.bit_length() - 1
    bits = tuple(range(1, n_bits))
    r1, r4 = D // n, FF // n
    me = lax.axis_index("dp").astype(jnp.int32).reshape(1)

    def row(v):
        return v.reshape(1, -1)

    bias = jnp.concatenate([query_value_bias[:D], jnp.zeros((D,), f32), query_value_bias[D:]])
    bias = jnp.broadcast_to(bias[:, None], (3 * D, SL))
    qa, qb = gather_halves(qkv_weight, n, n_bits)
    rest = jnp.concatenate(
        [proj_weight] + [up_weight[:, D * q : D * (q + 1)] for q in range(4)] + [down_weight], axis=0)
    wa, wb = gather_halves(rest, n, n_bits)
    pt, wt, oT, qkv = run_fwd(n, me, qa, qb, block_input, row(first_gain), row(first_shift), bias)
    out, dx1, doT, keep, send = run_mlp(
        n, bits, me, wa, wb, block_input, oT, output_cotangent, row(proj_bias), row(second_gain),
        row(second_shift), row(up_bias), row(down_bias))
    mp = reduce_parts(keep, send, n, bits)
    din, keep, send = run_bwd(n, bits, me, block_input, pt, wt, doT, dx1, row(first_gain), row(first_shift), qkv)
    ap = reduce_parts(keep, send, n, bits)
    g_up = jnp.concatenate([mp[r1 * (1 + q) : r1 * (2 + q)] for q in range(4)], axis=1)
    g_qkv = jnp.concatenate([ap[r1 * q : r1 * (q + 1)] for q in range(3)], axis=1)
    sm, sa = mp[9 * r1], ap[3 * r1]
    return (out, din, sa[:r1], sa[r1 : 2 * r1], g_qkv, sa[2 * r1 : 4 * r1], mp[:r1], sm[2 * r1 : 3 * r1],
            sm[:r1], sm[r1 : 2 * r1], g_up, sm[4 * r1 : 4 * r1 + r4], mp[5 * r1 : 9 * r1], sm[3 * r1 : 4 * r1])


def solution(mesh):
    rows, vec, imgs = P("dp", None), P("dp"), P("dp", None, None)
    n = mesh.shape["dp"]
    return jax.shard_map(
        lambda *args: on_device(n, *args), mesh=mesh,
        in_specs=(imgs, P(), P(), rows, P(), rows, P(), P(), P(), rows, P(), rows, P(), imgs),
        out_specs=(imgs, imgs, vec, vec, rows, vec, rows, vec, vec, vec, rows, vec, rows, vec),
        check_vma=False)
```

time: 714 us -> 349 us (0.49); the launches traced: 702 us -> 348 us
  matrix products: 218 us -> 0 us
  Pallas kernels: 0 us -> 215 us
  blocking collectives: 206 us -> 0 us
  other arithmetic: 118 us -> 3.75 us
  waiting for transfers between devices: 3.02 us -> 90.9 us
  local copies, waits for them, and re-layouts: 78.2 us -> 17.1 us
  starting transfers between devices: 64.2 us -> 20.6 us
  between operations: 15 us -> 1.05 us
    pallas_call x0 -> x3, Pallas kernels: none -> 215 us  [the longest x1 105 us: run_mlp(): pl.pallas_call(lambda *refs: mlp(*refs, n=n, bits=bits), grid=(m,), name=...]
    dot_general x17 -> x0, matrix products: 202 us -> none  [the longest x1 39.9 us: on_device(): jnp.einsum('isd,fd->isf', output_cotangent, down_full, preferred_element_...]
    unnamed x2 -> x0, blocking collectives: 119 us -> none
    ppermute x0 -> x20, waiting for transfers between devices: none -> 90.9 us  [swap(): return lax.ppermute(v, 'dp', [(i, i ^ 1 << bit) for i in range(n)])]
    convert_element_type x3 -> x0, other arithmetic: 88.7 us -> none  [the longest x1 58.8 us: on_device(): hidden = hidden_full.astype(bf16)]
    all_gather x2 -> x0, blocking collectives: 87.5 us -> none  [the longest x1 49.5 us: on_device(): lax.all_gather(qkv_weight, 'dp', axis=0, tiled=True)]
    unnamed x24 -> x0, starting transfers between devices: 64.1 us -> none
    unnamed x112 -> x34, local copies, waits for them, and re-layouts: 36 us -> 0.99 us
  transfers between devices with their start and end apart: 27 -> 20, of which waited for: 1 -> 14; matrix products, arithmetic and copies ran while one was open for 31% -> 4% of each run, Pallas kernels for 0% -> 16%
where the time goes in v1:
time: 349 us; the launch traced here: 348 us
  Pallas kernels  215 us (62%)
  waiting for transfers between devices  90.9 us (26%)
  starting transfers between devices  20.6 us (6%)
  local copies, waits for them, and re-layouts  17.1 us (5%)
  other arithmetic  3.75 us (1%)
    pallas_call x1, Pallas kernels, run_mlp(): pl.pallas_call(lambda *refs: mlp(*refs, n=n, bits=bits), grid=(m,), name=...  105 us
    ppermute x20, waiting for transfers between devices, swap(): return lax.ppermute(v, 'dp', [(i, i ^ 1 << bit) for i in range(n)])  90.9 us
    pallas_call x1, Pallas kernels, run_bwd(): pl.pallas_call(lambda *refs: attn_bwd(*refs, n=n, bits=bits), grid=(m,),...  55.4 us
    pallas_call x1, Pallas kernels, run_fwd(): pl.pallas_call(lambda *refs: attn_fwd(*refs, n=n), grid=(m,), name='attn_...  54.9 us
    ppermute x20, starting transfers between devices, swap(): return lax.ppermute(v, 'dp', [(i, i ^ 1 << bit) for i in range(n)])  20.6 us
  transfers between devices with their start and end apart: 20, of which 14 were waited for; matrix products, arithmetic and copies ran while one was open for 4% of the time, Pallas kernels for 16%

profile of v1, /device:TPU:0, one launch (start us, length us, event | category | flops | bytes accessed | tf_op | source)
XLA Modules:
  0.0 348.3 jit_solution(1675578320165560305)
XLA Ops:
  0.7 0.8 fusion
  1.4 1.8 concatenate.42
  3.3 3.0 collective-permute-start
  6.4 2.6 collective-permute-done
  9.0 2.3 collective-permute-start.1
  11.3 0.8 constant_dynamic-update-slice_fusion.8
  12.1 2.6 collective-permute-done.1
  14.8 2.1 collective-permute-start.2
  17.0 1.6 collective-permute-start.6
  18.5 4.0 %collective-permute-done.2 = bf16[4,108,384]{2,1,0:T(8,128)(2,1)S(1)} collective-permute-done((bf16[4,108,384]{2,1,0:T(8,128)(2,1)S(1)}, bf16[4,108,384]{2,1,0:T(8,128)(2,1)S(1)}, u32[]{:S(2)}, u32[]{:S(2)}) %collective-permute-start.2) | collective-permute-done | bytes 331808 | tf_op jit(solution)/shard_map/ppermute | solution.py:336
  22.8 3.9 %collective-permute-start.3 = (bf16[8,108,384]{2,0,1:T(8,128)(2,1)S(1)}, bf16[8,108,384]{2,0,1:T(8,128)(2,1)S(1)}, u32[]{:S(2)}, u32[]{:S(2)}) collective-permute-start(bf16[8,108,384]{2,0,1:T(8,128)(2,1)S(1)} %copy.28), channel_id=1, source_target_pairs={{0,16},{1,17},{2,18},{3,19},{4,20},{5,21},{6,22},{7,23},{8,24},{9,... | collective-permute-start | bytes 1990664 | tf_op jit(solution)/shard_map/ppermute | solution.py:336
  26.8 1.5 collective-permute-start.7
  28.3 23.3 %collective-permute-done.3 = bf16[8,108,384]{2,0,1:T(8,128)(2,1)S(1)} collective-permute-done((bf16[8,108,384]{2,0,1:T(8,128)(2,1)S(1)}, bf16[8,108,384]{2,0,1:T(8,128)(2,1)S(1)}, u32[]{:S(2)}, u32[]{:S(2)}) %collective-permute-start.3) | collective-permute-done | bytes 663584 | tf_op jit(solution)/shard_map/ppermute | solution.py:336
  51.8 1.5 copy.30
  53.7 16.6 %collective-permute-done.8 = bf16[8,12,1152]{2,1,0:T(8,128)(2,1)S(1)} collective-permute-done((bf16[8,12,1152]{2,1,0:T(8,128)(2,1)S(1)}, bf16[8,12,1152]{2,1,0:T(8,128)(2,1)S(1)}, u32[]{:S(2)}, u32[]{:S(2)}) %collective-permute-start.8) | collective-permute-done | bytes 221216 | tf_op jit(solution)/shard_map/ppermute | solution.py:336
  70.5 0.6 reshape.77.refs_4_.refs_6_
  71.6 0.6 reshape.82.refs_9_
  72.8 0.6 reshape.80.refs_7_
  73.4 0.6 reshape.81.refs_8_
  74.5 1.0 copy.32.refs_2_
  75.5 1.3 broadcast_in_dim.18.refs_6_
  76.8 54.9 %attn_fwd.1 = (bf16[20,1152,256]{2,1,0:T(8,128)(2,1)}, bf16[20,6,208,256]{3,2,1,0:T(8,128)(2,1)}, bf16[20,384,256]{2,1,0:T(8,128)(2,1)}, bf16[384,1152]{1,0:T(8,128)(2,1)}) custom-call(s32[1]{0:T(128)} %bitcast.refs_0_, bf16[16,12,1152]{2,1,0:T(8,128)(2,1)} %copy-done.2, bf16[16,12,1152]{2,1,0:T(8,128)(2,1)} %copy.32.refs_2_, bf16[20,197,384]{2,1,0:T(8,128)(2,1)} %refs_1_.1, ...), custom_call_target="tpu_custom_call" | custom-call | tf_op jit(solution)/shard_map/attn_fwd/pallas_call | solution.py:287
  131.7 1.4 copy.33.refs_2_
  133.2 104.6 %mlp.1 = (f32[20,197,384]{2,1,0:T(8,128)}, f32[20,197,384]{2,1,0:T(8,128)}, bf16[20,384,256]{2,1,0:T(8,128)(2,1)}, f32[16,112,384]{2,1,0:T(8,128)}, bf16[16,112,384]{2,1,0:T(8,128)(2,1)}) custom-call(s32[1]{0:T(128)} %bitcast.refs_0_, bf16[16,108,384]{2,1,0:T(8,128)(2,1)} %copy-done, bf16[16,108,384]{2,1,0:T(8,128)(2,1)} %copy.33.refs_2_, ...), custom_call_target="tpu_custom_call" | custom-call | tf_op jit(solution)/shard_map/mlp/pallas_call | solution.py:305
  237.8 55.4 %attn_bwd.1 = (f32[20,197,384]{2,1,0:T(8,128)}, f32[16,48,384]{2,1,0:T(8,128)}, bf16[16,48,384]{2,1,0:T(8,128)(2,1)}) custom-call(s32[1]{0:T(128)} %bitcast.refs_0_, bf16[20,197,384]{2,1,0:T(8,128)(2,1)} %refs_1_.1, bf16[20,1152,256]{2,1,0:T(8,128)(2,1)} %get-tuple-element.28.refs_2_, bf16[20,6,208,256]{3,2,1,0:T(8,128)(2,1)} %get-tuple-element.29.refs_3_, ...), custom_call_target="tpu_custom_call" | custom-call | tf_op jit(solution)/shard_map/attn_bwd/pallas_call | solution.py:323
  293.1 0.6 collective-permute-start.10
  293.8 1.8 collective-permute-done.10
  295.5 1.6 convert_add_fusion.1
  297.1 1.1 collective-permute-start.11
  298.2 8.3 %collective-permute-done.11 = bf16[8,48,384]{2,1,0:T(8,128)(2,1)S(1)} collective-permute-done((bf16[8,48,384]{2,1,0:T(8,128)(2,1)S(1)}, bf16[8,48,384]{2,1,0:T(8,128)(2,1)S(1)}, u32[]{:S(2)}, u32[]{:S(2)}) %collective-permute-start.11) | collective-permute-done | bytes 294944 | tf_op jit(solution)/shard_map/ppermute | solution.py:336
  306.6 0.9 collective-permute-start.12
  307.8 1.8 collective-permute-start.16
  309.6 2.3 collective-permute-done.12
  312.1 4.3 %collective-permute-done.13 = bf16[2,48,384]{2,1,0:T(8,128)(2,1)S(1)} collective-permute-done((bf16[2,48,384]{2,1,0:T(8,128)(2,1)S(1)}, bf16[2,48,384]{2,1,0:T(8,128)(2,1)S(1)}, u32[]{:S(2)}, u32[]{:S(2)}) %collective-permute-start.13) | collective-permute-done | bytes 73760 | tf_op jit(solution)/shard_map/ppermute | solution.py:336
  316.5 4.8 %collective-permute-done.14 = bf16[1,48,384]{2,1,0:T(8,128)(2,1)S(1)} collective-permute-done((bf16[1,48,384]{2,1,0:T(8,128)(2,1)S(1)}, bf16[1,48,384]{2,1,0:T(8,128)(2,1)S(1)}, u32[]{:S(2)}, u32[]{:S(2)}) %collective-permute-start.14) | collective-permute-done | bytes 36896 | tf_op jit(solution)/shard_map/ppermute | solution.py:336
  321.4 3.2 collective-permute-done.16
  324.7 1.2 collective-permute-start.17
  325.9 0.6 pad_maximum_fusion.7
  326.5 6.6 %collective-permute-done.17 = bf16[4,112,384]{2,1,0:T(8,128)(2,1)S(1)} collective-permute-done((bf16[4,112,384]{2,1,0:T(8,128)(2,1)S(1)}, bf16[4,112,384]{2,1,0:T(8,128)(2,1)S(1)}, u32[]{:S(2)}, u32[]{:S(2)}) %collective-permute-start.17) | collective-permute-done | bytes 344096 | tf_op jit(solution)/shard_map/ppermute | solution.py:336
  333.4 0.6 slice_bitcast_fusion.15
  334.0 4.8 %collective-permute-done.18 = bf16[2,112,384]{2,1,0:T(8,128)(2,1)S(1)} collective-permute-done((bf16[2,112,384]{2,1,0:T(8,128)(2,1)S(1)}, bf16[2,112,384]{2,1,0:T(8,128)(2,1)S(1)}, u32[]{:S(2)}, u32[]{:S(2)}) %collective-permute-start.18) | collective-permute-done | bytes 172064 | tf_op jit(solution)/shard_map/ppermute | solution.py:336
  338.9 0.6 slice_bitcast_fusion.14
  339.5 5.7 %collective-permute-done.19 = bf16[1,112,384]{2,1,0:T(8,128)(2,1)S(1)} collective-permute-done((bf16[1,112,384]{2,1,0:T(8,128)(2,1)S(1)}, bf16[1,112,384]{2,1,0:T(8,128)(2,1)S(1)}, u32[]{:S(2)}, u32[]{:S(2)}) %collective-permute-start.19) | collective-permute-done | bytes 86048 | tf_op jit(solution)/shard_map/ppermute | solution.py:336
  345.2 0.6 slice_bitcast_fusion.4
  345.8 0.6 slice_bitcast_fusion
  346.5 0.6 slice_bitcast_fusion.9
  347.1 0.6 slice_bitcast_fusion.10
  347.6 0.6 pad_maximum_fusion.5
  (82 shorter events, 4.1 us)
Async XLA Ops:
  0.6 16.3 %copy-start.3 = (bf16[12,1152]{1,0:T(8,128)(2,1)S(1)}, bf16[12,1152]{1,0:T(8,128)(2,1)}, u32[]{:S(2)}) copy-start(bf16[12,1152]{1,0:T(8,128)(2,1)} %param.17) | copy-start | bytes 82948
  3.3 5.7 %collective-permute-start = (bf16[1,108,384]{2,1,0:T(8,128)(2,1)S(1)}, bf16[1,108,384]{2,1,0:T(8,128)(2,1)S(1)}, u32[]{:S(2)}, u32[]{:S(2)}) collective-permute-start(bf16[1,108,384]{2,1,0:T(8,128)(2,1)S(1)} %bitcast.39), channel_id=1, source_target_pairs={{0,2},{1,3},{2,0},{3,1},{4,6},{5,7},{6,4},{7,5},{8,10},{9,11},{10,... | collective-permute-start | bytes 248840 | tf_op jit(solution)/shard_map/ppermute | solution.py:336
  6.3 10.6 %collective-permute-start.5 = (bf16[1,12,1152]{2,1,0:T(8,128)(2,1)}, bf16[1,12,1152]{2,1,0:T(8,128)(2,1)S(1)}, u32[]{:S(2)}, u32[]{:S(2)}) collective-permute-start(bf16[1,12,1152]{2,1,0:T(8,128)(2,1)} %bitcast.43), channel_id=1, source_target_pairs={{0,2},{1,3},{2,0},{3,1},{4,6},{5,7},{6,4},{7,5},{8,10},{9,11},{10,... | collective-permute-start | bytes 82952 | tf_op jit(solution)/shard_map/ppermute | solution.py:336
  9.0 5.7 %collective-permute-start.1 = (bf16[2,108,384]{2,1,0:T(8,128)(2,1)S(1)}, bf16[2,108,384]{2,1,0:T(8,128)(2,1)S(1)}, u32[]{:S(2)}, u32[]{:S(2)}) collective-permute-start(bf16[2,108,384]{2,1,0:T(8,128)(2,1)S(1)} %pad_maximum_fusion.3), channel_id=1, source_target_pairs={{0,4},{1,5},{2,6},{3,7},{4,0},{5,1},{6,2},{7,3},{8,12},{9,13},{10,... | collective-permute-start | bytes 497672 | tf_op jit(solution)/shard_map/ppermute | solution.py:336
  14.8 7.8 %collective-permute-start.2 = (bf16[4,108,384]{2,1,0:T(8,128)(2,1)S(1)}, bf16[4,108,384]{2,1,0:T(8,128)(2,1)S(1)}, u32[]{:S(2)}, u32[]{:S(2)}) collective-permute-start(bf16[4,108,384]{2,1,0:T(8,128)(2,1)S(1)} %pad_maximum_fusion.1), channel_id=1, source_target_pairs={{0,8},{1,9},{2,10},{3,11},{4,12},{5,13},{6,14},{7,15},{8,0},{9,1},... | collective-permute-start | bytes 995336 | tf_op jit(solution)/shard_map/ppermute | solution.py:336
  17.0 9.8 %collective-permute-start.6 = (bf16[2,12,1152]{2,1,0:T(8,128)(2,1)S(1)}, bf16[2,12,1152]{2,1,0:T(8,128)(2,1)S(1)}, u32[]{:S(2)}, u32[]{:S(2)}) collective-permute-start(bf16[2,12,1152]{2,1,0:T(8,128)(2,1)S(1)} %pad_maximum_fusion.6), channel_id=1, source_target_pairs={{0,4},{1,5},{2,6},{3,7},{4,0},{5,1},{6,2},{7,3},{8,12},{9,13},{10,... | collective-permute-start | bytes 165896 | tf_op jit(solution)/shard_map/ppermute | solution.py:336
  22.8 28.8 %collective-permute-start.3 = (bf16[8,108,384]{2,0,1:T(8,128)(2,1)S(1)}, bf16[8,108,384]{2,0,1:T(8,128)(2,1)S(1)}, u32[]{:S(2)}, u32[]{:S(2)}) collective-permute-start(bf16[8,108,384]{2,0,1:T(8,128)(2,1)S(1)} %copy.28), channel_id=1, source_target_pairs={{0,16},{1,17},{2,18},{3,19},{4,20},{5,21},{6,22},{7,23},{8,24},{9,... | collective-permute-start | bytes 1990664 | tf_op jit(solution)/shard_map/ppermute | solution.py:336
  26.8 26.7 %collective-permute-start.7 = (bf16[4,12,1152]{2,1,0:T(8,128)(2,1)S(1)}, bf16[4,12,1152]{2,1,0:T(8,128)(2,1)S(1)}, u32[]{:S(2)}, u32[]{:S(2)}) collective-permute-start(bf16[4,12,1152]{2,1,0:T(8,128)(2,1)S(1)} %pad_maximum_fusion.4), channel_id=1, source_target_pairs={{0,8},{1,9},{2,10},{3,11},{4,12},{5,13},{6,14},{7,15},{8,0},{9,1},... | collective-permute-start | bytes 331784 | tf_op jit(solution)/shard_map/ppermute | solution.py:336
  51.8 1.7 copy-start
  53.3 17.1 %copy-start.6 = (f32[384]{0:T(512)S(1)}, f32[384]{0:T(512)}, u32[]{:S(2)}) copy-start(f32[384]{0:T(512)} %param.15) | copy-start | bytes 4612
  53.3 17.7 %copy-start.7 = (f32[384]{0:T(512)S(1)}, f32[384]{0:T(512)}, u32[]{:S(2)}) copy-start(f32[384]{0:T(512)} %param.16) | copy-start | bytes 4612
  53.3 18.3 %copy-start.4 = (f32[1536]{0:T(1024)S(1)}, f32[1536]{0:T(1024)}, u32[]{:S(2)}) copy-start(f32[1536]{0:T(1024)} %param.24) | copy-start | bytes 18436
  53.3 18.9 %copy-start.8 = (f32[384]{0:T(512)S(1)}, f32[384]{0:T(512)}, u32[]{:S(2)}) copy-start(f32[384]{0:T(512)} %param.20) | copy-start | bytes 4612
  53.3 19.5 %copy-start.9 = (f32[384]{0:T(512)S(1)}, f32[384]{0:T(512)}, u32[]{:S(2)}) copy-start(f32[384]{0:T(512)} %param.21) | copy-start | bytes 4612
  53.3 20.0 %copy-start.10 = (f32[384]{0:T(512)S(1)}, f32[384]{0:T(512)}, u32[]{:S(2)}) copy-start(f32[384]{0:T(512)} %param.22) | copy-start | bytes 4612
  53.3 20.6 %copy-start.11 = (f32[384]{0:T(512)S(1)}, f32[384]{0:T(512)}, u32[]{:S(2)}) copy-start(f32[384]{0:T(512)} %param.26) | copy-start | bytes 4612
  53.3 21.2 %copy-start.5 = (f32[768]{0:T(1024)S(1)}, f32[768]{0:T(1024)}, u32[]{:S(2)}) copy-start(f32[768]{0:T(1024)} %param.18) | copy-start | bytes 9220
  53.4 78.4 %collective-permute-start.4 = (bf16[16,108,384]{2,0,1:T(8,128)(2,1)}, bf16[16,108,384]{2,0,1:T(8,128)(2,1)S(1)}, u32[]{:S(2)}, u32[]{:S(2)}) collective-permute-start(bf16[16,108,384]{2,0,1:T(8,128)(2,1)} %copy.30), channel_id=1, source_target_pairs={{0,1},{1,0},{2,3},{3,2},{4,5},{5,4},{6,7},{7,6},{8,9},{9,8},{10,11... | collective-permute-start | bytes 3981320 | tf_op jit(solution)/shard_map/ppermute | solution.py:336
  53.5 16.7 %collective-permute-start.8 = (bf16[8,12,1152]{2,1,0:T(8,128)(2,1)S(1)}, bf16[8,12,1152]{2,1,0:T(8,128)(2,1)S(1)}, u32[]{:S(2)}, u32[]{:S(2)}) collective-permute-start(bf16[8,12,1152]{2,1,0:T(8,128)(2,1)S(1)} %pad_maximum_fusion.2), channel_id=1, source_target_pairs={{0,16},{1,17},{2,18},{3,19},{4,20},{5,21},{6,22},{7,23},{8,24},{9,... | collective-permute-start | bytes 663560 | tf_op jit(solution)/shard_map/ppermute | solution.py:336
  70.3 6.6 %copy-start.2 = (bf16[16,12,1152]{2,1,0:T(8,128)(2,1)}, bf16[16,12,1152]{2,1,0:T(8,128)(2,1)S(1)}, u32[]{:S(2)}) copy-start(bf16[16,12,1152]{2,1,0:T(8,128)(2,1)S(1)} %constant_dynamic-update-slice_fusion.4.refs_1_) | copy-start | bytes 1327108
  70.4 4.2 %collective-permute-start.9 = (bf16[16,12,1152]{2,0,1:T(8,128)(2,1)S(1)}, bf16[16,12,1152]{2,0,1:T(8,128)(2,1)S(1)}, u32[]{:S(2)}, u32[]{:S(2)}) collective-permute-start(bf16[16,12,1152]{2,0,1:T(8,128)(2,1)S(1)} %copy.31), channel_id=1, source_target_pairs={{0,1},{1,0},{2,3},{3,2},{4,5},{5,4},{6,7},{7,6},{8,9},{9,8},{10,11... | collective-permute-start | bytes 1327112 | tf_op jit(solution)/shard_map/ppermute | solution.py:336
  237.8 55.9 %copy-start.12 = (bf16[16,112,384]{2,1,0:T(8,128)(2,1)S(1)}, bf16[16,112,384]{2,1,0:T(8,128)(2,1)}, u32[]{:S(2)}) copy-start(bf16[16,112,384]{2,1,0:T(8,128)(2,1)} %get-tuple-element.37) | copy-start | bytes 4128772
  293.1 2.4 collective-permute-start.10
  293.7 13.8 %collective-permute-start.15 = (bf16[16,112,384]{2,1,0:T(8,128)(2,1)S(1)}, bf16[16,112,384]{2,1,0:T(8,128)(2,1)S(1)}, u32[]{:S(2)}, u32[]{:S(2)}) collective-permute-start(bf16[16,112,384]{2,1,0:T(8,128)(2,1)S(1)} %copy-done.12), channel_id=1, source_target_pairs={{0,1},{1,0},{2,3},{3,2},{4,5},{5,4},{6,7},{7,6},{8,9},{9,8},{10,11... | collective-permute-start | bytes 4128776 | tf_op jit(solution)/shard_map/ppermute | solution.py:336
  295.5 11.9 %copy-start.1 = (f32[16,112,384]{2,1,0:T(8,128)S(1)}, f32[16,112,384]{2,1,0:T(8,128)}, u32[]{:S(2)}) copy-start(f32[16,112,384]{2,1,0:T(8,128)} %get-tuple-element.36) | copy-start | bytes 8257540
  297.1 9.4 %collective-permute-start.11 = (bf16[8,48,384]{2,1,0:T(8,128)(2,1)S(1)}, bf16[8,48,384]{2,1,0:T(8,128)(2,1)S(1)}, u32[]{:S(2)}, u32[]{:S(2)}) collective-permute-start(bf16[8,48,384]{2,1,0:T(8,128)(2,1)S(1)} %slice.312), channel_id=1, source_target_pairs={{0,2},{1,3},{2,0},{3,1},{4,6},{5,7},{6,4},{7,5},{8,10},{9,11},{10,... | collective-permute-start | bytes 884744 | tf_op jit(solution)/shard_map/ppermute | solution.py:336
  306.6 5.3 %collective-permute-start.12 = (bf16[4,48,384]{2,1,0:T(8,128)(2,1)S(1)}, bf16[4,48,384]{2,1,0:T(8,128)(2,1)S(1)}, u32[]{:S(2)}, u32[]{:S(2)}) collective-permute-start(bf16[4,48,384]{2,1,0:T(8,128)(2,1)S(1)} %slice.314), channel_id=1, source_target_pairs={{0,4},{1,5},{2,6},{3,7},{4,0},{5,1},{6,2},{7,3},{8,12},{9,13},{10,... | collective-permute-start | bytes 442376 | tf_op jit(solution)/shard_map/ppermute | solution.py:336
  307.8 16.7 %collective-permute-start.16 = (bf16[8,112,384]{2,1,0:T(8,128)(2,1)S(1)}, bf16[8,112,384]{2,1,0:T(8,128)(2,1)S(1)}, u32[]{:S(2)}, u32[]{:S(2)}) collective-permute-start(bf16[8,112,384]{2,1,0:T(8,128)(2,1)S(1)} %slice.310), channel_id=1, source_target_pairs={{0,2},{1,3},{2,0},{3,1},{4,6},{5,7},{6,4},{7,5},{8,10},{9,11},{10,... | collective-permute-start | bytes 2064392 | tf_op jit(solution)/shard_map/ppermute | solution.py:336
  312.0 4.4 %collective-permute-start.13 = (bf16[2,48,384]{2,1,0:T(8,128)(2,1)S(1)}, bf16[2,48,384]{2,1,0:T(8,128)(2,1)S(1)}, u32[]{:S(2)}, u32[]{:S(2)}) collective-permute-start(bf16[2,48,384]{2,1,0:T(8,128)(2,1)S(1)} %slice.316), channel_id=1, source_target_pairs={{0,8},{1,9},{2,10},{3,11},{4,12},{5,13},{6,14},{7,15},{8,0},{9,1},... | collective-permute-start | bytes 221192 | tf_op jit(solution)/shard_map/ppermute | solution.py:336
  316.4 4.9 %collective-permute-start.14 = (bf16[1,48,384]{2,1,0:T(8,128)(2,1)S(1)}, bf16[1,48,384]{2,1,0:T(8,128)(2,1)S(1)}, u32[]{:S(2)}, u32[]{:S(2)}) collective-permute-start(bf16[1,48,384]{2,1,0:T(8,128)(2,1)S(1)} %slice.317), channel_id=1, source_target_pairs={{0,16},{1,17},{2,18},{3,19},{4,20},{5,21},{6,22},{7,23},{8,24},{9,... | collective-permute-start | bytes 110600 | tf_op jit(solution)/shard_map/ppermute | solution.py:336
  324.7 8.5 %collective-permute-start.17 = (bf16[4,112,384]{2,1,0:T(8,128)(2,1)S(1)}, bf16[4,112,384]{2,1,0:T(8,128)(2,1)S(1)}, u32[]{:S(2)}, u32[]{:S(2)}) collective-permute-start(bf16[4,112,384]{2,1,0:T(8,128)(2,1)S(1)} %slice.311), channel_id=1, source_target_pairs={{0,4},{1,5},{2,6},{3,7},{4,0},{5,1},{6,2},{7,3},{8,12},{9,13},{10,... | collective-permute-start | bytes 1032200 | tf_op jit(solution)/shard_map/ppermute | solution.py:336
  333.3 5.5 %collective-permute-start.18 = (bf16[2,112,384]{2,1,0:T(8,128)(2,1)S(1)}, bf16[2,112,384]{2,1,0:T(8,128)(2,1)S(1)}, u32[]{:S(2)}, u32[]{:S(2)}) collective-permute-start(bf16[2,112,384]{2,1,0:T(8,128)(2,1)S(1)} %slice.313), channel_id=1, source_target_pairs={{0,8},{1,9},{2,10},{3,11},{4,12},{5,13},{6,14},{7,15},{8,0},{9,1},... | collective-permute-start | bytes 516104 | tf_op jit(solution)/shard_map/ppermute | solution.py:336
  338.8 6.4 %collective-permute-start.19 = (bf16[1,112,384]{2,1,0:T(8,128)(2,1)S(1)}, bf16[1,112,384]{2,1,0:T(8,128)(2,1)S(1)}, u32[]{:S(2)}, u32[]{:S(2)}) collective-permute-start(bf16[1,112,384]{2,1,0:T(8,128)(2,1)S(1)} %slice.315), channel_id=1, source_target_pairs={{0,16},{1,17},{2,18},{3,19},{4,20},{5,21},{6,22},{7,23},{8,24},{9,... | collective-permute-start | bytes 258056 | tf_op jit(solution)/shard_map/ppermute | solution.py:336

commit v2 on v1

v2 whole, which is shorter than its diff:
```python
import jax
import jax.numpy as jnp
from jax import lax
from jax.experimental import pallas as pl
from jax.experimental.pallas import tpu as pltpu
from jax.sharding import PartitionSpec as P


D = 384
H = 6
FF = 1536
S = 197
SR = 208
SL = 256
CH = 256
NI = 2
FWD_CUT = 14
BWD_CUT = 6
SC = 0.125 * 1.4426950408889634
norm_eps = 1e-06
f32 = jnp.float32
bf16 = jnp.bfloat16
NN = (((1,), (0,)), ((), ()))
NT = (((1,), (1,)), ((), ()))
TN = (((0,), (0,)), ((), ()))


def dot(a, b, dims):
    return lax.dot_general(a, b, dims, preferred_element_type=f32)


def norm(x):
    c = x - jnp.mean(x, axis=-1, keepdims=True)
    r = lax.rsqrt(jnp.mean(c * c, axis=-1, keepdims=True) + norm_eps)
    return c * r, r


def stage_bits(n):
    top = n.bit_length() - 1
    return tuple(range(3, top)) + tuple(range(1, min(3, top)))


def place(k, n):
    return sum(((k >> b) & 1) << i for i, b in enumerate(stage_bits(n)))


def rest_rows(n):
    return -(-9 * (D // n) // 16) * 16


def for_parity(me, body):
    for parity in (0, 1):
        @pl.when((me & 1) == parity)
        def _():
            body(parity)


def attn_fwd(me_ref, *refs, n, lead):
    if lead:
        ga_ref, gb_ref, x_ref, g_ref, b_ref, bias_ref, pt_ref, wt_ref, ot_ref, wT_s, a_s, w_s = refs
    else:
        wT_s, x_ref, g_ref, b_ref, bias_ref, _, _, _, pt_ref, wt_ref, ot_ref, a_s = refs

    @pl.when(pl.program_id(0) == 0)
    def _():
        a_s[...] = jnp.zeros_like(a_s)
        if lead:
            me = me_ref[0]
            r1 = D // n

            def gather(parity):
                for k in range(n):
                    src = ga_ref if (k & 1) == parity else gb_ref
                    p = place(k, n)
                    w_s[r1 * k : r1 * (k + 1), :] = src[r1 * p : r1 * (p + 1), :]

            for_parity(me, gather)
            wT_s[...] = w_s[...].T

    valid = lax.broadcasted_iota(jnp.int32, (16, SL), 0) < S - 192

    def ln(i):
        n1, _ = norm(x_ref[i].astype(f32))
        a_s[i, :S, :] = (n1 * g_ref[...] + b_ref[...]).astype(bf16)

    def proj(i):
        pT = dot(wT_s[...], a_s[i], NT) + bias_ref[...]
        pt_ref[i] = pT.astype(bf16)

    def soft(i, h):
        qT = pt_ref[i, 64 * h : 64 * h + 64, :]
        kT = pt_ref[i, D + 64 * h : D + 64 * h + 64, :SR]
        z = dot(kT, qT, TN)
        zt = z[:192]
        zb = jnp.where(valid, z[192:], -jnp.inf)
        m = jnp.maximum(jnp.max(zt, axis=0, keepdims=True), jnp.max(zb, axis=0, keepdims=True))
        et = jnp.exp2((zt - m) * SC)
        eb = jnp.exp2((zb - m) * SC)
        l = jnp.sum(et, axis=0, keepdims=True) + jnp.sum(eb, axis=0, keepdims=True)
        inv = 1.0 / l
        wt_ref[i, h, :192, :] = (et * inv).astype(bf16)
        wt_ref[i, h, 192:, :] = (eb * inv).astype(bf16)

    def pv(i, h):
        vT = pt_ref[i, 2 * D + 64 * h : 2 * D + 64 * h + 64, :SR]
        ot_ref[i, 64 * h : 64 * h + 64, :] = dot(vT, wt_ref[i, h], NN).astype(bf16)

    for i in range(NI): ln(i)
    for i in range(NI): proj(i)
    for i in range(NI):
        for h in range(H):
            soft(i, h)
            if i > 0: pv(i - 1, h)
    for h in range(H): pv(NI - 1, h)


ERF_P = 0.3275911
ERF_A = (0.254829592, -0.284496736, 1.421413741, -1.453152027, 1.061405429)


def gelu_parts(u):
    e = jnp.exp2(u * u * (-0.5 * 1.4426950408889634))
    t = 1.0 / (1.0 + jnp.abs(u) * (ERF_P * 0.7071067811865476))
    poly = ERF_A[4] * 0.5
    for a in ERF_A[3::-1]:
        poly = poly * t + a * 0.5
    q = poly * t * e
    phi = jnp.where(u >= 0, 1.0 - q, q)
    return u * phi, phi + u * (e * 0.3989422804014327)


def spread(vec, width, shift, n):
    size = n * width
    d = lax.broadcasted_iota(jnp.int32, (n, size), 1)
    k = lax.broadcasted_iota(jnp.int32, (n, size), 0)
    picked = jnp.where(d // width == k, jnp.broadcast_to(vec, (n, size)), 0.0).astype(bf16)
    dd = lax.broadcasted_iota(jnp.int32, (size, 128), 0)
    j = lax.broadcasted_iota(jnp.int32, (size, 128), 1)
    place = jnp.where(dd % width + shift == j, 1.0, 0.0).astype(bf16)
    return dot(picked, place, NN)


def emit(me, stage, keep_ref, send_ref, n, bits):
    def one(k, carry):
        m = me ^ k
        pos = 0
        for b in bits:
            pos = pos * 2 + ((m >> b) & 1)

        @pl.when((m & 1) == 0)
        def _():
            keep_ref[pos] = stage[k]

        @pl.when((m & 1) == 1)
        def _():
            send_ref[pos] = stage[k].astype(bf16)

        return carry

    lax.fori_loop(0, n, one, 0)


def mlp(me_ref, ga_ref, gb_ref, x_ref, ot_ref, e_ref, pb_ref, g_ref, b_ref, ub_ref, db_ref,
        out_ref, dx1_ref, dot_ref, keep_ref, send_ref,
        xs, es, fs, pj_s, up_s, dn_s, gup, gdn, gpj, small, stage, upT, dnT, gs, us, bt, *, n, bits):
    me = me_ref[0]
    step = pl.program_id(0)
    r1, r4 = D // n, FF // n
    rw = rest_rows(n)

    @pl.when(step == 0)
    def _():
        xs[...] = jnp.zeros_like(xs)
        es[...] = jnp.zeros_like(es)
        fs[...] = jnp.zeros_like(fs)
        gup[...] = jnp.zeros_like(gup)
        gdn[...] = jnp.zeros_like(gdn)
        gpj[...] = jnp.zeros_like(gpj)
        small[...] = jnp.zeros_like(small)
        bt[:, D:, :] = jnp.ones((NI, 16, SR), bf16)

        def gather(parity):
            for k in range(n):
                src = ga_ref if (k & 1) == parity else gb_ref
                p = place(k, n)
                part = src[rw * p : rw * (p + 1), :]
                rows = slice(r1 * k, r1 * (k + 1))
                pj_s[rows, :] = part[:r1]
                for q in range(4):
                    up_s[rows, D * q : D * (q + 1)] = part[r1 * (1 + q) : r1 * (2 + q)]
                dn_s[r4 * k : r4 * (k + 1), :] = part[5 * r1 : 9 * r1]

        for_parity(me, gather)
        upT[...] = up_s[...].T
        dnT[...] = dn_s[...].T

    def fold(v):
        return jnp.sum(v.reshape(SR // 8, 8, v.shape[1]), axis=0)

    st = [dict() for _ in range(NI)]

    def p1(i):
        s = st[i]
        xs[i, :S, :] = x_ref[i]
        es[i, :S, :] = e_ref[i]
        s["oT"] = ot_ref[i, :, :SR]
        s["x1"] = xs[i].astype(f32) + dot(s["oT"], pj_s[...], TN) + pb_ref[...]
        s["n2"], s["r2"] = norm(s["x1"])
        bb = (s["n2"] * g_ref[...] + b_ref[...]).astype(bf16)
        s["bb"] = bb
        bt[i, :D, :] = bb.T
        s["eT"] = es[i].T

    def p2(i, c):
        cols = slice(c * CH, (c + 1) * CH)
        u = dot(st[i]["bb"], up_s[:, cols], NN) + ub_ref[:, cols]
        g, gp = gelu_parts(u)
        gs[i, :, cols] = g.astype(bf16)
        us[i, :, cols] = (dot(es[i], dnT[:, cols], NN) * gp).astype(bf16)

    def p3(i, c):
        cols = slice(c * CH, (c + 1) * CH)
        gdn[:, cols] += dot(st[i]["eT"], gs[i, :, cols], NN)
        gup[:, cols] += dot(bt[i], us[i, :, cols], NN)

    def p4(i):
        s = st[i]
        s["dB"] = dot(us[i], upT[...], NN)
        out_ref[i] = (s["x1"] + db_ref[...] + dot(gs[i], dn_s[...], NN))[:S]

    def p5(i):
        s = st[i]
        dB, n2 = s["dB"], s["n2"]
        dn = dB * g_ref[...]
        ef = es[i].astype(f32)
        dx1 = ef + s["r2"] * (dn - jnp.mean(dn, axis=-1, keepdims=True) - n2 * jnp.mean(dn * n2, axis=-1, keepdims=True))
        dx1_ref[i] = dx1[:S]
        ff = dx1.astype(bf16)
        fs[i, :SR, :] = ff
        small[0:8, 0:384] += fold(dB * n2)
        small[0:8, 384:768] += fold(dB)
        small[0:8, 768:1152] += fold(ff.astype(f32))
        small[0:8, 1152:1536] += fold(ef)

    def p6(i):
        gpj[...] += dot(st[i]["oT"], fs[i, :SR, :], NN)
        dot_ref[i] = dot(pj_s[...], fs[i], NT).astype(bf16)

    C = FF // CH
    p1(0)
    p1(1)
    for c in range(C): p2(0, c)
    for c in range(C):
        p2(1, c)
        p3(0, c)
    p4(0)
    p4(1)
    p5(0)
    for c in range(C // 2): p3(1, c)
    p6(0)
    p5(1)
    for c in range(C // 2, C): p3(1, c)
    p6(1)

    @pl.when(step == pl.num_programs(0) - 1)
    def _():
        tot = jnp.sum(small[...], axis=0, keepdims=True)
        sm = spread(gup[D : D + 1, :], r4, 4 * r1, n)
        for q in range(4):
            sm = sm + spread(tot[:, D * q : D * (q + 1)], r1, r1 * q, n)
        for k in range(n):
            rows = slice(r1 * k, r1 * (k + 1))
            stage[k, :r1, :] = gpj[rows, :]
            for q in range(4):
                stage[k, r1 * (1 + q) : r1 * (2 + q), :] = gup[rows, D * q : D * (q + 1)]
            stage[k, 9 * r1 : 9 * r1 + 1, :128] = sm[k : k + 1]
        for c in range(FF // 384):
            gT = gdn[:, 384 * c : 384 * (c + 1)].T
            for k in range(384 // r4):
                stage[c * (384 // r4) + k, 5 * r1 : 9 * r1, :] = gT[r4 * k : r4 * (k + 1)]
        emit(me, stage, keep_ref, send_ref, n, bits)


def attn_bwd(me_ref, x_ref, pt_ref, wt_ref, dot_ref, dx1_ref, g_ref, b_ref, wT_s, *refs, n, bits, lead, last):
    if not lead:
        gqi_ref, smi_ref, _ = refs[:3]
        refs = refs[3:]
    if last:
        din_ref, keep_ref, send_ref, as_, dp_s, dz_s, gq, small, stage = refs
    else:
        din_ref, gq, small, as_, dp_s, dz_s = refs
    step = pl.program_id(0)

    @pl.when(step == 0)
    def _():
        as_[:, :, :D] = jnp.zeros((NI, SR, D), bf16)
        as_[:, :, D:] = jnp.ones((NI, SR, 128), bf16)
        gq[...] = jnp.zeros_like(gq) if lead else gqi_ref[...]
        small[...] = jnp.zeros_like(small) if lead else smi_ref[...]

    hs = [slice(64 * h, 64 * h + 64) for h in range(H)]
    ks = [slice(D + 64 * h, D + 64 * h + 64) for h in range(H)]
    vs = [slice(2 * D + 64 * h, 2 * D + 64 * h + 64) for h in range(H)]
    st = [dict() for _ in range(NI)]

    def ln(i):
        n1, r1 = norm(x_ref[i].astype(f32))
        st[i].update(n1=n1, r1=r1)
        as_[i, :S, :D] = (n1 * g_ref[...] + b_ref[...]).astype(bf16)

    def dz(i, h):
        w = wt_ref[i, h].astype(f32)
        t = dot(pt_ref[i, vs[h], :SR], dot_ref[i, hs[h], :], TN) * w
        dz_s[i, h] = (t - w * jnp.sum(t, axis=0, keepdims=True)).astype(bf16)

    def dv(i, h):
        dp_s[i, vs[h], :] = dot(dot_ref[i, hs[h], :], wt_ref[i, h], NT).astype(bf16)

    def dq(i, h):
        dp_s[i, hs[h], :] = (dot(pt_ref[i, ks[h], :SR], dz_s[i, h], NN) * 0.125)[:, :SR].astype(bf16)

    def dk(i, h):
        dp_s[i, ks[h], :] = (dot(pt_ref[i, hs[h], :], dz_s[i, h], NT) * 0.125).astype(bf16)

    def gr(i):
        st[i]["dA"] = dot(dp_s[i], wT_s[...], TN)[:S]
        gq[...] += dot(dp_s[i], as_[i], NN)

    def fin(i):
        n1, r1, dA = st[i]["n1"], st[i]["r1"], st[i]["dA"]
        dm = dA * g_ref[...]
        din_ref[i] = dx1_ref[i] + r1 * (
            dm - jnp.mean(dm, axis=-1, keepdims=True) - n1 * jnp.mean(dm * n1, axis=-1, keepdims=True))
        small[0:1, 0:384] += jnp.sum(dA * n1, axis=0, keepdims=True)
        small[0:1, 384:768] += jnp.sum(dA, axis=0, keepdims=True)

    for i in range(NI): ln(i)
    for h in range(H): dz(0, h)
    for h in range(H):
        dz(1, h)
        dv(0, h)
        dq(0, h)
        dk(0, h)
    for h in range(H):
        dv(1, h)
        dq(1, h)
        dk(1, h)
    gr(0)
    gr(1)
    fin(0)
    fin(1)

    if last:
        @pl.when(step == pl.num_programs(0) - 1)
        def _():
            me = me_ref[0]
            r1 = D // n
            cs = gq[:, D : D + 128].T[0:1, :]
            sm = spread(small[0:1, :D], r1, 0, n) + spread(small[0:1, D : 2 * D], r1, r1, n)
            sm = sm + spread(jnp.concatenate([cs[:, :D], cs[:, 2 * D :]], axis=1), 2 * r1, 2 * r1, n)
            for q in range(3):
                gT = gq[D * q : D * (q + 1), :D].T
                for k in range(n):
                    stage[k, r1 * q : r1 * (q + 1), :] = gT[r1 * k : r1 * (k + 1)]
            for k in range(n):
                stage[k, 3 * r1 : 3 * r1 + 1, :128] = sm[k : k + 1]
            emit(me, stage, keep_ref, send_ref, n, bits)


def img(shape, at=0):
    return pl.BlockSpec((NI,) + shape, lambda i: (i + at // NI,) + (0,) * len(shape))


def res(shape):
    return pl.BlockSpec(shape, lambda i: (0,) * len(shape))


smem = pl.BlockSpec(memory_space=pltpu.SMEM)
hbm = pl.BlockSpec(memory_space=pl.ANY)
params = pltpu.CompilerParams(dimension_semantics=("arbitrary",), vmem_limit_bytes=60 * 2**20)


def shape_of(*dims, dtype=f32):
    return jax.ShapeDtypeStruct(dims, dtype)


def vmem(*dims, dtype=bf16):
    return pltpu.VMEM(dims, dtype)


def run_fwd(n, me, weights, x, g1, b1, bias, at, count, kept=()):
    m = x.shape[0]
    lead = not kept
    out_specs = [img((3 * D, SL), at), img((H, SR, SL), at), img((D, SL), at)]
    out_shape = [shape_of(m, 3 * D, SL, dtype=bf16), shape_of(m, H, SR, SL, dtype=bf16), shape_of(m, D, SL, dtype=bf16)]
    scratch = [vmem(NI, SL, D)]
    if lead:
        out_specs, out_shape = out_specs + [res((3 * D, D))], out_shape + [shape_of(3 * D, D, dtype=bf16)]
        scratch = scratch + [vmem(D, 3 * D)]
    base = 1 + len(weights) + 4
    return pl.pallas_call(
        lambda *refs: attn_fwd(*refs, n=n, lead=lead), grid=(count // NI,), name="attn_fwd",
        in_specs=[smem] + [res(w.shape) for w in weights] + [img((S, D), at), res((1, D)), res((1, D)), res((3 * D, SL))]
        + [hbm] * len(kept),
        out_specs=out_specs, out_shape=out_shape, scratch_shapes=scratch,
        input_output_aliases={base + i: i for i in range(len(kept))},
        compiler_params=params,
    )(me, *weights, x, g1, b1, bias, *kept)


def chunk_rows(n, parts):
    return -(-(parts * (D // n) + 1) // 16) * 16


def run_mlp(n, bits, me, ga, gb, x, oT, e, pb, g2, b2, ub, db):
    m = x.shape[0]
    cr = chunk_rows(n, 9)
    return pl.pallas_call(
        lambda *refs: mlp(*refs, n=n, bits=bits), grid=(m // NI,), name="mlp",
        in_specs=[smem, res(ga.shape), res(gb.shape), img((S, D)), img((D, SL)), img((S, D)),
                  res((1, D)), res((1, D)), res((1, D)), res((1, FF)), res((1, D))],
        out_specs=[img((S, D)), img((S, D)), img((D, SL)), res((n // 2, cr, D)), res((n // 2, cr, D))],
        out_shape=[shape_of(m, S, D), shape_of(m, S, D), shape_of(m, D, SL, dtype=bf16),
                   shape_of(n // 2, cr, D), shape_of(n // 2, cr, D, dtype=bf16)],
        scratch_shapes=[vmem(NI, SR, D), vmem(NI, SR, D), vmem(NI, SL, D), vmem(D, D), vmem(D, FF), vmem(FF, D),
                        vmem(D + 16, FF, dtype=f32), vmem(D, FF, dtype=f32), vmem(D, D, dtype=f32),
                        vmem(8, FF, dtype=f32), vmem(n, cr, D, dtype=f32), vmem(FF, D), vmem(D, FF),
                        vmem(NI, SR, FF), vmem(NI, SR, FF), vmem(NI, D + 16, SR)],
        compiler_params=params,
    )(me, ga, gb, x, oT, e, pb, g2, b2, ub, db)


def run_bwd(n, bits, me, x, pt, wt, doT, dx1, g1, b1, wT, at, count, kept=()):
    m = x.shape[0]
    cr = chunk_rows(n, 3)
    lead, last = not kept, at + count == m
    out_specs, out_shape = [img((S, D), at)], [shape_of(m, S, D)]
    scratch = [vmem(NI, SR, 512), vmem(NI, 3 * D, SR), vmem(NI, H, SR, SL)]
    sums = [((3 * D, 512), f32), ((8, 2 * D), f32)]
    if last:
        out_specs = out_specs + [res((n // 2, cr, D))] * 2
        out_shape = out_shape + [shape_of(n // 2, cr, D), shape_of(n // 2, cr, D, dtype=bf16)]
        scratch = scratch + [vmem(*s, dtype=t) for s, t in sums] + [vmem(n, cr, D, dtype=f32)]
    else:
        out_specs = out_specs + [res(s) for s, _ in sums]
        out_shape = out_shape + [shape_of(*s, dtype=t) for s, t in sums]
    return pl.pallas_call(
        lambda *refs: attn_bwd(*refs, n=n, bits=bits, lead=lead, last=last), grid=(count // NI,), name="attn_bwd",
        in_specs=[smem, img((S, D), at), img((3 * D, SL), at), img((H, SR, SL), at), img((D, SL), at), img((S, D), at),
                  res((1, D)), res((1, D)), res((3 * D, D))]
        + ([] if lead else [res(s) for s, _ in sums] + [hbm]),
        out_specs=out_specs, out_shape=out_shape, scratch_shapes=scratch,
        input_output_aliases={} if lead else {11: 0},
        compiler_params=params,
    )(me, x, pt, wt, doT, dx1, g1, b1, wT, *kept)


def swap(v, bit, n):
    return lax.ppermute(v, "dp", [(i, i ^ (1 << bit)) for i in range(n)])


def gather_halves(v, me, n):
    bits = stage_bits(n)
    for b in bits:
        other = swap(v, b, n)
        high = (me >> b) & 1 == 1
        v = jnp.where(high, jnp.concatenate([other, v], axis=0), jnp.concatenate([v, other], axis=0))
    return v, swap(v, 0, n)


def reduce_parts(keep, send, n, bits):
    got = swap(send, 0, n)
    total = keep + got.astype(f32)
    for b in bits:
        half = total.shape[0] // 2
        part = total[half:].astype(bf16)
        got = swap(part, b, n)
        total = total[:half] + got.astype(f32)
    return total[0]


def on_device(n, block_input, first_gain, first_shift, qkv_weight, query_value_bias, proj_weight, proj_bias,
              second_gain, second_shift, up_weight, up_bias, down_weight, down_bias, output_cotangent):
    n_bits = n.bit_length() - 1
    bits = tuple(range(1, n_bits))
    r1, r4 = D // n, FF // n
    at = lax.axis_index("dp").astype(jnp.int32)
    me = at.reshape(1)

    def row(v):
        return v.reshape(1, -1)

    bias = jnp.concatenate([query_value_bias[:D], jnp.zeros((D,), f32), query_value_bias[D:]])
    bias = jnp.broadcast_to(bias[:, None], (3 * D, SL))
    qa, qb = gather_halves(qkv_weight, at, n)
    rest = jnp.concatenate(
        [proj_weight] + [up_weight[:, D * q : D * (q + 1)] for q in range(4)] + [down_weight]
        + [jnp.zeros((rest_rows(n) - 9 * r1, D), bf16)], axis=0)
    wa, wb = gather_halves(rest, at, n)
    m = block_input.shape[0]
    norm1 = (row(first_gain), row(first_shift))
    cut = FWD_CUT
    *acts, wT = run_fwd(n, me, (qa, qb), block_input, *norm1, bias, 0, cut)
    pt, wt, oT = run_fwd(n, me, (wT,), block_input, *norm1, bias, cut, m - cut, acts)
    out, dx1, doT, keep, send = run_mlp(
        n, bits, me, wa, wb, block_input, oT, output_cotangent, row(proj_bias), row(second_gain),
        row(second_shift), row(up_bias), row(down_bias))
    mp = reduce_parts(keep, send, n, bits)
    cut = BWD_CUT
    dins, gq, sm = run_bwd(n, bits, me, block_input, pt, wt, doT, dx1, *norm1, wT, 0, cut)
    din, keep, send = run_bwd(n, bits, me, block_input, pt, wt, doT, dx1, *norm1, wT, cut, m - cut, (gq, sm, dins))
    ap = reduce_parts(keep, send, n, bits)
    g_up = jnp.concatenate([mp[r1 * (1 + q) : r1 * (2 + q)] for q in range(4)], axis=1)
    g_qkv = jnp.concatenate([ap[r1 * q : r1 * (q + 1)] for q in range(3)], axis=1)
    sm, sa = mp[9 * r1], ap[3 * r1]
    return (out, din, sa[:r1], sa[r1 : 2 * r1], g_qkv, sa[2 * r1 : 4 * r1], mp[:r1], sm[2 * r1 : 3 * r1],
            sm[:r1], sm[r1 : 2 * r1], g_up, sm[4 * r1 : 4 * r1 + r4], mp[5 * r1 : 9 * r1], sm[3 * r1 : 4 * r1])


def solution(mesh):
    rows, vec, imgs = P("dp", None), P("dp"), P("dp", None, None)
    n = mesh.shape["dp"]

    def body(*args):
        return on_device(n, *args)

    return jax.shard_map(
        body, mesh=mesh,
        in_specs=(imgs, P(), P(), rows, P(), rows, P(), P(), P(), rows, P(), rows, P(), imgs),
        out_specs=(imgs, imgs, vec, vec, rows, vec, rows, vec, vec, vec, rows, vec, rows, vec),
        check_vma=False)
```

time: 349 us -> 256 us (0.73)
  Pallas kernels: 215 us -> 132 us
  waiting for transfers between devices: 90.9 us -> 70.7 us
  starting transfers between devices: 20.6 us -> 30.6 us
    pallas_call x3 -> x5, Pallas kernels: 215 us -> 132 us  [the longest x1 65.9 us: run_mlp(): pl.pallas_call(lambda *refs: mlp(*refs, n=n, bits=bits), grid=(m // NI,),...]
    ppermute x20, waiting for transfers between devices: 90.9 us -> 70.7 us  [swap(): return lax.ppermute(v, 'dp', [(i, i ^ 1 << bit) for i in range(n)])]
    ppermute x20, starting transfers between devices: 20.6 us -> 30.6 us  [swap(): return lax.ppermute(v, 'dp', [(i, i ^ 1 << bit) for i in range(n)])]
  transfers between devices with their start and end apart: 20 -> 20, of which waited for: 14 -> 16; matrix products, arithmetic and copies ran while one was open for 4% -> 4% of each run, Pallas kernels for 16% -> 11%
where the time goes in v2:
time: 256 us; the launch traced here: 255 us
  Pallas kernels  132 us (52%)
  waiting for transfers between devices  70.7 us (28%)
  starting transfers between devices  30.6 us (12%)
  local copies, waits for them, and re-layouts  16.7 us (7%)
  other arithmetic  4.36 us (2%)
    ppermute x20, waiting for transfers between devices, swap(): return lax.ppermute(v, 'dp', [(i, i ^ 1 << bit) for i in range(n)])  70.7 us
    pallas_call x1, Pallas kernels, run_mlp(): pl.pallas_call(lambda *refs: mlp(*refs, n=n, bits=bits), grid=(m // NI,),...  65.9 us
    pallas_call x2, Pallas kernels, run_bwd(): pl.pallas_call(lambda *refs: attn_bwd(*refs, n=n, bits=bits, lead=lead, l...  39 us
    ppermute x20, starting transfers between devices, swap(): return lax.ppermute(v, 'dp', [(i, i ^ 1 << bit) for i in range(n)])  30.6 us
    pallas_call x2, Pallas kernels, run_fwd(): pl.pallas_call(lambda *refs: attn_fwd(*refs, n=n, lead=lead), grid=(count...  26.9 us
  transfers between devices with their start and end apart: 20, of which 16 were waited for; matrix products, arithmetic and copies ran while one was open for 4% of the time, Pallas kernels for 11%

profile of v2, /device:TPU:0, one launch (start us, length us, event | category | flops | bytes accessed | tf_op | source)
XLA Modules:
  0.0 255.1 jit_solution(14915509256685360997)
XLA Ops:
  0.6 0.8 fusion
  1.4 1.9 concatenate.62
  3.3 3.1 %collective-permute-start = (bf16[112,384]{1,0:T(8,128)(2,1)S(1)}, bf16[112,384]{1,0:T(8,128)(2,1)S(1)}, u32[]{:S(2)}, u32[]{:S(2)}) collective-permute-start(bf16[112,384]{1,0:T(8,128)(2,1)S(1)} %concatenate.62), channel_id=1, source_target_pairs={{0,8},{1,9},{2,10},{3,11},{4,12},{5,13},{6,14},{7,15},{8,0},{9,1},... | collective-permute-start | bytes 258056 | tf_op jit(solution)/shard_map/ppermute | solution.py:459
  6.4 2.5 collective-permute-done
  8.9 1.9 concatenate.64
  10.8 1.9 concatenate.63
  12.7 3.0 %collective-permute-start.1 = (bf16[224,384]{1,0:T(8,128)(2,1)S(1)}, bf16[224,384]{1,0:T(8,128)(2,1)S(1)}, u32[]{:S(2)}, u32[]{:S(2)}) collective-permute-start(bf16[224,384]{1,0:T(8,128)(2,1)S(1)} %broadcast_select_fusion), channel_id=1, source_target_pairs={{0,16},{1,17},{2,18},{3,19},{4,20},{5,21},{6,22},{7,23},{8,24},{9,... | collective-permute-start | bytes 516104 | tf_op jit(solution)/shard_map/ppermute | solution.py:459
  15.8 7.2 %collective-permute-done.1 = bf16[224,384]{1,0:T(8,128)(2,1)S(1)} collective-permute-done((bf16[224,384]{1,0:T(8,128)(2,1)S(1)}, bf16[224,384]{1,0:T(8,128)(2,1)S(1)}, u32[]{:S(2)}, u32[]{:S(2)}) %collective-permute-start.1) | collective-permute-done | bytes 172064 | tf_op jit(solution)/shard_map/ppermute | solution.py:459
  23.0 1.4 collective-permute-start.2
  24.4 7.9 %collective-permute-done.2 = bf16[448,384]{1,0:T(8,128)(2,1)S(1)} collective-permute-done((bf16[448,384]{1,0:T(8,128)(2,1)S(1)}, bf16[448,384]{1,0:T(8,128)(2,1)S(1)}, u32[]{:S(2)}, u32[]{:S(2)}) %collective-permute-start.2) | collective-permute-done | bytes 344096 | tf_op jit(solution)/shard_map/ppermute | solution.py:459
  32.5 1.2 collective-permute-start.3
  33.7 1.3 collective-permute-start.5
  35.1 2.6 %collective-permute-done.5 = bf16[12,1152]{1,0:T(8,128)(2,1)S(1)} collective-permute-done((bf16[12,1152]{1,0:T(8,128)(2,1)S(1)}, bf16[12,1152]{1,0:T(8,128)(2,1)S(1)}, u32[]{:S(2)}, u32[]{:S(2)}) %collective-permute-start.5) | collective-permute-done | bytes 27680 | tf_op jit(solution)/shard_map/ppermute | solution.py:459
  37.7 2.8 %collective-permute-start.6 = (bf16[24,1152]{1,0:T(8,128)(2,1)S(1)}, bf16[24,1152]{1,0:T(8,128)(2,1)S(1)}, u32[]{:S(2)}, u32[]{:S(2)}) collective-permute-start(bf16[24,1152]{1,0:T(8,128)(2,1)S(1)} %maximum_select_fusion.6), channel_id=1, source_target_pairs={{0,16},{1,17},{2,18},{3,19},{4,20},{5,21},{6,22},{7,23},{8,24},{9,... | collective-permute-start | bytes 165896 | tf_op jit(solution)/shard_map/ppermute | solution.py:459
  40.5 7.8 %collective-permute-done.3 = bf16[896,384]{1,0:T(8,128)(2,1)S(1)} collective-permute-done((bf16[896,384]{1,0:T(8,128)(2,1)S(1)}, bf16[896,384]{1,0:T(8,128)(2,1)S(1)}, u32[]{:S(2)}, u32[]{:S(2)}) %collective-permute-start.3) | collective-permute-done | bytes 688160 | tf_op jit(solution)/shard_map/ppermute | solution.py:459
  48.8 1.0 collective-permute-start.7
  49.8 4.5 %collective-permute-done.7 = bf16[48,1152]{1,0:T(8,128)(2,1)S(1)} collective-permute-done((bf16[48,1152]{1,0:T(8,128)(2,1)S(1)}, bf16[48,1152]{1,0:T(8,128)(2,1)S(1)}, u32[]{:S(2)}, u32[]{:S(2)}) %collective-permute-start.7) | collective-permute-done | bytes 110624 | tf_op jit(solution)/shard_map/ppermute | solution.py:459
  54.4 1.0 collective-permute-start.8
  55.4 6.0 %collective-permute-done.8 = bf16[96,1152]{1,0:T(8,128)(2,1)S(1)} collective-permute-done((bf16[96,1152]{1,0:T(8,128)(2,1)S(1)}, bf16[96,1152]{1,0:T(8,128)(2,1)S(1)}, u32[]{:S(2)}, u32[]{:S(2)}) %collective-permute-start.8) | collective-permute-done | bytes 221216 | tf_op jit(solution)/shard_map/ppermute | solution.py:459
  65.7 1.2 broadcast_in_dim.14.refs_6_.refs_5_
  66.9 17.7 %attn_fwd.2 = (bf16[20,1152,256]{2,1,0:T(8,128)(2,1)}, bf16[20,6,208,256]{3,2,1,0:T(8,128)(2,1)}, bf16[20,384,256]{2,1,0:T(8,128)(2,1)}, bf16[1152,384]{1,0:T(8,128)(2,1)}) custom-call(s32[1]{0:T(128)} %bitcast.refs_0_, bf16[192,1152]{1,0:T(8,128)(2,1)} %copy-done.2, bf16[192,1152]{1,0:T(8,128)(2,1)} %copy-done.4, bf16[20,197,384]{2,1,0:T(8,128)(2,1)} %refs_1_.3, ...), custom_call_target="tpu_custom_call" | custom-call | tf_op jit(solution)/shard_map/attn_fwd/pallas_call | solution.py:401
  84.7 9.2 %attn_fwd.3 = (bf16[20,1152,256]{2,1,0:T(8,128)(2,1)}, bf16[20,6,208,256]{3,2,1,0:T(8,128)(2,1)}, bf16[20,384,256]{2,1,0:T(8,128)(2,1)}) custom-call(s32[1]{0:T(128)} %bitcast.refs_0_, bf16[1152,384]{1,0:T(8,128)(2,1)} %get-tuple-element.32.refs_1_.refs_8_, ...), custom_call_target="tpu_custom_call", output_to_operand_aliasing={{0}: (6, {}), {1}: (7, {}), {2}: (8, {})} | custom-call | tf_op jit(solution)/shard_map/attn_fwd/pallas_call | solution.py:401
  93.9 1.1 copy-done.3
  95.0 65.9 %mlp.1 = (f32[20,197,384]{2,1,0:T(8,128)}, f32[20,197,384]{2,1,0:T(8,128)}, bf16[20,384,256]{2,1,0:T(8,128)(2,1)}, f32[16,112,384]{2,1,0:T(8,128)}, bf16[16,112,384]{2,1,0:T(8,128)(2,1)}) custom-call(s32[1]{0:T(128)} %bitcast.refs_0_, bf16[1792,384]{1,0:T(8,128)(2,1)} %copy-done, bf16[1792,384]{1,0:T(8,128)(2,1)} %copy-done.3, ...), custom_call_target="tpu_custom_call" | custom-call | tf_op jit(solution)/shard_map/mlp/pallas_call | solution.py:418
  160.9 12.7 %attn_bwd.2 = (f32[20,197,384]{2,1,0:T(8,128)}, f32[1152,512]{1,0:T(8,128)}, f32[8,768]{1,0:T(8,128)}) custom-call(s32[1]{0:T(128)} %bitcast.refs_0_, bf16[20,197,384]{2,1,0:T(8,128)(2,1)} %refs_1_.3, bf16[20,1152,256]{2,1,0:T(8,128)(2,1)} %get-tuple-element.38.refs_2_, bf16[20,6,208,256]{3,2,1,0:T(8,128)(2,1)} %get-tuple-element.39.refs_3_, ...), custom_call_target="tpu_custom_call" | custom-call | tf_op jit(solution)/shard_map/attn_bwd/pallas_call | solution.py:447
  173.6 26.3 %attn_bwd.3 = (f32[20,197,384]{2,1,0:T(8,128)}, f32[16,48,384]{2,1,0:T(8,128)}, bf16[16,48,384]{2,1,0:T(8,128)(2,1)}) custom-call(s32[1]{0:T(128)} %bitcast.refs_0_, bf16[20,197,384]{2,1,0:T(8,128)(2,1)} %refs_1_.3, bf16[20,1152,256]{2,1,0:T(8,128)(2,1)} %get-tuple-element.38.refs_2_, ...), custom_call_target="tpu_custom_call", output_to_operand_aliasing={{0}: (11, {})} | custom-call | tf_op jit(solution)/shard_map/attn_bwd/pallas_call | solution.py:447
  200.5 1.8 collective-permute-done.10
  202.3 1.6 convert_add_fusion.1
  203.9 1.0 collective-permute-start.11
  204.8 8.4 %collective-permute-done.11 = bf16[8,48,384]{2,1,0:T(8,128)(2,1)S(1)} collective-permute-done((bf16[8,48,384]{2,1,0:T(8,128)(2,1)S(1)}, bf16[8,48,384]{2,1,0:T(8,128)(2,1)S(1)}, u32[]{:S(2)}, u32[]{:S(2)}) %collective-permute-start.11) | collective-permute-done | bytes 294944 | tf_op jit(solution)/shard_map/ppermute | solution.py:459
  213.3 1.0 collective-permute-start.12
  214.6 1.6 collective-permute-start.16
  216.2 2.5 collective-permute-done.12
  218.7 1.5 collective-permute-start.13
  220.2 2.9 %collective-permute-done.13 = bf16[2,48,384]{2,1,0:T(8,128)(2,1)S(1)} collective-permute-done((bf16[2,48,384]{2,1,0:T(8,128)(2,1)S(1)}, bf16[2,48,384]{2,1,0:T(8,128)(2,1)S(1)}, u32[]{:S(2)}, u32[]{:S(2)}) %collective-permute-start.13) | collective-permute-done | bytes 73760 | tf_op jit(solution)/shard_map/ppermute | solution.py:459
  223.1 2.8 %collective-permute-start.14 = (bf16[1,48,384]{2,1,0:T(8,128)(2,1)S(1)}, bf16[1,48,384]{2,1,0:T(8,128)(2,1)S(1)}, u32[]{:S(2)}, u32[]{:S(2)}) collective-permute-start(bf16[1,48,384]{2,1,0:T(8,128)(2,1)S(1)} %slice.317), channel_id=1, source_target_pairs={{0,16},{1,17},{2,18},{3,19},{4,20},{5,21},{6,22},{7,23},{8,24},{9,... | collective-permute-start | bytes 110600 | tf_op jit(solution)/shard_map/ppermute | solution.py:459
  226.0 2.1 collective-permute-done.14
  228.1 3.2 %collective-permute-done.16 = bf16[8,112,384]{2,1,0:T(8,128)(2,1)S(1)} collective-permute-done((bf16[8,112,384]{2,1,0:T(8,128)(2,1)S(1)}, bf16[8,112,384]{2,1,0:T(8,128)(2,1)S(1)}, u32[]{:S(2)}, u32[]{:S(2)}) %collective-permute-start.16) | collective-permute-done | bytes 688160 | tf_op jit(solution)/shard_map/ppermute | solution.py:459
  231.4 1.2 collective-permute-start.17
  232.6 0.6 pad_maximum_fusion.1
  233.3 6.6 %collective-permute-done.17 = bf16[4,112,384]{2,1,0:T(8,128)(2,1)S(1)} collective-permute-done((bf16[4,112,384]{2,1,0:T(8,128)(2,1)S(1)}, bf16[4,112,384]{2,1,0:T(8,128)(2,1)S(1)}, u32[]{:S(2)}, u32[]{:S(2)}) %collective-permute-start.17) | collective-permute-done | bytes 344096 | tf_op jit(solution)/shard_map/ppermute | solution.py:459
  240.0 2.1 collective-permute-start.18
  242.6 2.8 %collective-permute-done.18 = bf16[2,112,384]{2,1,0:T(8,128)(2,1)S(1)} collective-permute-done((bf16[2,112,384]{2,1,0:T(8,128)(2,1)S(1)}, bf16[2,112,384]{2,1,0:T(8,128)(2,1)S(1)}, u32[]{:S(2)}, u32[]{:S(2)}) %collective-permute-start.18) | collective-permute-done | bytes 172064 | tf_op jit(solution)/shard_map/ppermute | solution.py:459
  245.5 4.1 %collective-permute-start.19 = (bf16[1,112,384]{2,1,0:T(8,128)(2,1)S(1)}, bf16[1,112,384]{2,1,0:T(8,128)(2,1)S(1)}, u32[]{:S(2)}, u32[]{:S(2)}) collective-permute-start(bf16[1,112,384]{2,1,0:T(8,128)(2,1)S(1)} %slice.315), channel_id=1, source_target_pairs={{0,16},{1,17},{2,18},{3,19},{4,20},{5,21},{6,22},{7,23},{8,24},{9,... | collective-permute-start | bytes 258056 | tf_op jit(solution)/shard_map/ppermute | solution.py:459
  250.1 1.9 collective-permute-done.19
  252.1 0.6 slice_bitcast_fusion.4
  252.7 0.6 slice_bitcast_fusion
  254.5 0.6 pad_maximum_fusion
  (78 shorter events, 9.0 us)
Async XLA Ops:
  3.3 5.6 %collective-permute-start = (bf16[112,384]{1,0:T(8,128)(2,1)S(1)}, bf16[112,384]{1,0:T(8,128)(2,1)S(1)}, u32[]{:S(2)}, u32[]{:S(2)}) collective-permute-start(bf16[112,384]{1,0:T(8,128)(2,1)S(1)} %concatenate.62), channel_id=1, source_target_pairs={{0,8},{1,9},{2,10},{3,11},{4,12},{5,13},{6,14},{7,15},{8,0},{9,1},... | collective-permute-start | bytes 258056 | tf_op jit(solution)/shard_map/ppermute | solution.py:459
  12.7 21.0 %copy-start.5 = (bf16[12,1152]{1,0:T(8,128)(2,1)S(1)}, bf16[12,1152]{1,0:T(8,128)(2,1)}, u32[]{:S(2)}) copy-start(bf16[12,1152]{1,0:T(8,128)(2,1)} %param.17) | copy-start | bytes 82948
  12.7 10.2 %collective-permute-start.1 = (bf16[224,384]{1,0:T(8,128)(2,1)S(1)}, bf16[224,384]{1,0:T(8,128)(2,1)S(1)}, u32[]{:S(2)}, u32[]{:S(2)}) collective-permute-start(bf16[224,384]{1,0:T(8,128)(2,1)S(1)} %broadcast_select_fusion), channel_id=1, source_target_pairs={{0,16},{1,17},{2,18},{3,19},{4,20},{5,21},{6,22},{7,23},{8,24},{9,... | collective-permute-start | bytes 516104 | tf_op jit(solution)/shard_map/ppermute | solution.py:459
  23.0 9.2 %collective-permute-start.2 = (bf16[448,384]{1,0:T(8,128)(2,1)S(1)}, bf16[448,384]{1,0:T(8,128)(2,1)S(1)}, u32[]{:S(2)}, u32[]{:S(2)}) collective-permute-start(bf16[448,384]{1,0:T(8,128)(2,1)S(1)} %maximum_select_fusion.3), channel_id=1, source_target_pairs={{0,2},{1,3},{2,0},{3,1},{4,6},{5,7},{6,4},{7,5},{8,10},{9,11},{10,... | collective-permute-start | bytes 1032200 | tf_op jit(solution)/shard_map/ppermute | solution.py:459
  32.5 15.7 %collective-permute-start.3 = (bf16[896,384]{1,0:T(8,128)(2,1)S(1)}, bf16[896,384]{1,0:T(8,128)(2,1)S(1)}, u32[]{:S(2)}, u32[]{:S(2)}) collective-permute-start(bf16[896,384]{1,0:T(8,128)(2,1)S(1)} %maximum_select_fusion.1), channel_id=1, source_target_pairs={{0,4},{1,5},{2,6},{3,7},{4,0},{5,1},{6,2},{7,3},{8,12},{9,13},{10,... | collective-permute-start | bytes 2064392 | tf_op jit(solution)/shard_map/ppermute | solution.py:459
  33.7 4.0 %collective-permute-start.5 = (bf16[12,1152]{1,0:T(8,128)(2,1)S(1)}, bf16[12,1152]{1,0:T(8,128)(2,1)S(1)}, u32[]{:S(2)}, u32[]{:S(2)}) collective-permute-start(bf16[12,1152]{1,0:T(8,128)(2,1)S(1)} %copy-done.5), channel_id=1, source_target_pairs={{0,8},{1,9},{2,10},{3,11},{4,12},{5,13},{6,14},{7,15},{8,0},{9,1},... | collective-permute-start | bytes 82952 | tf_op jit(solution)/shard_map/ppermute | solution.py:459
  37.7 11.1 %collective-permute-start.6 = (bf16[24,1152]{1,0:T(8,128)(2,1)S(1)}, bf16[24,1152]{1,0:T(8,128)(2,1)S(1)}, u32[]{:S(2)}, u32[]{:S(2)}) collective-permute-start(bf16[24,1152]{1,0:T(8,128)(2,1)S(1)} %maximum_select_fusion.6), channel_id=1, source_target_pairs={{0,16},{1,17},{2,18},{3,19},{4,20},{5,21},{6,22},{7,23},{8,24},{9,... | collective-permute-start | bytes 165896 | tf_op jit(solution)/shard_map/ppermute | solution.py:459
  48.6 18.3 %copy-start = (bf16[1792,384]{1,0:T(8,128)(2,1)}, bf16[1792,384]{1,0:T(8,128)(2,1)S(1)}, u32[]{:S(2)}) copy-start(bf16[1792,384]{1,0:T(8,128)(2,1)S(1)} %maximum_select_fusion.refs_1_) | copy-start | bytes 4128772
  48.6 13.0 %copy-start.8 = (f32[384]{0:T(512)S(1)}, f32[384]{0:T(512)}, u32[]{:S(2)}) copy-start(f32[384]{0:T(512)} %param.15) | copy-start | bytes 4612
  48.6 13.6 %copy-start.9 = (f32[384]{0:T(512)S(1)}, f32[384]{0:T(512)}, u32[]{:S(2)}) copy-start(f32[384]{0:T(512)} %param.16) | copy-start | bytes 4612
  48.6 14.1 %copy-start.6 = (f32[1536]{0:T(1024)S(1)}, f32[1536]{0:T(1024)}, u32[]{:S(2)}) copy-start(f32[1536]{0:T(1024)} %param.24) | copy-start | bytes 18436
  48.6 14.7 %copy-start.10 = (f32[384]{0:T(512)S(1)}, f32[384]{0:T(512)}, u32[]{:S(2)}) copy-start(f32[384]{0:T(512)} %param.20) | copy-start | bytes 4612
  48.7 15.3 %copy-start.11 = (f32[384]{0:T(512)S(1)}, f32[384]{0:T(512)}, u32[]{:S(2)}) copy-start(f32[384]{0:T(512)} %param.21) | copy-start | bytes 4612
  48.7 15.9 %copy-start.12 = (f32[384]{0:T(512)S(1)}, f32[384]{0:T(512)}, u32[]{:S(2)}) copy-start(f32[384]{0:T(512)} %param.22) | copy-start | bytes 4612
  48.7 16.4 %copy-start.13 = (f32[384]{0:T(512)S(1)}, f32[384]{0:T(512)}, u32[]{:S(2)}) copy-start(f32[384]{0:T(512)} %param.26) | copy-start | bytes 4612
  48.7 17.0 %copy-start.7 = (f32[768]{0:T(1024)S(1)}, f32[768]{0:T(1024)}, u32[]{:S(2)}) copy-start(f32[768]{0:T(1024)} %param.18) | copy-start | bytes 9220
  48.7 45.2 %collective-permute-start.4 = (bf16[1792,384]{1,0:T(8,128)(2,1)S(1)}, bf16[1792,384]{1,0:T(8,128)(2,1)S(1)}, u32[]{:S(2)}, u32[]{:S(2)}) collective-permute-start(bf16[1792,384]{1,0:T(8,128)(2,1)S(1)} %maximum_select_fusion.refs_1_), channel_id=1, source_target_pairs={{0,1},{1,0},{2,3},{3,2},{4,5},{5,4},{6,7},{7,6},{8,9},{9,8},{10,11... | collective-permute-start | bytes 4128776 | tf_op jit(solution)/shard_map/ppermute | solution.py:459
  48.8 5.5 %collective-permute-start.7 = (bf16[48,1152]{1,0:T(8,128)(2,1)S(1)}, bf16[48,1152]{1,0:T(8,128)(2,1)S(1)}, u32[]{:S(2)}, u32[]{:S(2)}) collective-permute-start(bf16[48,1152]{1,0:T(8,128)(2,1)S(1)} %maximum_select_fusion.5), channel_id=1, source_target_pairs={{0,2},{1,3},{2,0},{3,1},{4,6},{5,7},{6,4},{7,5},{8,10},{9,11},{10,... | collective-permute-start | bytes 331784 | tf_op jit(solution)/shard_map/ppermute | solution.py:459
  54.4 7.0 %collective-permute-start.8 = (bf16[96,1152]{1,0:T(8,128)(2,1)S(1)}, bf16[96,1152]{1,0:T(8,128)(2,1)S(1)}, u32[]{:S(2)}, u32[]{:S(2)}) collective-permute-start(bf16[96,1152]{1,0:T(8,128)(2,1)S(1)} %maximum_select_fusion.4), channel_id=1, source_target_pairs={{0,4},{1,5},{2,6},{3,7},{4,0},{5,1},{6,2},{7,3},{8,12},{9,13},{10,... | collective-permute-start | bytes 663560 | tf_op jit(solution)/shard_map/ppermute | solution.py:459
  61.5 5.4 %copy-start.2 = (bf16[192,1152]{1,0:T(8,128)(2,1)}, bf16[192,1152]{1,0:T(8,128)(2,1)S(1)}, u32[]{:S(2)}) copy-start(bf16[192,1152]{1,0:T(8,128)(2,1)S(1)} %maximum_select_fusion.2.refs_1_) | copy-start | bytes 1327108
  61.5 4.2 %collective-permute-start.9 = (bf16[192,1152]{1,0:T(8,128)(2,1)S(1)}, bf16[192,1152]{1,0:T(8,128)(2,1)S(1)}, u32[]{:S(2)}, u32[]{:S(2)}) collective-permute-start(bf16[192,1152]{1,0:T(8,128)(2,1)S(1)} %maximum_select_fusion.2.refs_1_), channel_id=1, source_target_pairs={{0,1},{1,0},{2,3},{3,2},{4,5},{5,4},{6,7},{7,6},{8,9},{9,8},{10,11... | collective-permute-start | bytes 1327112 | tf_op jit(solution)/shard_map/ppermute | solution.py:459
  65.7 1.2 copy-start.4
  93.9 1.1 copy-start.3
  173.6 26.8 %copy-start.14 = (bf16[16,112,384]{2,1,0:T(8,128)(2,1)S(1)}, bf16[16,112,384]{2,1,0:T(8,128)(2,1)}, u32[]{:S(2)}) copy-start(bf16[16,112,384]{2,1,0:T(8,128)(2,1)} %get-tuple-element.49) | copy-start | bytes 4128772
  199.9 2.3 collective-permute-start.10
  200.4 13.9 %collective-permute-start.15 = (bf16[16,112,384]{2,1,0:T(8,128)(2,1)S(1)}, bf16[16,112,384]{2,1,0:T(8,128)(2,1)S(1)}, u32[]{:S(2)}, u32[]{:S(2)}) collective-permute-start(bf16[16,112,384]{2,1,0:T(8,128)(2,1)S(1)} %copy-done.14), channel_id=1, source_target_pairs={{0,1},{1,0},{2,3},{3,2},{4,5},{5,4},{6,7},{7,6},{8,9},{9,8},{10,11... | collective-permute-start | bytes 4128776 | tf_op jit(solution)/shard_map/ppermute | solution.py:459
  202.3 12.0 %copy-start.1 = (f32[16,112,384]{2,1,0:T(8,128)S(1)}, f32[16,112,384]{2,1,0:T(8,128)}, u32[]{:S(2)}) copy-start(f32[16,112,384]{2,1,0:T(8,128)} %get-tuple-element.48) | copy-start | bytes 8257540
  203.9 9.4 %collective-permute-start.11 = (bf16[8,48,384]{2,1,0:T(8,128)(2,1)S(1)}, bf16[8,48,384]{2,1,0:T(8,128)(2,1)S(1)}, u32[]{:S(2)}, u32[]{:S(2)}) collective-permute-start(bf16[8,48,384]{2,1,0:T(8,128)(2,1)S(1)} %slice.312), channel_id=1, source_target_pairs={{0,2},{1,3},{2,0},{3,1},{4,6},{5,7},{6,4},{7,5},{8,10},{9,11},{10,... | collective-permute-start | bytes 884744 | tf_op jit(solution)/shard_map/ppermute | solution.py:459
  213.3 5.3 %collective-permute-start.12 = (bf16[4,48,384]{2,1,0:T(8,128)(2,1)S(1)}, bf16[4,48,384]{2,1,0:T(8,128)(2,1)S(1)}, u32[]{:S(2)}, u32[]{:S(2)}) collective-permute-start(bf16[4,48,384]{2,1,0:T(8,128)(2,1)S(1)} %slice.314), channel_id=1, source_target_pairs={{0,4},{1,5},{2,6},{3,7},{4,0},{5,1},{6,2},{7,3},{8,12},{9,13},{10,... | collective-permute-start | bytes 442376 | tf_op jit(solution)/shard_map/ppermute | solution.py:459
  214.6 16.6 %collective-permute-start.16 = (bf16[8,112,384]{2,1,0:T(8,128)(2,1)S(1)}, bf16[8,112,384]{2,1,0:T(8,128)(2,1)S(1)}, u32[]{:S(2)}, u32[]{:S(2)}) collective-permute-start(bf16[8,112,384]{2,1,0:T(8,128)(2,1)S(1)} %slice.310), channel_id=1, source_target_pairs={{0,2},{1,3},{2,0},{3,1},{4,6},{5,7},{6,4},{7,5},{8,10},{9,11},{10,... | collective-permute-start | bytes 2064392 | tf_op jit(solution)/shard_map/ppermute | solution.py:459
  218.7 4.4 %collective-permute-start.13 = (bf16[2,48,384]{2,1,0:T(8,128)(2,1)S(1)}, bf16[2,48,384]{2,1,0:T(8,128)(2,1)S(1)}, u32[]{:S(2)}, u32[]{:S(2)}) collective-permute-start(bf16[2,48,384]{2,1,0:T(8,128)(2,1)S(1)} %slice.316), channel_id=1, source_target_pairs={{0,8},{1,9},{2,10},{3,11},{4,12},{5,13},{6,14},{7,15},{8,0},{9,1},... | collective-permute-start | bytes 221192 | tf_op jit(solution)/shard_map/ppermute | solution.py:459
  223.1 4.9 %collective-permute-start.14 = (bf16[1,48,384]{2,1,0:T(8,128)(2,1)S(1)}, bf16[1,48,384]{2,1,0:T(8,128)(2,1)S(1)}, u32[]{:S(2)}, u32[]{:S(2)}) collective-permute-start(bf16[1,48,384]{2,1,0:T(8,128)(2,1)S(1)} %slice.317), channel_id=1, source_target_pairs={{0,16},{1,17},{2,18},{3,19},{4,20},{5,21},{6,22},{7,23},{8,24},{9,... | collective-permute-start | bytes 110600 | tf_op jit(solution)/shard_map/ppermute | solution.py:459
  231.4 8.4 %collective-permute-start.17 = (bf16[4,112,384]{2,1,0:T(8,128)(2,1)S(1)}, bf16[4,112,384]{2,1,0:T(8,128)(2,1)S(1)}, u32[]{:S(2)}, u32[]{:S(2)}) collective-permute-start(bf16[4,112,384]{2,1,0:T(8,128)(2,1)S(1)} %slice.311), channel_id=1, source_target_pairs={{0,4},{1,5},{2,6},{3,7},{4,0},{5,1},{6,2},{7,3},{8,12},{9,13},{10,... | collective-permute-start | bytes 1032200 | tf_op jit(solution)/shard_map/ppermute | solution.py:459
  240.0 5.5 %collective-permute-start.18 = (bf16[2,112,384]{2,1,0:T(8,128)(2,1)S(1)}, bf16[2,112,384]{2,1,0:T(8,128)(2,1)S(1)}, u32[]{:S(2)}, u32[]{:S(2)}) collective-permute-start(bf16[2,112,384]{2,1,0:T(8,128)(2,1)S(1)} %slice.313), channel_id=1, source_target_pairs={{0,8},{1,9},{2,10},{3,11},{4,12},{5,13},{6,14},{7,15},{8,0},{9,1},... | collective-permute-start | bytes 516104 | tf_op jit(solution)/shard_map/ppermute | solution.py:459
  245.5 6.5 %collective-permute-start.19 = (bf16[1,112,384]{2,1,0:T(8,128)(2,1)S(1)}, bf16[1,112,384]{2,1,0:T(8,128)(2,1)S(1)}, u32[]{:S(2)}, u32[]{:S(2)}) collective-permute-start(bf16[1,112,384]{2,1,0:T(8,128)(2,1)S(1)} %slice.315), channel_id=1, source_target_pairs={{0,16},{1,17},{2,18},{3,19},{4,20},{5,21},{6,22},{7,23},{8,24},{9,... | collective-permute-start | bytes 258056 | tf_op jit(solution)/shard_map/ppermute | solution.py:459

commit v3 on v2

--- a/solution.py
+++ b/solution.py
@@ -14,8 +14,9 @@
 SL = 256
 CH = 256
 NI = 2
-FWD_CUT = 14
-BWD_CUT = 6
+NF = 4
+FWD_CUTS = (16,)
+BWD_CUTS = (4,)
 SC = 0.125 * 1.4426950408889634
 norm_eps = 1e-06
 f32 = jnp.float32
@@ -55,17 +56,24 @@
             body(parity)
 
 
-def attn_fwd(me_ref, *refs, n, lead):
+def row(v_ref):
+    return v_ref[...].reshape(1, -1)
+
+
+def attn_fwd(g_ref, b_ref, qv_ref, *refs, n, lead):
     if lead:
-        ga_ref, gb_ref, x_ref, g_ref, b_ref, bias_ref, pt_ref, wt_ref, ot_ref, wT_s, a_s, w_s = refs
+        me_ref, ga_ref, gb_ref, x_ref, pt_ref, wt_ref, ot_ref, wT_s, bias, a_s, w_s = refs
     else:
-        wT_s, x_ref, g_ref, b_ref, bias_ref, _, _, _, pt_ref, wt_ref, ot_ref, a_s = refs
+        wT_s, x_ref, _, _, _, pt_ref, wt_ref, ot_ref, bias, a_s = refs
 
     @pl.when(pl.program_id(0) == 0)
     def _():
         a_s[...] = jnp.zeros_like(a_s)
+        bias[D : 2 * D, :] = jnp.zeros((D, SL), f32)
+        for q in (0, 1):
+            col = jnp.broadcast_to(qv_ref[D * q : D * (q + 1)].reshape(1, D), (8, D)).T[:, 0:1]
+            bias[2 * D * q : 2 * D * q + D, :] = jnp.broadcast_to(col, (D, SL))
         if lead:
-            me = me_ref[0]
             r1 = D // n
 
             def gather(parity):
@@ -74,18 +82,17 @@
                     p = place(k, n)
                     w_s[r1 * k : r1 * (k + 1), :] = src[r1 * p : r1 * (p + 1), :]
 
-            for_parity(me, gather)
+            for_parity(me_ref[0], gather)
             wT_s[...] = w_s[...].T
 
     valid = lax.broadcasted_iota(jnp.int32, (16, SL), 0) < S - 192
 
     def ln(i):
         n1, _ = norm(x_ref[i].astype(f32))
-        a_s[i, :S, :] = (n1 * g_ref[...] + b_ref[...]).astype(bf16)
+        a_s[i, :S, :] = (n1 * row(g_ref) + row(b_ref)).astype(bf16)
 
     def proj(i):
-        pT = dot(wT_s[...], a_s[i], NT) + bias_ref[...]
-        pt_ref[i] = pT.astype(bf16)
+        pt_ref[i] = (dot(wT_s[...], a_s[i], NT) + bias[...]).astype(bf16)
 
     def soft(i, h):
         qT = pt_ref[i, 64 * h : 64 * h + 64, :]
@@ -105,13 +112,17 @@
         vT = pt_ref[i, 2 * D + 64 * h : 2 * D + 64 * h + 64, :SR]
         ot_ref[i, 64 * h : 64 * h + 64, :] = dot(vT, wt_ref[i, h], NN).astype(bf16)
 
-    for i in range(NI): ln(i)
-    for i in range(NI): proj(i)
-    for i in range(NI):
+    for i in range(NF):
+        ln(i)
+    for i in range(NF):
+        proj(i)
+    for i in range(NF):
         for h in range(H):
             soft(i, h)
-            if i > 0: pv(i - 1, h)
-    for h in range(H): pv(NI - 1, h)
+            if i > 0:
+                pv(i - 1, h)
+    for h in range(H):
+        pv(NF - 1, h)
 
 
 ERF_P = 0.3275911
@@ -160,9 +171,9 @@
     lax.fori_loop(0, n, one, 0)
 
 
-def mlp(me_ref, ga_ref, gb_ref, x_ref, ot_ref, e_ref, pb_ref, g_ref, b_ref, ub_ref, db_ref,
+def mlp(pb_ref, g_ref, b_ref, ub_ref, db_ref, me_ref, ga_ref, gb_ref, x_ref, ot_ref, e_ref,
         out_ref, dx1_ref, dot_ref, keep_ref, send_ref,
-        xs, es, fs, pj_s, up_s, dn_s, gup, gdn, gpj, small, stage, upT, dnT, gs, us, bt, *, n, bits):
+        xs, es, fs, pj_s, up_s, dn_s, gup, gdn, gpj, small, stage, upT, dnT, gs, us, bt, ub_s, *, n, bits):
     me = me_ref[0]
     step = pl.program_id(0)
     r1, r4 = D // n, FF // n
@@ -177,6 +188,8 @@
         gdn[...] = jnp.zeros_like(gdn)
         gpj[...] = jnp.zeros_like(gpj)
         small[...] = jnp.zeros_like(small)
+        for q in range(4):
+            ub_s[:, D * q : D * (q + 1)] = ub_ref[D * q : D * (q + 1)].reshape(1, D)
         bt[:, D:, :] = jnp.ones((NI, 16, SR), bf16)
 
         def gather(parity):
@@ -204,16 +217,16 @@
         xs[i, :S, :] = x_ref[i]
         es[i, :S, :] = e_ref[i]
         s["oT"] = ot_ref[i, :, :SR]
-        s["x1"] = xs[i].astype(f32) + dot(s["oT"], pj_s[...], TN) + pb_ref[...]
+        s["x1"] = xs[i].astype(f32) + dot(s["oT"], pj_s[...], TN) + row(pb_ref)
         s["n2"], s["r2"] = norm(s["x1"])
-        bb = (s["n2"] * g_ref[...] + b_ref[...]).astype(bf16)
+        bb = (s["n2"] * row(g_ref) + row(b_ref)).astype(bf16)
         s["bb"] = bb
         bt[i, :D, :] = bb.T
         s["eT"] = es[i].T
 
     def p2(i, c):
         cols = slice(c * CH, (c + 1) * CH)
-        u = dot(st[i]["bb"], up_s[:, cols], NN) + ub_ref[:, cols]
+        u = dot(st[i]["bb"], up_s[:, cols], NN) + ub_s[:, cols]
         g, gp = gelu_parts(u)
         gs[i, :, cols] = g.astype(bf16)
         us[i, :, cols] = (dot(es[i], dnT[:, cols], NN) * gp).astype(bf16)
@@ -226,21 +239,21 @@
     def p4(i):
         s = st[i]
         s["dB"] = dot(us[i], upT[...], NN)
-        out_ref[i] = (s["x1"] + db_ref[...] + dot(gs[i], dn_s[...], NN))[:S]
+        out_ref[i] = (s["x1"] + row(db_ref) + dot(gs[i], dn_s[...], NN))[:S]
 
     def p5(i):
         s = st[i]
         dB, n2 = s["dB"], s["n2"]
-        dn = dB * g_ref[...]
+        dn = dB * row(g_ref)
         ef = es[i].astype(f32)
         dx1 = ef + s["r2"] * (dn - jnp.mean(dn, axis=-1, keepdims=True) - n2 * jnp.mean(dn * n2, axis=-1, keepdims=True))
         dx1_ref[i] = dx1[:S]
         ff = dx1.astype(bf16)
         fs[i, :SR, :] = ff
-        small[0:8, 0:384] += fold(dB * n2)
-        small[0:8, 384:768] += fold(dB)
-        small[0:8, 768:1152] += fold(ff.astype(f32))
-        small[0:8, 1152:1536] += fold(ef)
+        small[:, 0:384] += fold(dB * n2)
+        small[:, 384:768] += fold(dB)
+        small[:, 768:1152] += fold(ff.astype(f32))
+        small[:, 1152:1536] += fold(ef)
 
     def p6(i):
         gpj[...] += dot(st[i]["oT"], fs[i, :SR, :], NN)
@@ -281,7 +294,7 @@
         emit(me, stage, keep_ref, send_ref, n, bits)
 
 
-def attn_bwd(me_ref, x_ref, pt_ref, wt_ref, dot_ref, dx1_ref, g_ref, b_ref, wT_s, *refs, n, bits, lead, last):
+def attn_bwd(g_ref, b_ref, me_ref, x_ref, pt_ref, wt_ref, dot_ref, dx1_ref, wT_ref, *refs, n, bits, lead, last):
     if not lead:
         gqi_ref, smi_ref, _ = refs[:3]
         refs = refs[3:]
@@ -306,7 +319,7 @@
     def ln(i):
         n1, r1 = norm(x_ref[i].astype(f32))
         st[i].update(n1=n1, r1=r1)
-        as_[i, :S, :D] = (n1 * g_ref[...] + b_ref[...]).astype(bf16)
+        as_[i, :S, :D] = (n1 * row(g_ref) + row(b_ref)).astype(bf16)
 
     def dz(i, h):
         w = wt_ref[i, h].astype(f32)
@@ -323,32 +336,35 @@
         dp_s[i, ks[h], :] = (dot(pt_ref[i, hs[h], :], dz_s[i, h], NT) * 0.125).astype(bf16)
 
     def gr(i):
-        st[i]["dA"] = dot(dp_s[i], wT_s[...], TN)[:S]
+        st[i]["dA"] = dot(dp_s[i], wT_ref[...], TN)[:S]
         gq[...] += dot(dp_s[i], as_[i], NN)
 
     def fin(i):
         n1, r1, dA = st[i]["n1"], st[i]["r1"], st[i]["dA"]
-        dm = dA * g_ref[...]
+        dm = dA * row(g_ref)
         din_ref[i] = dx1_ref[i] + r1 * (
             dm - jnp.mean(dm, axis=-1, keepdims=True) - n1 * jnp.mean(dm * n1, axis=-1, keepdims=True))
-        small[0:1, 0:384] += jnp.sum(dA * n1, axis=0, keepdims=True)
-        small[0:1, 384:768] += jnp.sum(dA, axis=0, keepdims=True)
-
-    for i in range(NI): ln(i)
-    for h in range(H): dz(0, h)
-    for h in range(H):
-        dz(1, h)
-        dv(0, h)
-        dq(0, h)
-        dk(0, h)
-    for h in range(H):
-        dv(1, h)
-        dq(1, h)
-        dk(1, h)
-    gr(0)
-    gr(1)
-    fin(0)
-    fin(1)
+        small[0:1, 0:D] += jnp.sum(dA * n1, axis=0, keepdims=True)
+        small[0:1, D : 2 * D] += jnp.sum(dA, axis=0, keepdims=True)
+
+    for i in range(NI):
+        ln(i)
+    for i in range(NI + 1):
+        for h in range(H):
+            if i < NI:
+                dz(i, h)
+            if i > 0:
+                dv(i - 1, h)
+                dq(i - 1, h)
+                dk(i - 1, h)
+        if i > 1:
+            gr(i - 2)
+        if i > 2:
+            fin(i - 3)
+    gr(NI - 1)
+    if NI > 1:
+        fin(NI - 2)
+    fin(NI - 1)
 
     if last:
         @pl.when(step == pl.num_programs(0) - 1)
@@ -367,8 +383,53 @@
             emit(me, stage, keep_ref, send_ref, n, bits)
 
 
-def img(shape, at=0):
-    return pl.BlockSpec((NI,) + shape, lambda i: (i + at // NI,) + (0,) * len(shape))
+def pack_rest(pj_ref, up_ref, dn_ref, out_ref, *, n):
+    r1 = D // n
+    out_ref[:r1, :] = pj_ref[...]
+    for q in range(4):
+        out_ref[r1 * (1 + q) : r1 * (2 + q), :] = up_ref[:, D * q : D * (q + 1)]
+    out_ref[5 * r1 : 9 * r1, :] = dn_ref[...]
+    out_ref[9 * r1 :, :] = jnp.zeros((rest_rows(n) - 9 * r1, D), bf16)
+
+
+def total_of(refs):
+    total = refs[0][0]
+    for got in refs[1:]:
+        total = total + got[0].astype(f32)
+    return total
+
+
+def finish_mlp(*refs, n):
+    *parts, pj, pb, gain, shift, up, ub, dn, db = refs
+    r1, r4 = D // n, FF // n
+    t = total_of(parts)
+    pj[...] = t[:r1]
+    for q in range(4):
+        up[:, D * q : D * (q + 1)] = t[r1 * (1 + q) : r1 * (2 + q)]
+    dn[...] = t[5 * r1 : 9 * r1]
+    for i, out in enumerate((gain, shift, pb, db)):
+        out[...] = t[9 * r1, r1 * i : r1 * (i + 1)]
+    ub[...] = t[9 * r1, 4 * r1 : 4 * r1 + r4]
+
+
+def finish_attn(*refs, n):
+    *parts, gain, shift, qkv, qv = refs
+    r1 = D // n
+    t = total_of(parts)
+    for q in range(3):
+        qkv[:, D * q : D * (q + 1)] = t[r1 * q : r1 * (q + 1)]
+    for i, out in enumerate((gain, shift)):
+        out[...] = t[3 * r1, r1 * i : r1 * (i + 1)]
+    qv[...] = t[3 * r1, 2 * r1 : 4 * r1]
+
+
+def finish(body, parts, n, shapes):
+    return pl.pallas_call(
+        lambda *refs: body(*refs, n=n), name="finish", out_shape=[shape_of(*s) for s in shapes])(*parts)
+
+
+def img(shape, at=0, count=NI):
+    return pl.BlockSpec((count,) + shape, lambda i: (i + at // count,) + (0,) * len(shape))
 
 
 def res(shape):
@@ -377,7 +438,10 @@
 
 smem = pl.BlockSpec(memory_space=pltpu.SMEM)
 hbm = pl.BlockSpec(memory_space=pl.ANY)
-params = pltpu.CompilerParams(dimension_semantics=("arbitrary",), vmem_limit_bytes=60 * 2**20)
+
+
+def params(mib):
+    return pltpu.CompilerParams(dimension_semantics=("arbitrary",), vmem_limit_bytes=mib * 2**20)
 
 
 def shape_of(*dims, dtype=f32):
@@ -388,95 +452,122 @@
     return pltpu.VMEM(dims, dtype)
 
 
-def run_fwd(n, me, weights, x, g1, b1, bias, at, count, kept=()):
+def vec_specs(vecs):
+    return [pl.BlockSpec(v.shape, lambda i: (0,)) for v in vecs]
+
+
+def run_fwd(n, me, vecs, weights, x, at, count, kept=()):
     m = x.shape[0]
     lead = not kept
-    out_specs = [img((3 * D, SL), at), img((H, SR, SL), at), img((D, SL), at)]
-    out_shape = [shape_of(m, 3 * D, SL, dtype=bf16), shape_of(m, H, SR, SL, dtype=bf16), shape_of(m, D, SL, dtype=bf16)]
-    scratch = [vmem(NI, SL, D)]
+    shapes = [(3 * D, SL), (H, SR, SL), (D, SL)]
+    out_specs = [img(s, at, NF) for s in shapes]
+    out_shape = [shape_of(m, *s, dtype=bf16) for s in shapes]
+    scratch = [vmem(3 * D, SL, dtype=f32), vmem(NF, SL, D)]
     if lead:
         out_specs, out_shape = out_specs + [res((3 * D, D))], out_shape + [shape_of(3 * D, D, dtype=bf16)]
         scratch = scratch + [vmem(D, 3 * D)]
-    base = 1 + len(weights) + 4
+    ins = [*vecs] + ([me] if lead else []) + list(weights) + [x]
     return pl.pallas_call(
-        lambda *refs: attn_fwd(*refs, n=n, lead=lead), grid=(count // NI,), name="attn_fwd",
-        in_specs=[smem] + [res(w.shape) for w in weights] + [img((S, D), at), res((1, D)), res((1, D)), res((3 * D, SL))]
+        lambda *refs: attn_fwd(*refs, n=n, lead=lead), grid=(count // NF,), name="attn_fwd",
+        in_specs=vec_specs(vecs) + ([smem] if lead else []) + [res(w.shape) for w in weights] + [img((S, D), at, NF)]
         + [hbm] * len(kept),
         out_specs=out_specs, out_shape=out_shape, scratch_shapes=scratch,
-        input_output_aliases={base + i: i for i in range(len(kept))},
-        compiler_params=params,
-    )(me, *weights, x, g1, b1, bias, *kept)
+        input_output_aliases={len(ins) + i: i for i in range(len(kept))},
+        compiler_params=params(60),
+    )(*ins, *kept)
 
 
 def chunk_rows(n, parts):
     return -(-(parts * (D // n) + 1) // 16) * 16
 
 
-def run_mlp(n, bits, me, ga, gb, x, oT, e, pb, g2, b2, ub, db):
+def run_mlp(n, bits, me, vecs, ga, gb, x, oT, e):
     m = x.shape[0]
     cr = chunk_rows(n, 9)
     return pl.pallas_call(
         lambda *refs: mlp(*refs, n=n, bits=bits), grid=(m // NI,), name="mlp",
-        in_specs=[smem, res(ga.shape), res(gb.shape), img((S, D)), img((D, SL)), img((S, D)),
-                  res((1, D)), res((1, D)), res((1, D)), res((1, FF)), res((1, D))],
+        in_specs=vec_specs(vecs) + [smem, res(ga.shape), res(gb.shape), img((S, D)), img((D, SL)), img((S, D))],
         out_specs=[img((S, D)), img((S, D)), img((D, SL)), res((n // 2, cr, D)), res((n // 2, cr, D))],
         out_shape=[shape_of(m, S, D), shape_of(m, S, D), shape_of(m, D, SL, dtype=bf16),
                    shape_of(n // 2, cr, D), shape_of(n // 2, cr, D, dtype=bf16)],
         scratch_shapes=[vmem(NI, SR, D), vmem(NI, SR, D), vmem(NI, SL, D), vmem(D, D), vmem(D, FF), vmem(FF, D),
                         vmem(D + 16, FF, dtype=f32), vmem(D, FF, dtype=f32), vmem(D, D, dtype=f32),
                         vmem(8, FF, dtype=f32), vmem(n, cr, D, dtype=f32), vmem(FF, D), vmem(D, FF),
-                        vmem(NI, SR, FF), vmem(NI, SR, FF), vmem(NI, D + 16, SR)],
-        compiler_params=params,
-    )(me, ga, gb, x, oT, e, pb, g2, b2, ub, db)
-
-
-def run_bwd(n, bits, me, x, pt, wt, doT, dx1, g1, b1, wT, at, count, kept=()):
+                        vmem(NI, SR, FF), vmem(NI, SR, FF), vmem(NI, D + 16, SR), vmem(1, FF, dtype=f32)],
+        compiler_params=params(60),
+    )(*vecs, me, ga, gb, x, oT, e)
+
+
+def run_bwd(n, bits, me, vecs, x, pt, wt, doT, dx1, wT, at, count, kept=()):
     m = x.shape[0]
     cr = chunk_rows(n, 3)
     lead, last = not kept, at + count == m
     out_specs, out_shape = [img((S, D), at)], [shape_of(m, S, D)]
     scratch = [vmem(NI, SR, 512), vmem(NI, 3 * D, SR), vmem(NI, H, SR, SL)]
-    sums = [((3 * D, 512), f32), ((8, 2 * D), f32)]
+    sums = [(3 * D, 512), (8, 2 * D)]
     if last:
         out_specs = out_specs + [res((n // 2, cr, D))] * 2
         out_shape = out_shape + [shape_of(n // 2, cr, D), shape_of(n // 2, cr, D, dtype=bf16)]
-        scratch = scratch + [vmem(*s, dtype=t) for s, t in sums] + [vmem(n, cr, D, dtype=f32)]
+        scratch = scratch + [vmem(*s, dtype=f32) for s in sums] + [vmem(n, cr, D, dtype=f32)]
     else:
-        out_specs = out_specs + [res(s) for s, _ in sums]
-        out_shape = out_shape + [shape_of(*s, dtype=t) for s, t in sums]
+        out_specs, out_shape = out_specs + [res(s) for s in sums], out_shape + [shape_of(*s) for s in sums]
     return pl.pallas_call(
         lambda *refs: attn_bwd(*refs, n=n, bits=bits, lead=lead, last=last), grid=(count // NI,), name="attn_bwd",
-        in_specs=[smem, img((S, D), at), img((3 * D, SL), at), img((H, SR, SL), at), img((D, SL), at), img((S, D), at),
-                  res((1, D)), res((1, D)), res((3 * D, D))]
-        + ([] if lead else [res(s) for s, _ in sums] + [hbm]),
+        in_specs=vec_specs(vecs)
+        + [smem, img((S, D), at), img((3 * D, SL), at), img((H, SR, SL), at), img((D, SL), at), img((S, D), at), res((3 * D, D))]
+        + ([] if lead else [res(s) for s in sums] + [hbm]),
         out_specs=out_specs, out_shape=out_shape, scratch_shapes=scratch,
         input_output_aliases={} if lead else {11: 0},
-        compiler_params=params,
-    )(me, x, pt, wt, doT, dx1, g1, b1, wT, *kept)
+        compiler_params=params(60),
+    )(*vecs, me, x, pt, wt, doT, dx1, wT, *kept)
+
+
+def swap_mask(v, mask, n):
+    return lax.ppermute(v, "dp", [(i, i ^ mask) for i in range(n)])
 
 
 def swap(v, bit, n):
-    return lax.ppermute(v, "dp", [(i, i ^ (1 << bit)) for i in range(n)])
-
-
-def gather_halves(v, me, n):
+    return swap_mask(v, 1 << bit, n)
+
+
+def pick(low, a, b):
+    return jnp.where(low, jnp.concatenate([a, b], axis=0), jnp.concatenate([b, a], axis=0))
+
+
+def gather_halves(v, at, n, paired):
     bits = stage_bits(n)
-    for b in bits:
+    low = {b: (at >> b) & 1 == 0 for b in bits}
+    alone = bits[:-2] if paired else bits
+    for b in alone:
         other = swap(v, b, n)
-        high = (me >> b) & 1 == 1
-        v = jnp.where(high, jnp.concatenate([other, v], axis=0), jnp.concatenate([v, other], axis=0))
+        v = pick(low[b], v, other)
+    if paired:
+        got = []
+        for w in (1, 2, 3):
+            mask = ((w & 1) << bits[-2]) | ((w >> 1) << bits[-1])
+            got.append(swap_mask(v, mask, n))
+        near, far = (v, got[0]), (got[1], got[2])
+        b0, b1 = low[bits[-2]], low[bits[-1]]
+        v = pick(b1, pick(b0, *near), pick(b0, *far))
     return v, swap(v, 0, n)
 
 
 def reduce_parts(keep, send, n, bits):
     got = swap(send, 0, n)
     total = keep + got.astype(f32)
-    for b in bits:
-        half = total.shape[0] // 2
-        part = total[half:].astype(bf16)
-        got = swap(part, b, n)
-        total = total[:half] + got.astype(f32)
-    return total[0]
+    for i in range(0, len(bits), 2):
+        pair = bits[i : i + 2]
+        ways = 1 << len(pair)
+        size = total.shape[0] // ways
+        rest = total[size:].astype(bf16)
+        parts = [total[:size]]
+        for w in range(1, ways):
+            mask = sum(((w >> (len(pair) - 1 - j)) & 1) << b for j, b in enumerate(pair))
+            parts.append(swap_mask(rest[size * (w - 1) : size * w], mask, n))
+        total = parts[0]
+        for got in parts[1:]:
+            total = total + got.astype(f32)
+    return parts
 
 
 def on_device(n, block_input, first_gain, first_shift, qkv_weight, query_value_bias, proj_weight, proj_bias,
@@ -487,34 +578,32 @@
     at = lax.axis_index("dp").astype(jnp.int32)
     me = at.reshape(1)
 
-    def row(v):
-        return v.reshape(1, -1)
-
-    bias = jnp.concatenate([query_value_bias[:D], jnp.zeros((D,), f32), query_value_bias[D:]])
-    bias = jnp.broadcast_to(bias[:, None], (3 * D, SL))
-    qa, qb = gather_halves(qkv_weight, at, n)
-    rest = jnp.concatenate(
-        [proj_weight] + [up_weight[:, D * q : D * (q + 1)] for q in range(4)] + [down_weight]
-        + [jnp.zeros((rest_rows(n) - 9 * r1, D), bf16)], axis=0)
-    wa, wb = gather_halves(rest, at, n)
+    qa, qb = gather_halves(qkv_weight, at, n, False)
+    rest = pl.pallas_call(
+        lambda *refs: pack_rest(*refs, n=n), name="pack",
+        out_shape=shape_of(rest_rows(n), D, dtype=bf16))(proj_weight, up_weight, down_weight)
+    wa, wb = gather_halves(rest, at, n, True)
     m = block_input.shape[0]
-    norm1 = (row(first_gain), row(first_shift))
-    cut = FWD_CUT
-    *acts, wT = run_fwd(n, me, (qa, qb), block_input, *norm1, bias, 0, cut)
-    pt, wt, oT = run_fwd(n, me, (wT,), block_input, *norm1, bias, cut, m - cut, acts)
-    out, dx1, doT, keep, send = run_mlp(
-        n, bits, me, wa, wb, block_input, oT, output_cotangent, row(proj_bias), row(second_gain),
-        row(second_shift), row(up_bias), row(down_bias))
+    acts, wT = (), None
+    vecs = (first_gain, first_shift, query_value_bias)
+    for i, (lo, hi) in enumerate(zip((0,) + FWD_CUTS, FWD_CUTS + (m,))):
+        made = run_fwd(n, me, vecs, (qa, qb) if i == 0 else (wT,), block_input, lo, hi - lo, acts)
+        acts, wT = made[:3], made[3] if i == 0 else wT
+    pt, wt, oT = acts
+    vecs = (proj_bias, second_gain, second_shift, up_bias, down_bias)
+    out, dx1, doT, keep, send = run_mlp(n, bits, me, vecs, wa, wb, block_input, oT, output_cotangent)
     mp = reduce_parts(keep, send, n, bits)
-    cut = BWD_CUT
-    dins, gq, sm = run_bwd(n, bits, me, block_input, pt, wt, doT, dx1, *norm1, wT, 0, cut)
-    din, keep, send = run_bwd(n, bits, me, block_input, pt, wt, doT, dx1, *norm1, wT, cut, m - cut, (gq, sm, dins))
+    kept = ()
+    vecs = (first_gain, first_shift)
+    for lo, hi in zip((0,) + BWD_CUTS, BWD_CUTS + (m,)):
+        made = run_bwd(n, bits, me, vecs, block_input, pt, wt, doT, dx1, wT, lo, hi - lo, kept)
+        kept = (made[1], made[2], made[0])
+    din, keep, send = made
     ap = reduce_parts(keep, send, n, bits)
-    g_up = jnp.concatenate([mp[r1 * (1 + q) : r1 * (2 + q)] for q in range(4)], axis=1)
-    g_qkv = jnp.concatenate([ap[r1 * q : r1 * (q + 1)] for q in range(3)], axis=1)
-    sm, sa = mp[9 * r1], ap[3 * r1]
-    return (out, din, sa[:r1], sa[r1 : 2 * r1], g_qkv, sa[2 * r1 : 4 * r1], mp[:r1], sm[2 * r1 : 3 * r1],
-            sm[:r1], sm[r1 : 2 * r1], g_up, sm[4 * r1 : 4 * r1 + r4], mp[5 * r1 : 9 * r1], sm[3 * r1 : 4 * r1])
+    g_proj, g_pb, gain2, shift2, g_up, g_ub, g_down, g_db = finish(
+        finish_mlp, mp, n, [(r1, D), (r1,), (r1,), (r1,), (r1, FF), (r4,), (r4, D), (r1,)])
+    gain1, shift1, g_qkv, g_qv = finish(finish_attn, ap, n, [(r1,), (r1,), (r1, 3 * D), (2 * r1,)])
+    return (out, din, gain1, shift1, g_qkv, g_qv, g_proj, g_pb, gain2, shift2, g_up, g_ub, g_down, g_db)
 
 
 def solution(mesh):

time: 256 us -> 238 us (0.930)
  waiting for transfers between devices: 70.7 us -> 58.8 us
  local copies, waits for them, and re-layouts: 16.7 us -> 5.26 us
  starting transfers between devices: 30.6 us -> 33.6 us
    ppermute x20 -> x25, waiting for transfers between devices: 70.7 us -> 58.8 us  [swap_mask(): return lax.ppermute(v, 'dp', [(i, i ^ mask) for i in range(n)])]
    concatenate x3 -> x0, local copies, waits for them, and re-layouts: 5.63 us -> none  [the longest x1 1.9 us: gather_halves(): jnp.concatenate([other, v], axis=0)]
    pallas_call x0 -> x3, Pallas kernels: none -> 4.9 us  [the longest x2 3.43 us: finish(): pl.pallas_call(lambda *refs: body(*refs, n=n), name='finish', out_shape=[...]
    reshape x7 -> x0, local copies, waits for them, and re-layouts: 4.04 us -> none  [row(): return v.reshape(1, -1)]
    slice x17 -> x6, local copies, waits for them, and re-layouts: 4.6 us -> 1.51 us  [the longest x2 1.31 us: reduce_parts(): parts = [total[:size]]]
    ppermute x20 -> x25, starting transfers between devices: 30.6 us -> 33.6 us  [swap_mask(): return lax.ppermute(v, 'dp', [(i, i ^ mask) for i in range(n)])]
    pallas_call x2, Pallas kernels: 26.9 us -> 24.1 us  [run_fwd(): pl.pallas_call(lambda *refs: attn_fwd(*refs, n=n, lead=lead), grid=(count...]
    unnamed x30 -> x22, local copies, waits for them, and re-layouts: 1.17 us -> 3.76 us
  transfers between devices with their start and end apart: 20 -> 25, of which waited for: 16 -> 16; matrix products, arithmetic and copies ran while one was open for 4% -> 2% of each run, Pallas kernels for 11% -> 27%
where the time goes in v3:
time: 238 us; the launch traced here: 237 us
  Pallas kernels  134 us (56%)
  waiting for transfers between devices  58.8 us (25%)
  starting transfers between devices  33.6 us (14%)
  local copies, waits for them, and re-layouts  5.26 us (2%)
  other arithmetic  5.14 us (2%)
    pallas_call x1, Pallas kernels, run_mlp(): pl.pallas_call(lambda *refs: mlp(*refs, n=n, bits=bits), grid=(m // NI,),...  66.1 us
    ppermute x25, waiting for transfers between devices, swap_mask(): return lax.ppermute(v, 'dp', [(i, i ^ mask) for i in range(n)])  58.8 us
    pallas_call x2, Pallas kernels, run_bwd(): pl.pallas_call(lambda *refs: attn_bwd(*refs, n=n, bits=bits, lead=lead, l...  38.8 us
    ppermute x25, starting transfers between devices, swap_mask(): return lax.ppermute(v, 'dp', [(i, i ^ mask) for i in range(n)])  33.6 us
    pallas_call x2, Pallas kernels, run_fwd(): pl.pallas_call(lambda *refs: attn_fwd(*refs, n=n, lead=lead), grid=(count...  24.1 us
  transfers between devices with their start and end apart: 25, of which 16 were waited for; matrix products, arithmetic and copies ran while one was open for 2% of the time, Pallas kernels for 27%

profile of v3, /device:TPU:0, one launch (start us, length us, event | category | flops | bytes accessed | tf_op | source)
XLA Modules:
  0.0 237.5 jit_solution(3820021560375298854)
XLA Ops:
  0.6 1.5 pack.1
  2.1 3.1 %collective-permute-start = (bf16[112,384]{1,0:T(8,128)(2,1)}, bf16[112,384]{1,0:T(8,128)(2,1)S(1)}, u32[]{:S(2)}, u32[]{:S(2)}) collective-permute-start(bf16[112,384]{1,0:T(8,128)(2,1)} %pack.1), channel_id=1, source_target_pairs={{0,8},{1,9},{2,10},{3,11},{4,12},{5,13},{6,14},{7,15},{8,0},{9,1},... | collective-permute-start | bytes 258056 | tf_op jit(solution)/shard_map/ppermute | solution.py:526
  5.2 2.7 %collective-permute-done = bf16[112,384]{1,0:T(8,128)(2,1)S(1)} collective-permute-done((bf16[112,384]{1,0:T(8,128)(2,1)}, bf16[112,384]{1,0:T(8,128)(2,1)S(1)}, u32[]{:S(2)}, u32[]{:S(2)}) %collective-permute-start) | collective-permute-done | bytes 86048 | tf_op jit(solution)/shard_map/ppermute | solution.py:526
  7.9 1.0 maximum_select_fusion.6
  8.9 3.0 %collective-permute-start.1 = (bf16[224,384]{1,0:T(8,128)(2,1)S(1)}, bf16[224,384]{1,0:T(8,128)(2,1)S(1)}, u32[]{:S(2)}, u32[]{:S(2)}) collective-permute-start(bf16[224,384]{1,0:T(8,128)(2,1)S(1)} %maximum_select_fusion.6), channel_id=1, source_target_pairs={{0,16},{1,17},{2,18},{3,19},{4,20},{5,21},{6,22},{7,23},{8,24},{9,... | collective-permute-start | bytes 516104 | tf_op jit(solution)/shard_map/ppermute | solution.py:526
  11.9 7.2 %collective-permute-done.1 = bf16[224,384]{1,0:T(8,128)(2,1)S(1)} collective-permute-done((bf16[224,384]{1,0:T(8,128)(2,1)S(1)}, bf16[224,384]{1,0:T(8,128)(2,1)S(1)}, u32[]{:S(2)}, u32[]{:S(2)}) %collective-permute-start.1) | collective-permute-done | bytes 172064 | tf_op jit(solution)/shard_map/ppermute | solution.py:526
  19.2 1.4 collective-permute-start.2
  20.6 0.7 collective-permute-start.6
  21.2 1.5 collective-permute-start.3
  23.2 1.5 collective-permute-done.6
  24.7 0.9 maximum_select_fusion.8
  25.6 2.1 collective-permute-start.7
  27.7 2.5 %collective-permute-done.2 = bf16[448,384]{1,0:T(8,128)(2,1)S(1)} collective-permute-done((bf16[448,384]{1,0:T(8,128)(2,1)S(1)}, bf16[448,384]{1,0:T(8,128)(2,1)S(1)}, u32[]{:S(2)}, u32[]{:S(2)}) %collective-permute-start.2) | collective-permute-done | bytes 344096 | tf_op jit(solution)/shard_map/ppermute | solution.py:526
  30.5 7.2 %collective-permute-done.3 = bf16[448,384]{1,0:T(8,128)(2,1)S(1)} collective-permute-done((bf16[448,384]{1,0:T(8,128)(2,1)S(1)}, bf16[448,384]{1,0:T(8,128)(2,1)S(1)}, u32[]{:S(2)}, u32[]{:S(2)}) %collective-permute-start.3) | collective-permute-done | bytes 344096 | tf_op jit(solution)/shard_map/ppermute | solution.py:526
  39.1 4.9 %collective-permute-done.8 = bf16[48,1152]{1,0:T(8,128)(2,1)S(1)} collective-permute-done((bf16[48,1152]{1,0:T(8,128)(2,1)S(1)}, bf16[48,1152]{1,0:T(8,128)(2,1)S(1)}, u32[]{:S(2)}, u32[]{:S(2)}) %collective-permute-start.8) | collective-permute-done | bytes 110624 | tf_op jit(solution)/shard_map/ppermute | solution.py:526
  44.0 1.6 collective-permute-start.9
  45.6 5.4 %collective-permute-done.9 = bf16[96,1152]{1,0:T(8,128)(2,1)S(1)} collective-permute-done((bf16[96,1152]{1,0:T(8,128)(2,1)S(1)}, bf16[96,1152]{1,0:T(8,128)(2,1)S(1)}, u32[]{:S(2)}, u32[]{:S(2)}) %collective-permute-start.9) | collective-permute-done | bytes 221216 | tf_op jit(solution)/shard_map/ppermute | solution.py:526
  51.2 1.8 collective-permute-done.10.refs_5_
  53.0 0.8 copy-done.4
  53.8 17.7 %attn_fwd.2 = (bf16[20,1152,256]{2,1,0:T(8,128)(2,1)}, bf16[20,6,208,256]{3,2,1,0:T(8,128)(2,1)}, bf16[20,384,256]{2,1,0:T(8,128)(2,1)}, bf16[1152,384]{1,0:T(8,128)(2,1)}) custom-call(f32[384]{0:T(512)} %refs_0_.11, f32[384]{0:T(512)} %refs_1_.11, f32[768]{0:T(1024)} %refs_2_.6, s32[1]{0:T(128)} %bitcast.refs_3_.refs_5_.refs_2_, ...), custom_call_target="tpu_custom_call" | custom-call | tf_op jit(solution)/shard_map/attn_fwd/pallas_call | solution.py:470
  71.4 6.4 %attn_fwd.3 = (bf16[20,1152,256]{2,1,0:T(8,128)(2,1)}, bf16[20,6,208,256]{3,2,1,0:T(8,128)(2,1)}, bf16[20,384,256]{2,1,0:T(8,128)(2,1)}) custom-call(f32[384]{0:T(512)} %refs_0_.11, f32[384]{0:T(512)} %refs_1_.11, f32[768]{0:T(1024)} %refs_2_.6, ...), custom_call_target="tpu_custom_call", output_to_operand_aliasing={{0}: (5, {}), {1}: (6, {}), {2}: (7, {})} | custom-call | tf_op jit(solution)/shard_map/attn_fwd/pallas_call | solution.py:470
  77.9 1.1 copy-done.3
  79.0 66.1 %mlp.1 = (f32[20,197,384]{2,1,0:T(8,128)}, f32[20,197,384]{2,1,0:T(8,128)}, bf16[20,384,256]{2,1,0:T(8,128)(2,1)}, f32[16,112,384]{2,1,0:T(8,128)}, bf16[16,112,384]{2,1,0:T(8,128)(2,1)}) custom-call(f32[384]{0:T(512)} %refs_0_.9, f32[384]{0:T(512)} %refs_1_.9, f32[384]{0:T(512)} %refs_2_.7, f32[1536]{0:T(1024)} %refs_3_.3, f32[384]{0:T(512)} %refs_4_.3, ...), custom_call_target="tpu_custom_call" | custom-call | tf_op jit(solution)/shard_map/mlp/pallas_call | solution.py:487
  145.3 9.9 %attn_bwd.2 = (f32[20,197,384]{2,1,0:T(8,128)}, f32[1152,512]{1,0:T(8,128)}, f32[8,768]{1,0:T(8,128)}) custom-call(f32[384]{0:T(512)} %refs_0_.11, f32[384]{0:T(512)} %refs_1_.11, s32[1]{0:T(128)} %bitcast.refs_3_.refs_5_.refs_2_, bf16[20,197,384]{2,1,0:T(8,128)(2,1)} %refs_3_.5, bf16[20,1152,256]{2,1,0:T(8,128)(2,1)} %get-tuple-element.50.refs_4_, ...), custom_call_target="tpu_custom_call" | custom-call | tf_op jit(solution)/shard_map/attn_bwd/pallas_call | solution.py:514
  155.2 28.9 %attn_bwd.3 = (f32[20,197,384]{2,1,0:T(8,128)}, f32[16,48,384]{2,1,0:T(8,128)}, bf16[16,48,384]{2,1,0:T(8,128)(2,1)}) custom-call(f32[384]{0:T(512)} %refs_0_.11, f32[384]{0:T(512)} %refs_1_.11, s32[1]{0:T(128)} %bitcast.refs_3_.refs_5_.refs_2_, bf16[20,197,384]{2,1,0:T(8,128)(2,1)} %refs_3_.5, ...), custom_call_target="tpu_custom_call", output_to_operand_aliasing={{0}: (11, {})} | custom-call | tf_op jit(solution)/shard_map/attn_bwd/pallas_call | solution.py:514
  184.5 1.9 collective-permute-done.11
  186.4 1.6 fusion.9
  188.0 1.6 collective-permute-start.12
  190.1 1.4 collective-permute-start.14
  192.0 1.6 collective-permute-start.19
  194.1 1.5 collective-permute-start.21
  195.6 0.7 collective-permute-done.13
  196.3 3.1 %collective-permute-done.14 = bf16[4,48,384]{2,1,0:T(8,128)(2,1)S(1)} collective-permute-done((bf16[4,48,384]{2,1,0:T(8,128)(2,1)S(1)}, bf16[4,48,384]{2,1,0:T(8,128)(2,1)S(1)}, u32[]{:S(2)}, u32[]{:S(2)}) %collective-permute-start.14) | collective-permute-done | bytes 147488 | tf_op jit(solution)/shard_map/ppermute | solution.py:526
  199.5 5.2 %collective-permute-done.19 = bf16[4,112,384]{2,1,0:T(8,128)(2,1)S(1)} collective-permute-done((bf16[4,112,384]{2,1,0:T(8,128)(2,1)S(1)}, bf16[4,112,384]{2,1,0:T(8,128)(2,1)S(1)}, u32[]{:S(2)}, u32[]{:S(2)}) %collective-permute-start.19) | collective-permute-done | bytes 344096 | tf_op jit(solution)/shard_map/ppermute | solution.py:526
  204.7 2.2 collective-permute-done.20
  206.9 6.4 %collective-permute-done.21 = bf16[4,112,384]{2,1,0:T(8,128)(2,1)S(1)} collective-permute-done((bf16[4,112,384]{2,1,0:T(8,128)(2,1)S(1)}, bf16[4,112,384]{2,1,0:T(8,128)(2,1)S(1)}, u32[]{:S(2)}, u32[]{:S(2)}) %collective-permute-start.21) | collective-permute-done | bytes 344096 | tf_op jit(solution)/shard_map/ppermute | solution.py:526
  213.5 3.5 %collective-permute-start.22 = (bf16[1,112,384]{2,1,0:T(8,128)(2,1)S(1)}, bf16[1,112,384]{2,1,0:T(8,128)(2,1)S(1)}, u32[]{:S(2)}, u32[]{:S(2)}) collective-permute-start(bf16[1,112,384]{2,1,0:T(8,128)(2,1)S(1)} %get-tuple-element.90), channel_id=1, source_target_pairs={{0,16},{1,17},{2,18},{3,19},{4,20},{5,21},{6,22},{7,23},{8,24},{9,... | collective-permute-start | bytes 258056 | tf_op jit(solution)/shard_map/ppermute | solution.py:526
  217.2 1.3 collective-permute-start.24
  218.5 2.0 collective-permute-start.15
  220.5 1.2 collective-permute-start.16
  221.7 4.0 %collective-permute-done.15.refs_1_ = bf16[1,48,384]{2,1,0:T(8,128)(2,1)S(1)} collective-permute-done((bf16[1,48,384]{2,1,0:T(8,128)(2,1)S(1)}, bf16[1,48,384]{2,1,0:T(8,128)(2,1)S(1)}, u32[]{:S(2)}, u32[]{:S(2)}) %collective-permute-start.15) | collective-permute-done | bytes 36896 | tf_op jit(solution)/shard_map/ppermute | solution.py:526
  225.7 3.1 %collective-permute-start.17 = (bf16[1,48,384]{2,1,0:T(8,128)(2,1)S(1)}, bf16[1,48,384]{2,1,0:T(8,128)(2,1)S(1)}, u32[]{:S(2)}, u32[]{:S(2)}) collective-permute-start(bf16[1,48,384]{2,1,0:T(8,128)(2,1)S(1)} %get-tuple-element.91), channel_id=1, source_target_pairs={{0,24},{1,25},{2,26},{3,27},{4,28},{5,29},{6,30},{7,31},{8,16},{9,... | collective-permute-start | bytes 110600 | tf_op jit(solution)/shard_map/ppermute | solution.py:526
  228.8 0.6 slice.88.refs_0_
  229.5 2.0 collective-permute-done.17.refs_3_
  232.1 1.6 finish.2
  233.7 0.7 slice.96.refs_0_
  235.1 0.6 copy-done.7
  235.7 1.8 finish.3
  (51 shorter events, 6.4 us)
Async XLA Ops:
  2.1 5.8 %collective-permute-start = (bf16[112,384]{1,0:T(8,128)(2,1)}, bf16[112,384]{1,0:T(8,128)(2,1)S(1)}, u32[]{:S(2)}, u32[]{:S(2)}) collective-permute-start(bf16[112,384]{1,0:T(8,128)(2,1)} %pack.1), channel_id=1, source_target_pairs={{0,8},{1,9},{2,10},{3,11},{4,12},{5,13},{6,14},{7,15},{8,0},{9,1},... | collective-permute-start | bytes 258056 | tf_op jit(solution)/shard_map/ppermute | solution.py:526
  8.9 10.2 %collective-permute-start.1 = (bf16[224,384]{1,0:T(8,128)(2,1)S(1)}, bf16[224,384]{1,0:T(8,128)(2,1)S(1)}, u32[]{:S(2)}, u32[]{:S(2)}) collective-permute-start(bf16[224,384]{1,0:T(8,128)(2,1)S(1)} %maximum_select_fusion.6), channel_id=1, source_target_pairs={{0,16},{1,17},{2,18},{3,19},{4,20},{5,21},{6,22},{7,23},{8,24},{9,... | collective-permute-start | bytes 516104 | tf_op jit(solution)/shard_map/ppermute | solution.py:526
  19.2 11.0 %collective-permute-start.2 = (bf16[448,384]{1,0:T(8,128)(2,1)S(1)}, bf16[448,384]{1,0:T(8,128)(2,1)S(1)}, u32[]{:S(2)}, u32[]{:S(2)}) collective-permute-start(bf16[448,384]{1,0:T(8,128)(2,1)S(1)} %maximum_select_fusion.4), channel_id=1, source_target_pairs={{0,2},{1,3},{2,0},{3,1},{4,6},{5,7},{6,4},{7,5},{8,10},{9,11},{10,... | collective-permute-start | bytes 1032200 | tf_op jit(solution)/shard_map/ppermute | solution.py:526
  20.6 4.2 %collective-permute-start.6 = (bf16[12,1152]{1,0:T(8,128)(2,1)}, bf16[12,1152]{1,0:T(8,128)(2,1)S(1)}, u32[]{:S(2)}, u32[]{:S(2)}) collective-permute-start(bf16[12,1152]{1,0:T(8,128)(2,1)} %param.17), channel_id=1, source_target_pairs={{0,8},{1,9},{2,10},{3,11},{4,12},{5,13},{6,14},{7,15},{8,0},{9,1},... | collective-permute-start | bytes 82952 | tf_op jit(solution)/shard_map/ppermute | solution.py:526
  21.2 16.5 %collective-permute-start.3 = (bf16[448,384]{1,0:T(8,128)(2,1)S(1)}, bf16[448,384]{1,0:T(8,128)(2,1)S(1)}, u32[]{:S(2)}, u32[]{:S(2)}) collective-permute-start(bf16[448,384]{1,0:T(8,128)(2,1)S(1)} %maximum_select_fusion.4), channel_id=1, source_target_pairs={{0,4},{1,5},{2,6},{3,7},{4,0},{5,1},{6,2},{7,3},{8,12},{9,13},{10,... | collective-permute-start | bytes 1032200 | tf_op jit(solution)/shard_map/ppermute | solution.py:526
  22.8 14.9 %collective-permute-start.4 = (bf16[448,384]{1,0:T(8,128)(2,1)S(1)}, bf16[448,384]{1,0:T(8,128)(2,1)S(1)}, u32[]{:S(2)}, u32[]{:S(2)}) collective-permute-start(bf16[448,384]{1,0:T(8,128)(2,1)S(1)} %maximum_select_fusion.4), channel_id=1, source_target_pairs={{0,6},{1,7},{2,4},{3,5},{4,2},{5,3},{6,0},{7,1},{8,14},{9,15},{10,... | collective-permute-start | bytes 1032200 | tf_op jit(solution)/shard_map/ppermute | solution.py:526
  25.6 12.8 %collective-permute-start.7 = (bf16[24,1152]{1,0:T(8,128)(2,1)S(1)}, bf16[24,1152]{1,0:T(8,128)(2,1)S(1)}, u32[]{:S(2)}, u32[]{:S(2)}) collective-permute-start(bf16[24,1152]{1,0:T(8,128)(2,1)S(1)} %maximum_select_fusion.8), channel_id=1, source_target_pairs={{0,16},{1,17},{2,18},{3,19},{4,20},{5,21},{6,22},{7,23},{8,24},{9,... | collective-permute-start | bytes 165896 | tf_op jit(solution)/shard_map/ppermute | solution.py:526
  38.3 33.1 %copy-start = (bf16[1792,384]{1,0:T(8,128)(2,1)}, bf16[1792,384]{1,0:T(8,128)(2,1)S(1)}, u32[]{:S(2)}) copy-start(bf16[1792,384]{1,0:T(8,128)(2,1)S(1)} %maximum_select_fusion.refs_6_) | copy-start | bytes 4128772
  38.4 39.5 %collective-permute-start.5 = (bf16[1792,384]{1,0:T(8,128)(2,1)S(1)}, bf16[1792,384]{1,0:T(8,128)(2,1)S(1)}, u32[]{:S(2)}, u32[]{:S(2)}) collective-permute-start(bf16[1792,384]{1,0:T(8,128)(2,1)S(1)} %maximum_select_fusion.refs_6_), channel_id=1, source_target_pairs={{0,1},{1,0},{2,3},{3,2},{4,5},{5,4},{6,7},{7,6},{8,9},{9,8},{10,11... | collective-permute-start | bytes 4128776 | tf_op jit(solution)/shard_map/ppermute | solution.py:526
  38.5 5.5 %collective-permute-start.8 = (bf16[48,1152]{1,0:T(8,128)(2,1)S(1)}, bf16[48,1152]{1,0:T(8,128)(2,1)S(1)}, u32[]{:S(2)}, u32[]{:S(2)}) collective-permute-start(bf16[48,1152]{1,0:T(8,128)(2,1)S(1)} %maximum_select_fusion.7), channel_id=1, source_target_pairs={{0,2},{1,3},{2,0},{3,1},{4,6},{5,7},{6,4},{7,5},{8,10},{9,11},{10,... | collective-permute-start | bytes 331784 | tf_op jit(solution)/shard_map/ppermute | solution.py:526
  44.0 7.0 %collective-permute-start.9 = (bf16[96,1152]{1,0:T(8,128)(2,1)S(1)}, bf16[96,1152]{1,0:T(8,128)(2,1)S(1)}, u32[]{:S(2)}, u32[]{:S(2)}) collective-permute-start(bf16[96,1152]{1,0:T(8,128)(2,1)S(1)} %maximum_select_fusion.5), channel_id=1, source_target_pairs={{0,4},{1,5},{2,6},{3,7},{4,0},{5,1},{6,2},{7,3},{8,12},{9,13},{10,... | collective-permute-start | bytes 663560 | tf_op jit(solution)/shard_map/ppermute | solution.py:526
  51.1 1.9 copy-start.2
  51.2 1.9 collective-permute-start.10
  53.0 0.8 copy-start.4
  77.9 1.1 copy-start.3
  145.1 46.5 %collective-permute-start.18 = (bf16[16,112,384]{2,1,0:T(8,128)(2,1)}, bf16[16,112,384]{2,1,0:T(8,128)(2,1)S(1)}, u32[]{:S(2)}, u32[]{:S(2)}) collective-permute-start(bf16[16,112,384]{2,1,0:T(8,128)(2,1)} %get-tuple-element.65), channel_id=1, source_target_pairs={{0,1},{1,0},{2,3},{3,2},{4,5},{5,4},{6,7},{7,6},{8,9},{9,8},{10,11... | collective-permute-start | bytes 4128776 | tf_op jit(solution)/shard_map/ppermute | solution.py:526
  184.1 2.3 collective-permute-start.11
  186.4 5.2 %copy-start.1 = (f32[16,112,384]{2,1,0:T(8,128)S(1)}, f32[16,112,384]{2,1,0:T(8,128)}, u32[]{:S(2)}) copy-start(f32[16,112,384]{2,1,0:T(8,128)} %get-tuple-element.64) | copy-start | bytes 8257540
  188.0 6.1 %collective-permute-start.12 = (bf16[4,48,384]{2,1,0:T(8,128)(2,1)S(1)}, bf16[4,48,384]{2,1,0:T(8,128)(2,1)S(1)}, u32[]{:S(2)}, u32[]{:S(2)}) collective-permute-start(bf16[4,48,384]{2,1,0:T(8,128)(2,1)S(1)} %get-tuple-element.85), channel_id=1, source_target_pairs={{0,4},{1,5},{2,6},{3,7},{4,0},{5,1},{6,2},{7,3},{8,12},{9,13},{10,... | collective-permute-start | bytes 442376 | tf_op jit(solution)/shard_map/ppermute | solution.py:526
  189.6 6.7 %collective-permute-start.13 = (bf16[4,48,384]{2,1,0:T(8,128)(2,1)S(1)}, bf16[4,48,384]{2,1,0:T(8,128)(2,1)S(1)}, u32[]{:S(2)}, u32[]{:S(2)}) collective-permute-start(bf16[4,48,384]{2,1,0:T(8,128)(2,1)S(1)} %get-tuple-element.87), channel_id=1, source_target_pairs={{0,2},{1,3},{2,0},{3,1},{4,6},{5,7},{6,4},{7,5},{8,10},{9,11},{10,... | collective-permute-start | bytes 442376 | tf_op jit(solution)/shard_map/ppermute | solution.py:526
  190.1 9.3 %collective-permute-start.14 = (bf16[4,48,384]{2,1,0:T(8,128)(2,1)S(1)}, bf16[4,48,384]{2,1,0:T(8,128)(2,1)S(1)}, u32[]{:S(2)}, u32[]{:S(2)}) collective-permute-start(bf16[4,48,384]{2,1,0:T(8,128)(2,1)S(1)} %get-tuple-element.86), channel_id=1, source_target_pairs={{0,6},{1,7},{2,4},{3,5},{4,2},{5,3},{6,0},{7,1},{8,14},{9,15},{10,... | collective-permute-start | bytes 442376 | tf_op jit(solution)/shard_map/ppermute | solution.py:526
  192.0 12.7 %collective-permute-start.19 = (bf16[4,112,384]{2,1,0:T(8,128)(2,1)S(1)}, bf16[4,112,384]{2,1,0:T(8,128)(2,1)S(1)}, u32[]{:S(2)}, u32[]{:S(2)}) collective-permute-start(bf16[4,112,384]{2,1,0:T(8,128)(2,1)S(1)} %get-tuple-element.82), channel_id=1, source_target_pairs={{0,4},{1,5},{2,6},{3,7},{4,0},{5,1},{6,2},{7,3},{8,12},{9,13},{10,... | collective-permute-start | bytes 1032200 | tf_op jit(solution)/shard_map/ppermute | solution.py:526
  193.6 13.3 %collective-permute-start.20 = (bf16[4,112,384]{2,1,0:T(8,128)(2,1)S(1)}, bf16[4,112,384]{2,1,0:T(8,128)(2,1)S(1)}, u32[]{:S(2)}, u32[]{:S(2)}) collective-permute-start(bf16[4,112,384]{2,1,0:T(8,128)(2,1)S(1)} %get-tuple-element.84), channel_id=1, source_target_pairs={{0,2},{1,3},{2,0},{3,1},{4,6},{5,7},{6,4},{7,5},{8,10},{9,11},{10,... | collective-permute-start | bytes 1032200 | tf_op jit(solution)/shard_map/ppermute | solution.py:526
  194.1 19.1 %collective-permute-start.21 = (bf16[4,112,384]{2,1,0:T(8,128)(2,1)S(1)}, bf16[4,112,384]{2,1,0:T(8,128)(2,1)S(1)}, u32[]{:S(2)}, u32[]{:S(2)}) collective-permute-start(bf16[4,112,384]{2,1,0:T(8,128)(2,1)S(1)} %get-tuple-element.83), channel_id=1, source_target_pairs={{0,6},{1,7},{2,4},{3,5},{4,2},{5,3},{6,0},{7,1},{8,14},{9,15},{10,... | collective-permute-start | bytes 1032200 | tf_op jit(solution)/shard_map/ppermute | solution.py:526
  213.5 20.9 %collective-permute-start.22 = (bf16[1,112,384]{2,1,0:T(8,128)(2,1)S(1)}, bf16[1,112,384]{2,1,0:T(8,128)(2,1)S(1)}, u32[]{:S(2)}, u32[]{:S(2)}) collective-permute-start(bf16[1,112,384]{2,1,0:T(8,128)(2,1)S(1)} %get-tuple-element.90), channel_id=1, source_target_pairs={{0,16},{1,17},{2,18},{3,19},{4,20},{5,21},{6,22},{7,23},{8,24},{9,... | collective-permute-start | bytes 258056 | tf_op jit(solution)/shard_map/ppermute | solution.py:526
  216.9 17.5 %collective-permute-start.23 = (bf16[1,112,384]{2,1,0:T(8,128)(2,1)S(1)}, bf16[1,112,384]{2,1,0:T(8,128)(2,1)S(1)}, u32[]{:S(2)}, u32[]{:S(2)}) collective-permute-start(bf16[1,112,384]{2,1,0:T(8,128)(2,1)S(1)} %get-tuple-element.89), channel_id=1, source_target_pairs={{0,8},{1,9},{2,10},{3,11},{4,12},{5,13},{6,14},{7,15},{8,0},{9,1},... | collective-permute-start | bytes 258056 | tf_op jit(solution)/shard_map/ppermute | solution.py:526
  217.2 17.2 %collective-permute-start.24 = (bf16[1,112,384]{2,1,0:T(8,128)(2,1)S(1)}, bf16[1,112,384]{2,1,0:T(8,128)(2,1)S(1)}, u32[]{:S(2)}, u32[]{:S(2)}) collective-permute-start(bf16[1,112,384]{2,1,0:T(8,128)(2,1)S(1)} %get-tuple-element.88), channel_id=1, source_target_pairs={{0,24},{1,25},{2,26},{3,27},{4,28},{5,29},{6,30},{7,31},{8,16},{9,... | collective-permute-start | bytes 258056 | tf_op jit(solution)/shard_map/ppermute | solution.py:526
  218.5 7.2 %collective-permute-start.15 = (bf16[1,48,384]{2,1,0:T(8,128)(2,1)S(1)}, bf16[1,48,384]{2,1,0:T(8,128)(2,1)S(1)}, u32[]{:S(2)}, u32[]{:S(2)}) collective-permute-start(bf16[1,48,384]{2,1,0:T(8,128)(2,1)S(1)} %get-tuple-element.93), channel_id=1, source_target_pairs={{0,16},{1,17},{2,18},{3,19},{4,20},{5,21},{6,22},{7,23},{8,24},{9,... | collective-permute-start | bytes 110600 | tf_op jit(solution)/shard_map/ppermute | solution.py:526
  220.5 9.0 %collective-permute-start.16 = (bf16[1,48,384]{2,1,0:T(8,128)(2,1)S(1)}, bf16[1,48,384]{2,1,0:T(8,128)(2,1)S(1)}, u32[]{:S(2)}, u32[]{:S(2)}) collective-permute-start(bf16[1,48,384]{2,1,0:T(8,128)(2,1)S(1)} %get-tuple-element.92), channel_id=1, source_target_pairs={{0,8},{1,9},{2,10},{3,11},{4,12},{5,13},{6,14},{7,15},{8,0},{9,1},... | collective-permute-start | bytes 110600 | tf_op jit(solution)/shard_map/ppermute | solution.py:526
  225.7 5.8 %copy-start.8 = (bf16[1,48,384]{2,1,0:T(8,128)(2,1)}, bf16[1,48,384]{2,1,0:T(8,128)(2,1)S(1)}, u32[]{:S(2)}) copy-start(bf16[1,48,384]{2,1,0:T(8,128)(2,1)S(1)} %collective-permute-done.15.refs_1_) | copy-start | bytes 110596
  225.7 5.8 %collective-permute-start.17 = (bf16[1,48,384]{2,1,0:T(8,128)(2,1)S(1)}, bf16[1,48,384]{2,1,0:T(8,128)(2,1)S(1)}, u32[]{:S(2)}, u32[]{:S(2)}) collective-permute-start(bf16[1,48,384]{2,1,0:T(8,128)(2,1)S(1)} %get-tuple-element.91), channel_id=1, source_target_pairs={{0,24},{1,25},{2,26},{3,27},{4,28},{5,29},{6,30},{7,31},{8,16},{9,... | collective-permute-start | bytes 110600 | tf_op jit(solution)/shard_map/ppermute | solution.py:526
  229.5 2.0 copy-start.9
  231.5 0.6 copy-start.10
  234.4 0.6 copy-start.5
  234.4 0.7 copy-start.6
  235.1 0.6 copy-start.7
